TPU v7x, 512 devices: a whole 4x8x8 slice. The times are simulated.
512 devices in a mesh: gx: 64 (over z_lo, y, x), gy: 8 (over z_hi, core).
Axes of the slice: x: 4, y: 8, z: 8 (z_hi: 4, z_lo: 2; z = z_hi * 2 + z_lo), core: 2. Of those that a mesh axis runs over, the one named last changes fastest.
Arguments:
- skip_feature_rows: bfloat16 [1024, 192, 512], P(('gx', 'gy')), may hold values from -6 to 6
- coarse_features: bfloat16 [1024, 192, 512], P(('gx', 'gy')), may hold values from -6 to 6
- cotangent: bfloat16 [1024, 192, 512], P(('gx', 'gy')), may hold values from -16 to 16
- fine_coords: int32 [1024, 3], P(('gx', 'gy')), may hold values from 0 to 3, as said below
- coarse_coords: int32 [1024, 3], P(('gx', 'gy')), may hold values from 0 to 1, as said below
- parents: int32 [1024], P(('gx', 'gy')), may hold values from 0 to 1
- counts: int32 [512], P(('gx', 'gy')), may hold values from 1 to 2
- conv_weight: bfloat16 [192, 27, 192], replicated, may hold values from -0.078125 to 0.078125
- up_weight: bfloat16 [8, 192, 192], replicated, may hold values from -0.4375 to 0.4375
Outputs:
- grad_skip: bfloat16 [1024, 192, 512], P(('gx', 'gy'))
- grad_coarse: bfloat16 [1024, 192, 512], P(('gx', 'gy'))
- grad_conv: float32 [192, 27, 192], P('gy')
Inputs may be any that keep to these rules, and one draw needn't show every extreme that they name: `fine_coords`: within one tile the fine slots have distinct coordinates in 0..1, 0..1, 0..3, and each equals 2 coarse_coords of its parent plus a 0/1 offset per axis. `coarse_coords`: within one tile the 2 coarse slots hold each coarse block position of the tile once.
All inputs are finite; a program needn't handle non-finite values.
Results may differ from a plain program's by a relative error of at most 0.013.
Values may be sent and summed in bfloat16 or wider, within the bound.
No kernel may reach another device: no remote copies, remote signals or barrier semaphores. Data moves between devices by JAX's collectives and lax.ppermute only.
A program may use at most 128 MiB of HBM per device.

v0:
```python
import jax
import jax.numpy as jnp
from jax import lax
from jax.sharding import PartitionSpec as P

FB_X = 2
FB_Y = 2
FB_Z = 4


def padded_2(block, sides, width):
    for axis, dim in sides:
        count = lax.axis_size(axis)
        forward = [(i, i + 1) for i in range(count - 1)]
        backward = [(target, source) for source, target in forward]
        low = lax.ppermute(
            lax.slice_in_dim(block, block.shape[dim] - width, None, axis=dim), axis, forward
        )
        high = lax.ppermute(lax.slice_in_dim(block, 0, width, axis=dim), axis, backward)
        block = jnp.concatenate([low, block, high], axis=dim)
    return block


def index_tuple(anchor):
    return tuple((jnp.asarray(entry).astype(jnp.int32) for entry in anchor))


def add_into(target, addend, anchor):
    anchor = index_tuple(anchor)
    current = lax.dynamic_slice(target, anchor, addend.shape)
    return lax.dynamic_update_slice(target, current + addend, anchor)


def upsample(coarse_row, octant, up_rows):
    channel_count = coarse_row.shape[0]
    block_cube = coarse_row.reshape(channel_count, 8, 8, 8)
    octant_cube = lax.dynamic_slice(
        block_cube,
        index_tuple((0, 4 * octant[0], 4 * octant[1], 4 * octant[2])),
        (channel_count, 4, 4, 4),
    )
    product = jnp.dot(
        up_rows, octant_cube.reshape(channel_count, 64), preferred_element_type=jnp.float32
    )
    product = product.reshape(2, 2, 2, channel_count, 4, 4, 4).transpose(3, 4, 0, 5, 1, 6, 2)
    return product.reshape(channel_count, 512)


def fold_down(grad_row, up_rows):
    channel_count = grad_row.shape[0]
    regrouped = (
        grad_row.reshape(channel_count, 4, 2, 4, 2, 4, 2)
        .transpose(2, 4, 6, 0, 1, 3, 5)
        .reshape(8 * channel_count, 64)
    )
    return lax.dot_general(
        up_rows, regrouped, (((0,), (0,)), ((), ())), preferred_element_type=jnp.float32
    )


def coarse_gradient(grad_rows, parent_ids, octants, coarse_count, up_rows):
    channel_count = grad_rows.shape[1]
    coarse_total = jnp.zeros((coarse_count, channel_count, 8, 8, 8), jnp.float32)
    for member in range(grad_rows.shape[0]):
        addend = fold_down(grad_rows[member], up_rows).reshape(1, channel_count, 4, 4, 4)
        anchor = (
            parent_ids[member],
            0,
            4 * octants[member, 0],
            4 * octants[member, 1],
            4 * octants[member, 2],
        )
        coarse_total = add_into(coarse_total, addend, anchor)
    return coarse_total.astype(jnp.bfloat16).reshape(coarse_count, channel_count, 512)


def columns(padded, coord, reverse):
    channel_count = padded.shape[0]
    window = lax.dynamic_slice(
        padded,
        index_tuple((0, 8 * coord[0], 8 * coord[1], 8 * coord[2])),
        (channel_count, 10, 10, 10),
    )
    shifted = []
    for step_x in range(3):
        for step_y in range(3):
            for step_z in range(3):
                if reverse:
                    first_x, first_y, first_z = (2 - step_x, 2 - step_y, 2 - step_z)
                else:
                    first_x, first_y, first_z = (step_x, step_y, step_z)
                view = window[
                    :, first_x : first_x + 8, first_y : first_y + 8, first_z : first_z + 8
                ]
                shifted.append(view.reshape(channel_count, 512))
    return jnp.concatenate(shifted, 0)


def forward_slot(hidden_cols, cot_row, occupied, weight_flat):
    pre = jnp.dot(weight_flat, hidden_cols, preferred_element_type=jnp.float32)
    sigma = jax.nn.sigmoid(pre)
    return (cot_row.astype(jnp.float32) * (sigma * (1.0 + pre * (1.0 - sigma))) * occupied).astype(
        jnp.bfloat16
    )


def dense_volume(features, coords):
    channel_count = features.shape[1]
    volume = jnp.zeros((channel_count, 8 * FB_X, 8 * FB_Y, 8 * FB_Z), jnp.bfloat16)
    for member in range(features.shape[0]):
        anchor = index_tuple(
            (0, 8 * coords[member, 0], 8 * coords[member, 1], 8 * coords[member, 2])
        )
        volume = lax.dynamic_update_slice(
            volume, features[member].reshape(channel_count, 8, 8, 8), anchor
        )
    return volume


def pad_depth(volume):
    return jnp.pad(volume, ((0, 0), (0, 0), (0, 0), (1, 1)))


def local(
    skip_feature_rows,
    coarse_features,
    cotangent,
    fine_coords,
    coarse_coords,
    parents,
    counts,
    conv_weight,
    up_weight,
):
    slot_count = skip_feature_rows.shape[0]
    channel_count = skip_feature_rows.shape[1]
    coarse_count = coarse_features.shape[0]
    occupied = (jnp.arange(slot_count, dtype=jnp.int32) < counts[0]).astype(jnp.float32)
    up_rows = up_weight.reshape(8 * channel_count, channel_count)
    octants = fine_coords - 2 * coarse_coords[parents]
    lifted = jnp.stack(
        [
            upsample(coarse_features[parents[member]], octants[member], up_rows)
            for member in range(slot_count)
        ],
        0,
    )
    hidden = ((lifted + skip_feature_rows.astype(jnp.float32)) * occupied[:, None, None]).astype(
        jnp.bfloat16
    )
    hidden_frame = pad_depth(padded_2(dense_volume(hidden, fine_coords), (("gx", 1), ("gy", 2)), 1))
    weight_flat = conv_weight.reshape(channel_count, 27 * channel_count)
    weight_flipped = jnp.transpose(conv_weight, (2, 1, 0)).reshape(
        channel_count, 27 * channel_count
    )
    grad_list = []
    local_grad = jnp.zeros((channel_count, 27 * channel_count), jnp.float32)
    for member in range(slot_count):
        cols_one = columns(hidden_frame, fine_coords[member], False)
        grad_one = forward_slot(cols_one, cotangent[member], occupied[member], weight_flat)
        local_grad = local_grad + lax.dot_general(
            grad_one, cols_one, (((1,), (1,)), ((), ())), preferred_element_type=jnp.float32
        )
        grad_list.append(grad_one)
    grad_pre = jnp.stack(grad_list, 0)
    grad_frame = pad_depth(padded_2(dense_volume(grad_pre, fine_coords), (("gx", 1), ("gy", 2)), 1))
    skip_list = []
    for member in range(slot_count):
        grad_cols = columns(grad_frame, fine_coords[member], True)
        backprop_one = jnp.dot(weight_flipped, grad_cols, preferred_element_type=jnp.float32)
        skip_list.append((backprop_one * occupied[member]).astype(jnp.bfloat16))
    grad_skip = jnp.stack(skip_list, 0)
    grad_coarse = coarse_gradient(grad_skip, parents, octants, coarse_count, up_rows)
    slab_sum = lax.psum(local_grad, "gx")
    grad_conv = lax.psum_scatter(
        slab_sum.astype(jnp.bfloat16), "gy", scatter_dimension=0, tiled=True
    ).astype(jnp.float32)
    return (grad_skip, grad_coarse, grad_conv.reshape(grad_conv.shape[0], 27, channel_count))


def solution(mesh):
    in_specs = (
        P(("gx", "gy"), None, None),
        P(("gx", "gy"), None, None),
        P(("gx", "gy"), None, None),
        P(("gx", "gy"), None),
        P(("gx", "gy"), None),
        P(("gx", "gy")),
        P(("gx", "gy")),
        P(),
        P(),
    )
    out_specs = (P(("gx", "gy"), None, None), P(("gx", "gy"), None, None), P("gy", None, None))
    return jax.shard_map(local, mesh=mesh, in_specs=in_specs, out_specs=out_specs, check_vma=False)
```

profile of v0, /device:TPU:320, one launch (start us, length us, event | category | flops | bytes accessed | tf_op | source)
XLA Modules:
  0.0 584.0 jit_solution(1936775195492149712)
XLA Ops:
  7.2 0.7 compare_select_fusion
  8.0 1.2 gather_fusion
  9.2 0.7 multiply_subtract_fusion
  9.9 0.6 fusion.40
  12.5 1.3 fusion.42
  18.3 1.6 fusion.39
  24.9 1.1 constant_dynamic-slice_fusion.111
  26.2 0.4 convolution_bitcast_fusion.1
  26.5 0.5 reshape.431
  27.0 0.3 copy.49
  27.3 0.4 stack_reshape.6
  27.9 0.4 convolution_bitcast_fusion
  28.3 0.5 reshape.433
  29.1 0.4 stack_reshape.7
  30.6 0.8 fusion.38
  31.4 0.5 broadcast.27.clone
  31.9 1.2 constant_dynamic-update-slice_fusion.4
  33.2 1.0 constant_dynamic-update-slice_fusion.3
  34.2 3.4 collective-permute-start
  37.6 6.7 %collective-permute-start.1 = (bf16[192,1,16,32]{0,3,2,1:T(8,128)(2,1)S(1)}, bf16[192,1,16,32]{0,3,2,1:T(8,128)(2,1)S(1)}, u32[]{:S(2)}, u32[]{:S(2)}) collective-permute-start(bf16[192,1,16,32]{0,3,2,1:T(8,128)(2,1)S(1)} %get-tuple-element.127), channel_id=1, source_target_pairs={{8,0},{16,8},{24,16},{32,24},{40,32},{48,40},{56,48},{64,56},{72,6... | collective-permute-start | bytes 589832 | tf_op jit(solution)/shard_map/ppermute | solution.py:19
  44.3 4.1 collective-permute-done
  48.4 1.2 collective-permute-done.1
  49.6 1.0 pad_maximum_fusion.6
  50.6 1.9 collective-permute-start.2
  52.5 5.9 %collective-permute-start.3 = (bf16[192,18,1,32]{0,3,2,1:T(8,128)(2,1)}, bf16[192,18,1,32]{0,3,2,1:T(8,128)(2,1)}, u32[]{:S(2)}, u32[]{:S(2)}) collective-permute-start(bf16[192,18,1,32]{0,3,2,1:T(8,128)(2,1)} %get-tuple-element.123), channel_id=1, source_target_pairs={{1,0},{2,1},{3,2},{4,3},{5,4},{6,5},{7,6},{9,8},{10,9},{11,10},{12... | collective-permute-start | bytes 663560 | tf_op jit(solution)/shard_map/ppermute | solution.py:19
  58.5 3.4 copy.35
  61.9 0.6 fusion.41
  62.6 1.4 collective-permute-done.2
  63.9 7.4 %fusion.10 = bf16[192,18,18,34]{0,3,2,1:T(8,128)(2,1)S(1)} fusion(bf16[192,18,1,32]{0,3,2,1:T(8,128)(2,1)} %collective-permute-done.3, bf16[192,18,1,32]{0,3,2,1:T(8,128)(2,1)} %collective-permute-done.2, bf16[192,1,16,32]{0,3,2,1:T(8,128)(2,1)} %copy-done.9, bf16[192,16,16,32]{0,3,2,1:T(8,128)(2,1)} %copy-done.2, bf16[192,1,16,32]{0,3,2,1:T(8,128)(2,1)} %copy-done.8), kind=kLoop, calls=%fused_computation.16 | loop fusion | flops 38071296 | bytes 8211456 | tf_op jit(solution)/shard_map/concatenate | solution.py:20
  71.4 10.6 %constant_dynamic-slice_fusion.106 = (bf16[192,8,8,8]{0,3,2,1:T(8,128)(2,1)}, bf16[192,8,8,8]{0,3,2,1:T(8,128)(2,1)}, bf16[192,8,8,8]{0,3,2,1:T(8,128)(2,1)}, bf...) fusion(bf16[192,18,18,34]{0,3,2,1:T(8,128)(2,1)S(1)} %fusion.10, ...), kind=kLoop, calls=%fused_computation.167 | loop fusion | bytes 21233736 | tf_op jit(solution)/shard_map/slice | solution.py:92
  82.0 10.2 %concatenate.26 = bf16[5184,512]{0,1:T(8,128)(2,1)} concatenate(bf16[192,512]{0,1:T(8,128)(2,1)} %bitcast.342, bf16[192,512]{0,1:T(8,128)(2,1)} %bitcast.341, bf16[192,512]{0,1:T(8,128)(2,1)} %bitcast.340, bf16[192,512]{0,1:T(8,128)(2,1)} %bitcast.339, bf16[192,512]{0,1:T(8,128)(2,1)} %bitcast.338, bf16[192,512]{0,1:T(8,128)(2,1)} %bitcast.337, bf16[192,512]{0,1:T(8,128)(2,1)} %bitcast.336, ...), dimensions={0} | concatenate | bytes 10616832 | tf_op jit(solution)/shard_map/concatenate | solution.py:96
  92.3 5.4 convolution_bitcast_fusion.3
  97.7 3.9 fusion.24
  101.6 10.2 %concatenate.27 = bf16[5184,512]{0,1:T(8,128)(2,1)} concatenate(bf16[192,512]{0,1:T(8,128)(2,1)} %bitcast.316, bf16[192,512]{0,1:T(8,128)(2,1)} %bitcast.315, bf16[192,512]{0,1:T(8,128)(2,1)} %bitcast.314, bf16[192,512]{0,1:T(8,128)(2,1)} %bitcast.313, bf16[192,512]{0,1:T(8,128)(2,1)} %bitcast.312, bf16[192,512]{0,1:T(8,128)(2,1)} %bitcast.311, bf16[192,512]{0,1:T(8,128)(2,1)} %bitcast.310, ...), dimensions={0} | concatenate | bytes 10616832 | tf_op jit(solution)/shard_map/concatenate | solution.py:96
  111.9 7.7 %fusion.20 = (bf16[192,512]{1,0:T(8,128)(2,1)}, bf16[192,512]{1,0:T(8,128)(2,1)}, f32[192,512]{1,0:T(8,128)}) fusion(f32[]{:T(128)} %bitcast.85, bf16[2,192,512]{2,1,0:T(8,128)(2,1)} %param.11, f32[]{:T(128)} %bitcast.54, f32[192,512]{1,0:T(8,128)} %copy-done.12, bf16[5184,512]{0,1:T(8,128)(2,1)} %concatenate.27, bf16[192,5184]{0,1:T(8,128)(2,1)} %bitcast.228), kind=kOutput, calls=%fused_computation.39 | convolution fusion | flops 1021378560 | bytes 8871944 | tf_op jit(solution)/shard_map/dot_general | solution.py:100
  119.5 1.8 copy.36
  121.3 1.8 copy.37
  123.1 0.5 broadcast.27
  123.6 1.2 constant_dynamic-update-slice_fusion.2
  124.9 1.0 constant_dynamic-update-slice_fusion.1
  125.9 1.9 collective-permute-start.4
  127.8 8.4 %collective-permute-start.5 = (bf16[192,1,16,32]{0,3,2,1:T(8,128)(2,1)S(1)}, bf16[192,1,16,32]{0,3,2,1:T(8,128)(2,1)S(1)}, u32[]{:S(2)}, u32[]{:S(2)}) collective-permute-start(bf16[192,1,16,32]{0,3,2,1:T(8,128)(2,1)S(1)} %get-tuple-element.125), channel_id=1, source_target_pairs={{8,0},{16,8},{24,16},{32,24},{40,32},{48,40},{56,48},{64,56},{72,6... | collective-permute-start | bytes 589832 | tf_op jit(solution)/shard_map/ppermute | solution.py:19
  136.2 6.4 %convolution_add_fusion = f32[192,5184]{1,0:T(8,128)} fusion(f32[192,5184]{1,0:T(8,128)S(1)} %copy-done.5, bf16[5184,512]{0,1:T(8,128)(2,1)} %concatenate.27, f32[192,512]{1,0:T(8,128)S(1)} %copy-done.13, f32[]{:T(128)} %bitcast.85, bf16[2,192,512]{2,1,0:T(8,128)(2,1)S(1)} %copy-done.17), kind=kOutput, calls=%fused_computation.4 | convolution fusion | flops 1021292544 | bytes 13910020 | tf_op jit(solution)/shard_map/dot_general | solution.py:161
  142.7 1.0 pad_maximum_fusion.3
  143.7 2.4 collective-permute-start.6
  146.0 5.3 collective-permute-start.7
  151.3 359.5 %all-reduce.4 = bf16[192,5184]{1,0:T(8,128)(2,1)} all-reduce(f32[192,5184]{1,0:T(8,128)} %convolution_add_fusion), channel_id=1, replica_groups=mesh['gx'=64,'gy'=8] {'gx'}, use_global_device_ids=true, to_apply=%region_0.1 | all-reduce | flops 995328 | bytes 5971968 | tf_op jit(solution)/shard_map/psum | solution.py:174
  510.9 7.4 %select_maximum_fusion = bf16[192,18,18,34]{0,3,2,1:T(8,128)(2,1)S(1)} fusion(bf16[192,18,1,32]{0,3,2,1:T(8,128)(2,1)} %collective-permute-done.7, bf16[192,18,1,32]{0,3,2,1:T(8,128)(2,1)} %collective-permute-done.6, bf16[192,1,16,32]{0,3,2,1:T(8,128)(2,1)} %copy-done.11, bf16[192,16,16,32]{0,3,2,1:T(8,128)(2,1)} %copy-done.1, ...), kind=kLoop, calls=%fused_computation.5 | loop fusion | flops 38071296 | bytes 8211456 | tf_op jit(solution)/shard_map/concatenate | solution.py:20
  518.3 10.9 %constant_dynamic-slice_fusion.105 = (bf16[192,8,8,8]{0,3,2,1:T(8,128)(2,1)}, bf16[192,8,8,8]{0,3,2,1:T(8,128)(2,1)}, bf16[192,8,8,8]{0,3,2,1:T(8,128)(2,1)}, bf...) fusion(bf16[192,18,18,34]{0,3,2,1:T(8,128)(2,1)S(1)} %select_ma, ...), kind=kLoop, calls=%fused_computation.165 | loop fusion | bytes 21233736 | tf_op jit(solution)/shard_map/slice | solution.py:92
  529.2 10.3 %concatenate.30 = bf16[5184,512]{0,1:T(8,128)(2,1)} concatenate(bf16[192,512]{0,1:T(8,128)(2,1)} %bitcast.289, bf16[192,512]{0,1:T(8,128)(2,1)} %bitcast.288, bf16[192,512]{0,1:T(8,128)(2,1)} %bitcast.287, bf16[192,512]{0,1:T(8,128)(2,1)} %bitcast.286, bf16[192,512]{0,1:T(8,128)(2,1)} %bitcast.285, bf16[192,512]{0,1:T(8,128)(2,1)} %bitcast.284, bf16[192,512]{0,1:T(8,128)(2,1)} %bitcast.283, ...), dimensions={0} | concatenate | bytes 10616832 | tf_op jit(solution)/shard_map/concatenate | solution.py:96
  539.5 5.9 %fusion.15 = bf16[512,192]{0,1:T(8,128)(2,1)} fusion(bf16[5184,512]{0,1:T(8,128)(2,1)} %concatenate.30, bf16[192,5184]{0,1:T(8,128)(2,1)S(1)} %bitcast.225, f32[]{:T(128)} %bitcast.54), kind=kOutput, calls=%fused_computation.27 | convolution fusion | flops 1019412480 | bytes 7495684 | tf_op jit(solution)/shard_map/dot_general | solution.py:170
  545.4 1.8 copy.38
  547.1 1.8 reshape_squeeze_stack.14
  548.9 1.9 copy.39
  550.8 1.8 reshape.544
  552.7 1.2 convolution_bitcast_fusion.5
  553.9 0.7 reshape.545
  554.5 10.2 %concatenate.31 = bf16[5184,512]{0,1:T(8,128)(2,1)} concatenate(bf16[192,512]{0,1:T(8,128)(2,1)} %bitcast.261, bf16[192,512]{0,1:T(8,128)(2,1)} %bitcast.260, bf16[192,512]{0,1:T(8,128)(2,1)} %bitcast.259, bf16[192,512]{0,1:T(8,128)(2,1)} %bitcast.258, bf16[192,512]{0,1:T(8,128)(2,1)} %bitcast.257, bf16[192,512]{0,1:T(8,128)(2,1)} %bitcast.256, bf16[192,512]{0,1:T(8,128)(2,1)} %bitcast.255, ...), dimensions={0} | concatenate | bytes 10616832 | tf_op jit(solution)/shard_map/concatenate | solution.py:96
  564.8 5.8 fusion.16
  570.6 1.1 copy.40
  572.9 0.9 copy.42
  573.9 0.8 pad_maximum_fusion
  574.6 1.3 reshape.554
  576.0 1.2 copy.43
  (66 shorter events, 2.5 us)
Async XLA Ops:
  7.2 19.0 %copy-start = (bf16[8,192,192]{2,1,0:T(8,128)(2,1)S(1)}, bf16[8,192,192]{2,1,0:T(8,128)(2,1)}, u32[]{:S(2)}) copy-start(bf16[8,192,192]{2,1,0:T(8,128)(2,1)} %param.17) | copy-start | bytes 1769476
  7.2 22.9 %copy-start.14 = (bf16[2,192,512]{2,1,0:T(8,128)(2,1)S(1)}, bf16[2,192,512]{2,1,0:T(8,128)(2,1)}, u32[]{:S(2)}) copy-start(bf16[2,192,512]{2,1,0:T(8,128)(2,1)} %param.9) | copy-start | bytes 1179652
  7.2 567.4 %reduce-scatter.4.cloned.1.call-start = ((), (), s32[]{:S(2)}) async-start(), calls=%async_computation.1 | async-start | bytes 2267136
  31.4 27.1 %copy-start.3 = (bf16[192,27,192]{2,0,1:T(8,128)(2,1)S(1)}, bf16[192,27,192]{2,0,1:T(8,128)(2,1)}, u32[]{:S(2)}) copy-start(bf16[192,27,192]{2,0,1:T(8,128)(2,1)} %param.16) | copy-start | bytes 5971972
  34.2 15.4 %copy-start.2 = (bf16[192,16,16,32]{0,3,2,1:T(8,128)(2,1)}, bf16[192,16,16,32]{0,3,2,1:T(8,128)(2,1)S(1)}, u32[]{:S(2)}) copy-start(bf16[192,16,16,32]{0,3,2,1:T(8,128)(2,1)S(1)} %constant_dynamic-update-slice_fusion.3) | copy-start | bytes 9437188
  34.2 14.2 %collective-permute-start = (bf16[192,1,16,32]{0,3,2,1:T(8,128)(2,1)S(1)}, bf16[192,1,16,32]{0,3,2,1:T(8,128)(2,1)S(1)}, u32[]{:S(2)}, u32[]{:S(2)}) collective-permute-start(bf16[192,1,16,32]{0,3,2,1:T(8,128)(2,1)S(1)} %get-tuple-element.126), channel_id=1, source_target_pairs={{0,8},{8,16},{16,24},{24,32},{32,40},{40,48},{48,56},{56,64},{64,7... | collective-permute-start | bytes 589832 | tf_op jit(solution)/shard_map/ppermute | solution.py:16
  37.6 11.9 %collective-permute-start.1 = (bf16[192,1,16,32]{0,3,2,1:T(8,128)(2,1)S(1)}, bf16[192,1,16,32]{0,3,2,1:T(8,128)(2,1)S(1)}, u32[]{:S(2)}, u32[]{:S(2)}) collective-permute-start(bf16[192,1,16,32]{0,3,2,1:T(8,128)(2,1)S(1)} %get-tuple-element.127), channel_id=1, source_target_pairs={{8,0},{16,8},{24,16},{32,24},{40,32},{48,40},{56,48},{64,56},{72,6... | collective-permute-start | bytes 589832 | tf_op jit(solution)/shard_map/ppermute | solution.py:19
  48.4 2.2 copy-start.8
  49.6 1.0 copy-start.9
  50.6 13.4 %collective-permute-start.2 = (bf16[192,18,1,32]{0,3,2,1:T(8,128)(2,1)}, bf16[192,18,1,32]{0,3,2,1:T(8,128)(2,1)}, u32[]{:S(2)}, u32[]{:S(2)}) collective-permute-start(bf16[192,18,1,32]{0,3,2,1:T(8,128)(2,1)} %get-tuple-element.122), channel_id=1, source_target_pairs={{0,1},{1,2},{2,3},{3,4},{4,5},{5,6},{6,7},{8,9},{9,10},{10,11},{11... | collective-permute-start | bytes 663560 | tf_op jit(solution)/shard_map/ppermute | solution.py:16
  52.5 11.5 %collective-permute-start.3 = (bf16[192,18,1,32]{0,3,2,1:T(8,128)(2,1)}, bf16[192,18,1,32]{0,3,2,1:T(8,128)(2,1)}, u32[]{:S(2)}, u32[]{:S(2)}) collective-permute-start(bf16[192,18,1,32]{0,3,2,1:T(8,128)(2,1)} %get-tuple-element.123), channel_id=1, source_target_pairs={{1,0},{2,1},{3,2},{4,3},{5,4},{6,5},{7,6},{9,8},{10,9},{11,10},{12... | collective-permute-start | bytes 663560 | tf_op jit(solution)/shard_map/ppermute | solution.py:19
  92.2 5.4 copy-start.4
  92.3 5.4 copy-start.16
  97.7 4.0 copy-start.12
  123.1 13.1 %copy-start.5 = (f32[192,5184]{1,0:T(8,128)S(1)}, f32[192,5184]{1,0:T(8,128)}, u32[]{:S(2)}) copy-start(f32[192,5184]{1,0:T(8,128)} %fusion.24) | copy-start | bytes 11943940
  123.1 13.1 %copy-start.13 = (f32[192,512]{1,0:T(8,128)S(1)}, f32[192,512]{1,0:T(8,128)}, u32[]{:S(2)}) copy-start(f32[192,512]{1,0:T(8,128)} %get-tuple-element.150) | copy-start | bytes 1179652
  123.1 13.1 %copy-start.17 = (bf16[2,192,512]{2,1,0:T(8,128)(2,1)S(1)}, bf16[2,192,512]{2,1,0:T(8,128)(2,1)}, u32[]{:S(2)}) copy-start(bf16[2,192,512]{2,1,0:T(8,128)(2,1)} %param.11) | copy-start | bytes 1179652
  125.9 16.8 %copy-start.1 = (bf16[192,16,16,32]{0,3,2,1:T(8,128)(2,1)}, bf16[192,16,16,32]{0,3,2,1:T(8,128)(2,1)S(1)}, u32[]{:S(2)}) copy-start(bf16[192,16,16,32]{0,3,2,1:T(8,128)(2,1)S(1)} %constant_dynamic-update-slice_fusion.1) | copy-start | bytes 9437188
  125.9 16.8 %collective-permute-start.4 = (bf16[192,1,16,32]{0,3,2,1:T(8,128)(2,1)S(1)}, bf16[192,1,16,32]{0,3,2,1:T(8,128)(2,1)S(1)}, u32[]{:S(2)}, u32[]{:S(2)}) collective-permute-start(bf16[192,1,16,32]{0,3,2,1:T(8,128)(2,1)S(1)} %get-tuple-element.124), channel_id=1, source_target_pairs={{0,8},{8,16},{16,24},{24,32},{32,40},{40,48},{48,56},{56,64},{64,7... | collective-permute-start | bytes 589832 | tf_op jit(solution)/shard_map/ppermute | solution.py:16
  127.8 14.8 %collective-permute-start.5 = (bf16[192,1,16,32]{0,3,2,1:T(8,128)(2,1)S(1)}, bf16[192,1,16,32]{0,3,2,1:T(8,128)(2,1)S(1)}, u32[]{:S(2)}, u32[]{:S(2)}) collective-permute-start(bf16[192,1,16,32]{0,3,2,1:T(8,128)(2,1)S(1)} %get-tuple-element.125), channel_id=1, source_target_pairs={{8,0},{16,8},{24,16},{32,24},{40,32},{48,40},{56,48},{64,56},{72,6... | collective-permute-start | bytes 589832 | tf_op jit(solution)/shard_map/ppermute | solution.py:19
  142.7 1.0 copy-start.10
  142.7 1.0 copy-start.11
  143.7 367.2 %collective-permute-start.6 = (bf16[192,18,1,32]{0,3,2,1:T(8,128)(2,1)}, bf16[192,18,1,32]{0,3,2,1:T(8,128)(2,1)}, u32[]{:S(2)}, u32[]{:S(2)}) collective-permute-start(bf16[192,18,1,32]{0,3,2,1:T(8,128)(2,1)} %get-tuple-element.120), channel_id=1, source_target_pairs={{0,1},{1,2},{2,3},{3,4},{4,5},{5,6},{6,7},{8,9},{9,10},{10,11},{11... | collective-permute-start | bytes 663560 | tf_op jit(solution)/shard_map/ppermute | solution.py:16
  146.0 364.8 %collective-permute-start.7 = (bf16[192,18,1,32]{0,3,2,1:T(8,128)(2,1)}, bf16[192,18,1,32]{0,3,2,1:T(8,128)(2,1)}, u32[]{:S(2)}, u32[]{:S(2)}) collective-permute-start(bf16[192,18,1,32]{0,3,2,1:T(8,128)(2,1)} %get-tuple-element.121), channel_id=1, source_target_pairs={{1,0},{2,1},{3,2},{4,3},{5,4},{6,5},{7,6},{9,8},{10,9},{11,10},{12... | collective-permute-start | bytes 663560 | tf_op jit(solution)/shard_map/ppermute | solution.py:19
  564.8 8.0 %copy-start.15 = (f32[1,192,4,4,4]{1,4,3,2,0:T(4,128)S(1)}, f32[1,192,4,4,4]{1,4,3,2,0:T(4,128)}, u32[]{:S(2)}) copy-start(f32[1,192,4,4,4]{1,4,3,2,0:T(4,128)} %reshape.545) | copy-start | bytes 147460
  570.6 3.3 copy-start.6
  570.6 3.3 copy-start.7
Sparse Core Ops, SparseCore 0:
  511.0 38.9 reduce-scatter.3
where the time goes:
time: 589 us; the launch traced here: 584 us
  blocking collectives  359 us (61%)
  local copies, waits for them, and re-layouts  98.5 us (17%)
  matrix products  37.3 us (6%)
  starting transfers between devices  35.9 us (6%)
  between operations  26.8 us (5%)
  other arithmetic  19.4 us (3%)
  waiting for transfers between devices  6.65 us (1%)
    psum x1, blocking collectives, local(): slab_sum = lax.psum(local_grad, 'gx')  359 us
    concatenate x4, local copies, waits for them, and re-layouts, columns(): return jnp.concatenate(shifted, 0)  41 us
    ppermute x4, starting transfers between devices, padded_2(): lax.ppermute(lax.slice_in_dim(block, 0, width, axis=dim), axis, backward)  26.3 us
    slice x2, local copies, waits for them, and re-layouts, columns(): window[:, first_x:first_x + 8, first_y:first_y + 8, first_z:first_z + 8]  21.5 us
    concatenate x2, other arithmetic, padded_2(): block = jnp.concatenate([low, block, high], axis=dim)  14.9 us
    dot_general x2, matrix products, forward_slot(): pre = jnp.dot(weight_flat, hidden_cols, preferred_element_type=jnp.float32)  13.1 us
  transfers between devices with their start and end apart: 9, of which 3 were waited for; matrix products, arithmetic and copies ran while one was open for 13% of the time, Pallas kernels for 0%

commit v1 on v0

--- a/solution.py
+++ b/solution.py
@@ -119,6 +119,99 @@
 
 def pad_depth(volume):
     return jnp.pad(volume, ((0, 0), (0, 0), (0, 0), (1, 1)))
+
+
+XS, YS, ZL, ZH, CORES = 4, 8, 2, 4, 2
+PAD_LANES = 1408
+
+
+def gx_pairs(move):
+    pairs = []
+    for low in range(ZL):
+        for row in range(YS):
+            for col in range(XS):
+                to_low, to_row, to_col = move(low, row, col)
+                pairs.append(((low * YS + row) * XS + col, (to_low * YS + to_row) * XS + to_col))
+    return pairs
+
+
+def gy_pairs(move):
+    pairs = []
+    for high in range(ZH):
+        for core in range(CORES):
+            to_high, to_core = move(high, core)
+            pairs.append((high * CORES + core, to_high * CORES + to_core))
+    return pairs
+
+
+def pick(array, index, axis):
+    return lax.dynamic_index_in_dim(array, index, axis, keepdims=False)
+
+
+def wire(array, axis, pairs):
+    return lax.ppermute(array.astype(jnp.bfloat16), axis, pairs)
+
+
+def reduce_grad(local_grad):
+    rows = local_grad.shape[0]
+    part = rows // (ZH * CORES)
+    gx = lax.axis_index("gx")
+    gy = lax.axis_index("gy")
+    core, high = gy % CORES, gy // CORES
+    col, row = gx % XS, (gx // XS) % YS
+    total = local_grad.shape[1]
+    padded = jnp.pad(local_grad, ((0, 0), (0, XS * PAD_LANES - total)))
+    split = padded.reshape(ZH, CORES, part, XS * PAD_LANES)
+    held = pick(split, core, 1) + wire(
+        pick(split, 1 - core, 1), "gy", gy_pairs(lambda h, c: (h, 1 - c))
+    ).astype(jnp.float32)
+    def lanes_of(array, index):
+        return lax.dynamic_slice_in_dim(array, index * PAD_LANES, PAD_LANES, axis=2)
+
+    arrived = []
+    for step in (1, 3, 2):
+        piece = lanes_of(held, (col + step) % XS)
+        arrived.append(wire(piece, "gx", gx_pairs(lambda l, r, c, s=step: (l, r, (c + s) % XS))))
+    held = lanes_of(held, col)
+    for piece in arrived:
+        held = held + piece.astype(jnp.float32)
+    held = held.reshape(ZH, part // YS, 2, 2, 2, PAD_LANES)
+    for bit, axis in ((0, 4), (1, 3), (2, 2)):
+        mine = (row >> bit) & 1
+        got = wire(
+            pick(held, 1 - mine, axis),
+            "gx",
+            gx_pairs(lambda l, r, c, b=bit: (l, r ^ (1 << b), c)),
+        )
+        held = pick(held, mine, axis) + got.astype(jnp.float32)
+    arrived = []
+    for step in (1, 3, 2):
+        piece = pick(held, (high + step) % ZH, 0)
+        arrived.append(wire(piece, "gy", gy_pairs(lambda h, c, s=step: ((h + s) % ZH, c))))
+    held = pick(held, high, 0)
+    for piece in arrived:
+        held = held + piece.astype(jnp.float32)
+    mine = held.astype(jnp.bfloat16)
+    other = wire(mine, "gx", gx_pairs(lambda l, r, c: (1 - l, r, c)))
+    held = (mine.astype(jnp.float32) + other.astype(jnp.float32)).astype(jnp.bfloat16)
+    held = held.reshape(part // YS, PAD_LANES)
+    for bit in (2, 1, 0):
+        mine = ((row >> bit) & 1) == 0
+        other = wire(held, "gx", gx_pairs(lambda l, r, c, b=bit: (l, r ^ (1 << b), c)))
+        low = jnp.where(mine, held, other)
+        high_half = jnp.where(mine, other, held)
+        held = jnp.stack([low, high_half], axis=1) if bit == 2 else jnp.stack(
+            [low, high_half], axis=held.ndim - 1
+        )
+    held = held.reshape(part, PAD_LANES)
+    pieces = jnp.zeros((part, XS * PAD_LANES), jnp.bfloat16)
+    pieces = lax.dynamic_update_slice_in_dim(pieces, held, col * PAD_LANES, axis=1)
+    for step in (1, 3, 2):
+        other = wire(held, "gx", gx_pairs(lambda l, r, c, s=step: (l, r, (c + s) % XS)))
+        pieces = lax.dynamic_update_slice_in_dim(
+            pieces, other, ((col - step) % XS) * PAD_LANES, axis=1
+        )
+    return pieces[:, :total].astype(jnp.float32)
 
 
 def local(
@@ -171,10 +264,7 @@
         skip_list.append((backprop_one * occupied[member]).astype(jnp.bfloat16))
     grad_skip = jnp.stack(skip_list, 0)
     grad_coarse = coarse_gradient(grad_skip, parents, octants, coarse_count, up_rows)
-    slab_sum = lax.psum(local_grad, "gx")
-    grad_conv = lax.psum_scatter(
-        slab_sum.astype(jnp.bfloat16), "gy", scatter_dimension=0, tiled=True
-    ).astype(jnp.float32)
+    grad_conv = reduce_grad(local_grad)
     return (grad_skip, grad_coarse, grad_conv.reshape(grad_conv.shape[0], 27, channel_count))
 
 

time: 589 us -> 322 us (0.55)
  the two profiles are of different devices: /device:TPU:320 before, /device:TPU:24 now
where the time goes in v1:
time: 322 us; the launch traced here: 317 us
  local copies, waits for them, and re-layouts  98.1 us (30%)
  starting transfers between devices  91.5 us (28%)
  waiting for transfers between devices  59.6 us (19%)
  matrix products  31.6 us (10%)
  other arithmetic  22.4 us (7%)
  between operations  14.1 us (4%)
    ppermute x17, starting transfers between devices, wire(): return lax.ppermute(array.astype(jnp.bfloat16), axis, pairs)  68.2 us
    ppermute x17, waiting for transfers between devices, wire(): return lax.ppermute(array.astype(jnp.bfloat16), axis, pairs)  45.8 us
    concatenate x4, local copies, waits for them, and re-layouts, columns(): return jnp.concatenate(shifted, 0)  40.9 us
    slice x2, local copies, waits for them, and re-layouts, columns(): window[:, first_x:first_x + 8, first_y:first_y + 8, first_z:first_z + 8]  21.5 us
    concatenate x2, other arithmetic, padded_2(): block = jnp.concatenate([low, block, high], axis=dim)  13.6 us
    dot_general x2, matrix products, forward_slot(): pre = jnp.dot(weight_flat, hidden_cols, preferred_element_type=jnp.float32)  12.9 us
    ppermute x4, starting transfers between devices, padded_2(): lax.ppermute(lax.slice_in_dim(block, 0, width, axis=dim), axis, backward)  12.7 us
    ppermute x4, starting transfers between devices, padded_2(): lax.ppermute(lax.slice_in_dim(block, block.shape[dim] - width, None, axis...  10.6 us
  transfers between devices with their start and end apart: 25, of which 14 were waited for; matrix products, arithmetic and copies ran while one was open for 21% of the time, Pallas kernels for 0%

profile of v1, /device:TPU:24, one launch (start us, length us, event | category | flops | bytes accessed | tf_op | source)
XLA Modules:
  0.0 317.4 jit_solution(15805593005762227085)
XLA Ops:
  1.4 1.2 gather_fusion
  5.8 1.3 fusion.48
  11.6 1.6 fusion.45
  25.3 1.2 constant_dynamic-update-slice_fusion.8
  27.6 3.4 %collective-permute-start = (bf16[192,1,16,32]{0,3,2,1:T(8,128)(2,1)S(1)}, bf16[192,1,16,32]{0,3,2,1:T(8,128)(2,1)S(1)}, u32[]{:S(2)}, u32[]{:S(2)}) collective-permute-start(bf16[192,1,16,32]{0,3,2,1:T(8,128)(2,1)S(1)} %get-tuple-element.129), channel_id=1, source_target_pairs={{0,8},{8,16},{16,24},{24,32},{32,40},{40,48},{48,56},{56,64},{64,7... | collective-permute-start | bytes 589832 | tf_op jit(solution)/shard_map/ppermute | solution.py:16
  31.0 4.5 %collective-permute-start.1 = (bf16[192,1,16,32]{0,3,2,1:T(8,128)(2,1)S(1)}, bf16[192,1,16,32]{0,3,2,1:T(8,128)(2,1)S(1)}, u32[]{:S(2)}, u32[]{:S(2)}) collective-permute-start(bf16[192,1,16,32]{0,3,2,1:T(8,128)(2,1)S(1)} %get-tuple-element.130), channel_id=1, source_target_pairs={{8,0},{16,8},{24,16},{32,24},{40,32},{48,40},{56,48},{64,56},{72,6... | collective-permute-start | bytes 589832 | tf_op jit(solution)/shard_map/ppermute | solution.py:19
  35.6 4.1 %collective-permute-done = bf16[192,1,16,32]{0,3,2,1:T(8,128)(2,1)S(1)} collective-permute-done((bf16[192,1,16,32]{0,3,2,1:T(8,128)(2,1)S(1)}, bf16[192,1,16,32]{0,3,2,1:T(8,128)(2,1)S(1)}, u32[]{:S(2)}, u32[]{:S(2)}) %collective-permute-start) | collective-permute-done | bytes 196640 | tf_op jit(solution)/shard_map/ppermute | solution.py:16
  41.8 2.0 collective-permute-start.2
  43.8 1.5 collective-permute-start.3
  45.6 3.4 %copy.81 = bf16[192,27,192]{0,2,1:T(8,128)(2,1)} copy(bf16[192,27,192]{2,0,1:T(8,128)(2,1)S(1)} %copy-done.2) | data formatting | bytes 3981312 | tf_op args[7]
  49.7 1.6 collective-permute-done.3
  51.3 7.4 %fusion.10 = bf16[192,18,18,34]{0,3,2,1:T(8,128)(2,1)S(1)} fusion(bf16[192,18,1,32]{0,3,2,1:T(8,128)(2,1)} %collective-permute-done.3, bf16[192,18,1,32]{0,3,2,1:T(8,128)(2,1)} %collective-permute-done.2, bf16[192,1,16,32]{0,3,2,1:T(8,128)(2,1)} %copy-done.11, bf16[192,16,16,32]{0,3,2,1:T(8,128)(2,1)} %copy-done.1, bf16[192,1,16,32]{0,3,2,1:T(8,128)(2,1)} %copy-done.10), kind=kLoop, calls=%fused_computation.16 | loop fusion | flops 38071296 | bytes 8211456 | tf_op jit(solution)/shard_map/concatenate | solution.py:20
  58.7 10.6 %constant_dynamic-slice_fusion.114 = (bf16[192,8,8,8]{0,3,2,1:T(8,128)(2,1)}, bf16[192,8,8,8]{0,3,2,1:T(8,128)(2,1)}, bf16[192,8,8,8]{0,3,2,1:T(8,128)(2,1)}, bf...) fusion(bf16[192,18,18,34]{0,3,2,1:T(8,128)(2,1)S(1)} %fusion.10, ...), kind=kLoop, calls=%fused_computation.199 | loop fusion | bytes 21233736 | tf_op jit(solution)/shard_map/slice | solution.py:92
  69.4 10.2 %concatenate.26 = bf16[5184,512]{0,1:T(8,128)(2,1)} concatenate(bf16[192,512]{0,1:T(8,128)(2,1)} %bitcast.396, bf16[192,512]{0,1:T(8,128)(2,1)} %bitcast.395, bf16[192,512]{0,1:T(8,128)(2,1)} %bitcast.394, bf16[192,512]{0,1:T(8,128)(2,1)} %bitcast.393, bf16[192,512]{0,1:T(8,128)(2,1)} %bitcast.392, bf16[192,512]{0,1:T(8,128)(2,1)} %bitcast.391, bf16[192,512]{0,1:T(8,128)(2,1)} %bitcast.390, ...), dimensions={0} | concatenate | bytes 10616832 | tf_op jit(solution)/shard_map/concatenate | solution.py:96
  79.6 5.4 %convolution_bitcast_fusion.3 = f32[192,512]{1,0:T(8,128)S(1)} fusion(bf16[5184,512]{0,1:T(8,128)(2,1)} %concatenate.26, bf16[192,5184]{0,1:T(8,128)(2,1)} %bitcast.279), kind=kOutput, calls=%fused_computation.28 | convolution fusion | flops 1019215872 | bytes 7692288 | tf_op jit(solution)/shard_map/dot_general | solution.py:100
  85.1 3.8 %fusion.24 = f32[192,5184]{1,0:T(8,128)} fusion(bf16[5184,512]{0,1:T(8,128)(2,1)S(1)} %copy-done.4, f32[192,512]{1,0:T(8,128)S(1)} %convolution_bitcast_fusion.3, f32[]{:T(128)} %bitcast.54, bf16[2,192,512]{2,1,0:T(8,128)(2,1)S(1)} %copy-done.15), kind=kOutput, calls=%fused_computation.50 | convolution fusion | flops 1020297216 | bytes 9945092 | tf_op jit(solution)/shard_map/dot_general | solution.py:254
  88.9 10.2 %concatenate.27 = bf16[5184,512]{0,1:T(8,128)(2,1)} concatenate(bf16[192,512]{0,1:T(8,128)(2,1)} %bitcast.370, bf16[192,512]{0,1:T(8,128)(2,1)} %bitcast.369, bf16[192,512]{0,1:T(8,128)(2,1)} %bitcast.368, bf16[192,512]{0,1:T(8,128)(2,1)} %bitcast.367, bf16[192,512]{0,1:T(8,128)(2,1)} %bitcast.366, bf16[192,512]{0,1:T(8,128)(2,1)} %bitcast.365, bf16[192,512]{0,1:T(8,128)(2,1)} %bitcast.364, ...), dimensions={0} | concatenate | bytes 10616832 | tf_op jit(solution)/shard_map/concatenate | solution.py:96
  99.1 7.5 %fusion.20 = (bf16[192,512]{1,0:T(8,128)(2,1)}, bf16[192,512]{1,0:T(8,128)(2,1)}, f32[192,512]{1,0:T(8,128)}) fusion(f32[]{:T(128)} %bitcast.85, bf16[2,192,512]{2,1,0:T(8,128)(2,1)} %param.11, f32[]{:T(128)} %bitcast.54, f32[192,512]{1,0:T(8,128)} %copy-done.12, bf16[5184,512]{0,1:T(8,128)(2,1)} %concatenate.27, bf16[192,5184]{0,1:T(8,128)(2,1)} %bitcast.280), kind=kOutput, calls=%fused_computation.46 | convolution fusion | flops 1021378560 | bytes 8871944 | tf_op jit(solution)/shard_map/dot_general | solution.py:100
  106.6 1.8 copy.82
  108.4 1.8 copy.83
  110.7 1.2 constant_dynamic-update-slice_fusion.6
  113.0 3.2 %collective-permute-start.4 = (bf16[192,1,16,32]{0,3,2,1:T(8,128)(2,1)S(1)}, bf16[192,1,16,32]{0,3,2,1:T(8,128)(2,1)S(1)}, u32[]{:S(2)}, u32[]{:S(2)}) collective-permute-start(bf16[192,1,16,32]{0,3,2,1:T(8,128)(2,1)S(1)} %get-tuple-element.127), channel_id=1, source_target_pairs={{0,8},{8,16},{16,24},{24,32},{32,40},{40,48},{48,56},{56,64},{64,7... | collective-permute-start | bytes 589832 | tf_op jit(solution)/shard_map/ppermute | solution.py:16
  116.2 5.4 %collective-permute-start.5 = (bf16[192,1,16,32]{0,3,2,1:T(8,128)(2,1)S(1)}, bf16[192,1,16,32]{0,3,2,1:T(8,128)(2,1)S(1)}, u32[]{:S(2)}, u32[]{:S(2)}) collective-permute-start(bf16[192,1,16,32]{0,3,2,1:T(8,128)(2,1)S(1)} %get-tuple-element.128), channel_id=1, source_target_pairs={{8,0},{16,8},{24,16},{32,24},{40,32},{48,40},{56,48},{64,56},{72,6... | collective-permute-start | bytes 589832 | tf_op jit(solution)/shard_map/ppermute | solution.py:19
  121.7 4.5 %convolution_add_fusion = f32[192,5184]{1,0:T(8,128)S(1)} fusion(f32[192,5184]{1,0:T(8,128)S(1)} %copy-done.7, bf16[5184,512]{0,1:T(8,128)(2,1)} %concatenate.27, f32[192,512]{1,0:T(8,128)S(1)} %copy-done.13, f32[]{:T(128)} %bitcast.85, bf16[2,192,512]{2,1,0:T(8,128)(2,1)S(1)} %copy-done.16), kind=kOutput, calls=%fused_computation.4 | convolution fusion | flops 1021292544 | bytes 13910020 | tf_op jit(solution)/shard_map/dot_general | solution.py:254
  126.8 1.6 copy.121
  128.4 10.7 %collective-permute-start.8 = (bf16[4,24,5632]{2,0,1:T(4,128)(2,1)}, bf16[4,24,5632]{2,0,1:T(4,128)(2,1)}, u32[]{:S(2)}, u32[]{:S(2)}) collective-permute-start(bf16[4,24,5632]{2,0,1:T(4,128)(2,1)} %bitcast.261), channel_id=1, source_target_pairs={{0,1},{1,0},{2,3},{3,2},{4,5},{5,4},{6,7},{7,6},{8,9},{9,8},{10,11... | collective-permute-start | bytes 3244040 | tf_op jit(solution)/shard_map/ppermute | solution.py:152
  139.2 1.9 collective-permute-start.6
  141.2 1.3 collective-permute-start.7
  142.5 1.5 constant_dynamic-slice_fusion.110
  144.0 6.9 %collective-permute-done.7 = bf16[192,18,1,32]{0,3,2,1:T(8,128)(2,1)S(1)} collective-permute-done((bf16[192,18,1,32]{0,3,2,1:T(8,128)(2,1)S(1)}, bf16[192,18,1,32]{0,3,2,1:T(8,128)(2,1)S(1)}, u32[]{:S(2)}, u32[]{:S(2)}) %collective-permute-start.7) | collective-permute-done | bytes 221216 | tf_op jit(solution)/shard_map/ppermute | solution.py:19
  150.8 6.2 %select_maximum_fusion = bf16[192,18,18,34]{0,3,2,1:T(8,128)(2,1)S(1)} fusion(bf16[192,18,1,32]{0,3,2,1:T(8,128)(2,1)S(1)} %collective-permute-done.7, bf16[192,18,1,32]{0,3,2,1:T(8,128)(2,1)S(1)} %collective-permute-done.6, bf16[192,1,16,32]{0,3,2,1:T(8,128)(2,1)S(1)} %collective-permute-done.5, ...), kind=kLoop, calls=%fused_computation.5 | loop fusion | flops 38071296 | bytes 8211456 | tf_op jit(solution)/shard_map/concatenate | solution.py:20
  157.0 10.9 %constant_dynamic-slice_fusion.113 = (bf16[192,8,8,8]{0,3,2,1:T(8,128)(2,1)}, bf16[192,8,8,8]{0,3,2,1:T(8,128)(2,1)}, bf16[192,8,8,8]{0,3,2,1:T(8,128)(2,1)}, bf...) fusion(bf16[192,18,18,34]{0,3,2,1:T(8,128)(2,1)S(1)} %select_ma, ...), kind=kLoop, calls=%fused_computation.197 | loop fusion | bytes 21233736 | tf_op jit(solution)/shard_map/slice | solution.py:92
  167.9 10.2 %concatenate.30 = bf16[5184,512]{0,1:T(8,128)(2,1)} concatenate(bf16[192,512]{0,1:T(8,128)(2,1)} %bitcast.343, bf16[192,512]{0,1:T(8,128)(2,1)} %bitcast.342, bf16[192,512]{0,1:T(8,128)(2,1)} %bitcast.341, bf16[192,512]{0,1:T(8,128)(2,1)} %bitcast.340, bf16[192,512]{0,1:T(8,128)(2,1)} %bitcast.339, bf16[192,512]{0,1:T(8,128)(2,1)} %bitcast.338, bf16[192,512]{0,1:T(8,128)(2,1)} %bitcast.337, ...), dimensions={0} | concatenate | bytes 10616832 | tf_op jit(solution)/shard_map/concatenate | solution.py:96
  178.2 10.2 %concatenate.31 = bf16[5184,512]{0,1:T(8,128)(2,1)} concatenate(bf16[192,512]{0,1:T(8,128)(2,1)} %bitcast.315, bf16[192,512]{0,1:T(8,128)(2,1)} %bitcast.314, bf16[192,512]{0,1:T(8,128)(2,1)} %bitcast.313, bf16[192,512]{0,1:T(8,128)(2,1)} %bitcast.312, bf16[192,512]{0,1:T(8,128)(2,1)} %bitcast.311, bf16[192,512]{0,1:T(8,128)(2,1)} %bitcast.310, bf16[192,512]{0,1:T(8,128)(2,1)} %bitcast.309, ...), dimensions={0} | concatenate | bytes 10616832 | tf_op jit(solution)/shard_map/concatenate | solution.py:96
  188.4 5.8 %fusion.15 = bf16[512,192]{0,1:T(8,128)(2,1)} fusion(bf16[5184,512]{0,1:T(8,128)(2,1)} %concatenate.30, bf16[192,5184]{0,1:T(8,128)(2,1)S(1)} %bitcast.275, f32[]{:T(128)} %bitcast.54), kind=kOutput, calls=%fused_computation.29 | convolution fusion | flops 1019412480 | bytes 7495684 | tf_op jit(solution)/shard_map/dot_general | solution.py:263
  194.2 3.1 bitcast_add_fusion
  197.3 1.4 copy-done.6
  199.8 6.1 %collective-permute-start.10 = (bf16[4,24,1408]{2,0,1:T(4,128)(2,1)}, bf16[4,24,1408]{2,0,1:T(4,128)(2,1)}, u32[]{:S(2)}, u32[]{:S(2)}) collective-permute-start(bf16[4,24,1408]{2,0,1:T(4,128)(2,1)} %get-tuple-element.133), channel_id=1, source_target_pairs={{0,24},{8,0},{16,8},{24,16},{32,56},{40,32},{48,40},{56,48},{64,88... | collective-permute-start | bytes 811016 | tf_op jit(solution)/shard_map/ppermute | solution.py:152
  205.9 1.9 collective-permute-start.11
  207.8 3.0 collective-permute-start.9
  210.9 3.3 %fusion.16 = bf16[512,192]{0,1:T(8,128)(2,1)} fusion(bf16[5184,512]{0,1:T(8,128)(2,1)S(1)} %copy-done.3, bf16[192,5184]{0,1:T(8,128)(2,1)S(1)} %bitcast.276, f32[]{:T(128)} %bitcast.85), kind=kOutput, calls=%fused_computation.30 | convolution fusion | flops 1019412480 | bytes 7495684 | tf_op jit(solution)/shard_map/dot_general | solution.py:263
  219.0 1.5 convert_add_fusion
  220.7 1.9 collective-permute-start.12
  222.7 4.9 %collective-permute-done.12 = bf16[4,3,2,2,1408]{4,3,2,1,0:T(2,128)(2,1)S(1)} collective-permute-done((bf16[4,3,2,2,1408]{4,3,2,1,0:T(2,128)(2,1)S(1)}, bf16[4,3,2,2,1408]{4,3,2,1,0:T(2,128)(2,1)S(1)}, u32[]{:S(2)}, u32[]{:S(2)}) %collective-permute-start.12) | collective-permute-done | bytes 135200 | tf_op jit(solution)/shard_map/ppermute | solution.py:152
  228.0 1.9 collective-permute-start.13
  230.1 5.2 %collective-permute-done.13 = bf16[4,3,2,1408]{3,2,1,0:T(2,128)(2,1)S(1)} collective-permute-done((bf16[4,3,2,1408]{3,2,1,0:T(2,128)(2,1)S(1)}, bf16[4,3,2,1408]{3,2,1,0:T(2,128)(2,1)S(1)}, u32[]{:S(2)}, u32[]{:S(2)}) %collective-permute-start.13) | collective-permute-done | bytes 67616 | tf_op jit(solution)/shard_map/ppermute | solution.py:152
  235.5 1.9 collective-permute-start.14
  237.5 8.0 %collective-permute-done.14 = bf16[4,3,1408]{2,0,1:T(4,128)(2,1)S(1)} collective-permute-done((bf16[4,3,1408]{2,0,1:T(4,128)(2,1)S(1)}, bf16[4,3,1408]{2,0,1:T(4,128)(2,1)S(1)}, u32[]{:S(2)}, u32[]{:S(2)}) %collective-permute-start.14) | collective-permute-done | bytes 33824 | tf_op jit(solution)/shard_map/ppermute | solution.py:152
  245.6 15.8 %collective-permute-start.15 = (bf16[3,1408]{1,0:T(4,128)(2,1)S(1)}, bf16[3,1408]{1,0:T(4,128)(2,1)S(1)}, u32[]{:S(2)}, u32[]{:S(2)}) collective-permute-start(bf16[3,1408]{1,0:T(4,128)(2,1)S(1)} %bitcast.409), channel_id=1, source_target_pairs={{0,2},{1,3},{2,4},{3,5},{4,6},{5,7},{6,0},{7,1},{8,10},{9,11},{10,... | collective-permute-start | bytes 25352 | tf_op jit(solution)/shard_map/ppermute | solution.py:152
  261.4 1.9 collective-permute-start.16
  263.4 5.9 %collective-permute-start.17 = (bf16[3,1408]{1,0:T(4,128)(2,1)S(1)}, bf16[3,1408]{1,0:T(4,128)(2,1)S(1)}, u32[]{:S(2)}, u32[]{:S(2)}) collective-permute-start(bf16[3,1408]{1,0:T(4,128)(2,1)S(1)} %bitcast.411), channel_id=1, source_target_pairs={{0,4},{1,5},{2,6},{3,7},{4,0},{5,1},{6,2},{7,3},{8,12},{9,13},{10,... | collective-permute-start | bytes 25352 | tf_op jit(solution)/shard_map/ppermute | solution.py:152
  269.3 3.7 %collective-permute-done.17 = bf16[3,1408]{1,0:T(4,128)(2,1)S(1)} collective-permute-done((bf16[3,1408]{1,0:T(4,128)(2,1)S(1)}, bf16[3,1408]{1,0:T(4,128)(2,1)S(1)}, u32[]{:S(2)}, u32[]{:S(2)}) %collective-permute-start.17) | collective-permute-done | bytes 8480 | tf_op jit(solution)/shard_map/ppermute | solution.py:152
  273.0 1.9 collective-permute-start.18
  275.2 3.4 %collective-permute-done.18 = bf16[3,1408]{1,0:T(4,128)(2,1)S(1)} collective-permute-done((bf16[3,1408]{1,0:T(4,128)(2,1)S(1)}, bf16[3,1408]{1,0:T(4,128)(2,1)S(1)}, u32[]{:S(2)}, u32[]{:S(2)}) %collective-permute-start.18) | collective-permute-done | bytes 8480 | tf_op jit(solution)/shard_map/ppermute | solution.py:152
  278.6 2.2 collective-permute-start.19
  281.0 7.1 %collective-permute-done.19 = bf16[3,1408]{1,0:T(4,128)(2,1)S(1)} collective-permute-done((bf16[3,1408]{1,0:T(4,128)(2,1)S(1)}, bf16[3,1408]{1,0:T(4,128)(2,1)S(1)}, u32[]{:S(2)}, u32[]{:S(2)}) %collective-permute-start.19) | collective-permute-done | bytes 8480 | tf_op jit(solution)/shard_map/ppermute | solution.py:152
  288.1 1.9 collective-permute-start.20
  290.1 4.6 %collective-permute-done.20 = bf16[3,2,1408]{2,0,1:T(4,128)(2,1)S(1)} collective-permute-done((bf16[3,2,1408]{2,0,1:T(4,128)(2,1)S(1)}, bf16[3,2,1408]{2,0,1:T(4,128)(2,1)S(1)}, u32[]{:S(2)}, u32[]{:S(2)}) %collective-permute-start.20) | collective-permute-done | bytes 16928 | tf_op jit(solution)/shard_map/ppermute | solution.py:152
  294.8 1.9 collective-permute-start.21
  298.6 2.2 collective-permute-done.21
  301.0 1.9 collective-permute-start.22
  302.9 5.1 %collective-permute-start.23 = (bf16[24,1408]{1,0:T(8,128)(2,1)S(1)}, bf16[24,1408]{1,0:T(8,128)(2,1)S(1)}, u32[]{:S(2)}, u32[]{:S(2)}) collective-permute-start(bf16[24,1408]{1,0:T(8,128)(2,1)S(1)} %reshape.567), channel_id=1, source_target_pairs={{0,24},{8,0},{16,8},{24,16},{32,56},{40,32},{48,40},{56,48},{64,88... | collective-permute-start | bytes 202760 | tf_op jit(solution)/shard_map/ppermute | solution.py:152
  308.0 1.9 collective-permute-start.24
  310.1 5.6 %collective-permute-done.24 = bf16[24,1408]{1,0:T(8,128)(2,1)S(1)} collective-permute-done((bf16[24,1408]{1,0:T(8,128)(2,1)S(1)}, bf16[24,1408]{1,0:T(8,128)(2,1)S(1)}, u32[]{:S(2)}, u32[]{:S(2)}) %collective-permute-start.24) | collective-permute-done | bytes 67616 | tf_op jit(solution)/shard_map/ppermute | solution.py:152
  (134 shorter events, 25.6 us)
Async XLA Ops:
  0.6 18.9 %copy-start = (bf16[8,192,192]{2,1,0:T(8,128)(2,1)S(1)}, bf16[8,192,192]{2,1,0:T(8,128)(2,1)}, u32[]{:S(2)}) copy-start(bf16[8,192,192]{2,1,0:T(8,128)(2,1)} %param.17) | copy-start | bytes 1769476
  0.6 22.8 %copy-start.14 = (bf16[2,192,512]{2,1,0:T(8,128)(2,1)S(1)}, bf16[2,192,512]{2,1,0:T(8,128)(2,1)}, u32[]{:S(2)}) copy-start(bf16[2,192,512]{2,1,0:T(8,128)(2,1)} %param.9) | copy-start | bytes 1179652
  24.8 20.8 %copy-start.2 = (bf16[192,27,192]{2,0,1:T(8,128)(2,1)S(1)}, bf16[192,27,192]{2,0,1:T(8,128)(2,1)}, u32[]{:S(2)}) copy-start(bf16[192,27,192]{2,0,1:T(8,128)(2,1)} %param.16) | copy-start | bytes 5971972
  27.6 13.3 %copy-start.1 = (bf16[192,16,16,32]{0,3,2,1:T(8,128)(2,1)}, bf16[192,16,16,32]{0,3,2,1:T(8,128)(2,1)S(1)}, u32[]{:S(2)}) copy-start(bf16[192,16,16,32]{0,3,2,1:T(8,128)(2,1)S(1)} %constant_dynamic-update-slice_fusion.7) | copy-start | bytes 9437188
  27.6 12.0 %collective-permute-start = (bf16[192,1,16,32]{0,3,2,1:T(8,128)(2,1)S(1)}, bf16[192,1,16,32]{0,3,2,1:T(8,128)(2,1)S(1)}, u32[]{:S(2)}, u32[]{:S(2)}) collective-permute-start(bf16[192,1,16,32]{0,3,2,1:T(8,128)(2,1)S(1)} %get-tuple-element.129), channel_id=1, source_target_pairs={{0,8},{8,16},{16,24},{24,32},{32,40},{40,48},{48,56},{56,64},{64,7... | collective-permute-start | bytes 589832 | tf_op jit(solution)/shard_map/ppermute | solution.py:16
  31.0 9.8 %collective-permute-start.1 = (bf16[192,1,16,32]{0,3,2,1:T(8,128)(2,1)S(1)}, bf16[192,1,16,32]{0,3,2,1:T(8,128)(2,1)S(1)}, u32[]{:S(2)}, u32[]{:S(2)}) collective-permute-start(bf16[192,1,16,32]{0,3,2,1:T(8,128)(2,1)S(1)} %get-tuple-element.130), channel_id=1, source_target_pairs={{8,0},{16,8},{24,16},{32,24},{40,32},{48,40},{56,48},{64,56},{72,6... | collective-permute-start | bytes 589832 | tf_op jit(solution)/shard_map/ppermute | solution.py:19
  39.7 2.1 copy-start.10
  40.8 0.9 copy-start.11
  41.8 7.9 %collective-permute-start.2 = (bf16[192,18,1,32]{0,3,2,1:T(8,128)(2,1)}, bf16[192,18,1,32]{0,3,2,1:T(8,128)(2,1)}, u32[]{:S(2)}, u32[]{:S(2)}) collective-permute-start(bf16[192,18,1,32]{0,3,2,1:T(8,128)(2,1)} %get-tuple-element.125), channel_id=1, source_target_pairs={{0,1},{1,2},{2,3},{3,4},{4,5},{5,6},{6,7},{8,9},{9,10},{10,11},{11... | collective-permute-start | bytes 663560 | tf_op jit(solution)/shard_map/ppermute | solution.py:16
  43.8 7.5 %collective-permute-start.3 = (bf16[192,18,1,32]{0,3,2,1:T(8,128)(2,1)}, bf16[192,18,1,32]{0,3,2,1:T(8,128)(2,1)}, u32[]{:S(2)}, u32[]{:S(2)}) collective-permute-start(bf16[192,18,1,32]{0,3,2,1:T(8,128)(2,1)} %get-tuple-element.126), channel_id=1, source_target_pairs={{1,0},{2,1},{3,2},{4,3},{5,4},{6,5},{7,6},{9,8},{10,9},{11,10},{12... | collective-permute-start | bytes 663560 | tf_op jit(solution)/shard_map/ppermute | solution.py:19
  79.6 5.4 %copy-start.4 = (bf16[5184,512]{0,1:T(8,128)(2,1)S(1)}, bf16[5184,512]{0,1:T(8,128)(2,1)}, u32[]{:S(2)}) copy-start(bf16[5184,512]{0,1:T(8,128)(2,1)} %concatenate.26) | copy-start | bytes 15925252
  79.6 5.4 %copy-start.15 = (bf16[2,192,512]{2,1,0:T(8,128)(2,1)S(1)}, bf16[2,192,512]{2,1,0:T(8,128)(2,1)}, u32[]{:S(2)}) copy-start(bf16[2,192,512]{2,1,0:T(8,128)(2,1)} %param.11) | copy-start | bytes 1179652
  85.0 3.8 %copy-start.12 = (f32[192,512]{1,0:T(8,128)}, f32[192,512]{1,0:T(8,128)S(1)}, u32[]{:S(2)}) copy-start(f32[192,512]{1,0:T(8,128)S(1)} %convolution_bitcast_fusion.3) | copy-start | bytes 1179652
  110.1 11.5 %copy-start.7 = (f32[192,5184]{1,0:T(8,128)S(1)}, f32[192,5184]{1,0:T(8,128)}, u32[]{:S(2)}) copy-start(f32[192,5184]{1,0:T(8,128)} %fusion.24) | copy-start | bytes 11943940
  110.1 11.5 %copy-start.13 = (f32[192,512]{1,0:T(8,128)S(1)}, f32[192,512]{1,0:T(8,128)}, u32[]{:S(2)}) copy-start(f32[192,512]{1,0:T(8,128)} %get-tuple-element.165) | copy-start | bytes 1179652
  110.1 11.5 %copy-start.16 = (bf16[2,192,512]{2,1,0:T(8,128)(2,1)S(1)}, bf16[2,192,512]{2,1,0:T(8,128)(2,1)}, u32[]{:S(2)}) copy-start(bf16[2,192,512]{2,1,0:T(8,128)(2,1)} %param.11) | copy-start | bytes 1179652
  113.0 26.1 %collective-permute-start.4 = (bf16[192,1,16,32]{0,3,2,1:T(8,128)(2,1)S(1)}, bf16[192,1,16,32]{0,3,2,1:T(8,128)(2,1)S(1)}, u32[]{:S(2)}, u32[]{:S(2)}) collective-permute-start(bf16[192,1,16,32]{0,3,2,1:T(8,128)(2,1)S(1)} %get-tuple-element.127), channel_id=1, source_target_pairs={{0,8},{8,16},{16,24},{24,32},{32,40},{40,48},{48,56},{56,64},{64,7... | collective-permute-start | bytes 589832 | tf_op jit(solution)/shard_map/ppermute | solution.py:16
  116.2 22.9 %collective-permute-start.5 = (bf16[192,1,16,32]{0,3,2,1:T(8,128)(2,1)S(1)}, bf16[192,1,16,32]{0,3,2,1:T(8,128)(2,1)S(1)}, u32[]{:S(2)}, u32[]{:S(2)}) collective-permute-start(bf16[192,1,16,32]{0,3,2,1:T(8,128)(2,1)S(1)} %get-tuple-element.128), channel_id=1, source_target_pairs={{8,0},{16,8},{24,16},{32,24},{40,32},{48,40},{56,48},{64,56},{72,6... | collective-permute-start | bytes 589832 | tf_op jit(solution)/shard_map/ppermute | solution.py:19
  128.4 65.9 %collective-permute-start.8 = (bf16[4,24,5632]{2,0,1:T(4,128)(2,1)}, bf16[4,24,5632]{2,0,1:T(4,128)(2,1)}, u32[]{:S(2)}, u32[]{:S(2)}) collective-permute-start(bf16[4,24,5632]{2,0,1:T(4,128)(2,1)} %bitcast.261), channel_id=1, source_target_pairs={{0,1},{1,0},{2,3},{3,2},{4,5},{5,4},{6,7},{7,6},{8,9},{9,8},{10,11... | collective-permute-start | bytes 3244040 | tf_op jit(solution)/shard_map/ppermute | solution.py:152
  139.2 4.8 %collective-permute-start.6 = (bf16[192,18,1,32]{0,3,2,1:T(8,128)(2,1)S(1)}, bf16[192,18,1,32]{0,3,2,1:T(8,128)(2,1)S(1)}, u32[]{:S(2)}, u32[]{:S(2)}) collective-permute-start(bf16[192,18,1,32]{0,3,2,1:T(8,128)(2,1)S(1)} %get-tuple-element.123), channel_id=1, source_target_pairs={{0,1},{1,2},{2,3},{3,4},{4,5},{5,6},{6,7},{8,9},{9,10},{10,11},{11... | collective-permute-start | bytes 663560 | tf_op jit(solution)/shard_map/ppermute | solution.py:16
  141.2 9.7 %collective-permute-start.7 = (bf16[192,18,1,32]{0,3,2,1:T(8,128)(2,1)S(1)}, bf16[192,18,1,32]{0,3,2,1:T(8,128)(2,1)S(1)}, u32[]{:S(2)}, u32[]{:S(2)}) collective-permute-start(bf16[192,18,1,32]{0,3,2,1:T(8,128)(2,1)S(1)} %get-tuple-element.124), channel_id=1, source_target_pairs={{1,0},{2,1},{3,2},{4,3},{5,4},{6,5},{7,6},{9,8},{10,9},{11,10},{12... | collective-permute-start | bytes 663560 | tf_op jit(solution)/shard_map/ppermute | solution.py:19
  188.4 5.8 %copy-start.5 = (f32[4,1,24,5632]{3,2,1,0:T(8,128)S(1)}, f32[4,1,24,5632]{3,2,1,0:T(8,128)}, u32[]{:S(2)}) copy-start(f32[4,1,24,5632]{3,2,1,0:T(8,128)} %constant_dynamic-slice_fusion.110) | copy-start | bytes 6488068
  194.2 16.7 %copy-start.3 = (bf16[5184,512]{0,1:T(8,128)(2,1)S(1)}, bf16[5184,512]{0,1:T(8,128)(2,1)}, u32[]{:S(2)}) copy-start(bf16[5184,512]{0,1:T(8,128)(2,1)} %concatenate.31) | copy-start | bytes 15925252
  197.3 1.4 copy-start.6
  199.8 18.1 %collective-permute-start.10 = (bf16[4,24,1408]{2,0,1:T(4,128)(2,1)}, bf16[4,24,1408]{2,0,1:T(4,128)(2,1)}, u32[]{:S(2)}, u32[]{:S(2)}) collective-permute-start(bf16[4,24,1408]{2,0,1:T(4,128)(2,1)} %get-tuple-element.133), channel_id=1, source_target_pairs={{0,24},{8,0},{16,8},{24,16},{32,56},{40,32},{48,40},{56,48},{64,88... | collective-permute-start | bytes 811016 | tf_op jit(solution)/shard_map/ppermute | solution.py:152
  205.9 11.9 %collective-permute-start.11 = (bf16[4,24,1408]{2,0,1:T(4,128)(2,1)}, bf16[4,24,1408]{2,0,1:T(4,128)(2,1)}, u32[]{:S(2)}, u32[]{:S(2)}) collective-permute-start(bf16[4,24,1408]{2,0,1:T(4,128)(2,1)} %get-tuple-element.132), channel_id=1, source_target_pairs={{0,16},{8,24},{16,0},{24,8},{32,48},{40,56},{48,32},{56,40},{64,80... | collective-permute-start | bytes 811016 | tf_op jit(solution)/shard_map/ppermute | solution.py:152
  207.8 11.1 %collective-permute-start.9 = (bf16[4,24,1408]{2,0,1:T(4,128)(2,1)}, bf16[4,24,1408]{2,0,1:T(4,128)(2,1)}, u32[]{:S(2)}, u32[]{:S(2)}) collective-permute-start(bf16[4,24,1408]{2,0,1:T(4,128)(2,1)} %get-tuple-element.131), channel_id=1, source_target_pairs={{0,8},{8,16},{16,24},{24,0},{32,40},{40,48},{48,56},{56,32},{64,72... | collective-permute-start | bytes 811016 | tf_op jit(solution)/shard_map/ppermute | solution.py:152
  217.1 79.7 %copy-start.8 = (bf16[512,192]{0,1:T(8,128)(2,1)S(1)}, bf16[512,192]{0,1:T(8,128)(2,1)}, u32[]{:S(2)}) copy-start(bf16[512,192]{0,1:T(8,128)(2,1)} %fusion.15) | copy-start | bytes 589828
  217.1 79.7 %copy-start.9 = (bf16[512,192]{0,1:T(8,128)(2,1)S(1)}, bf16[512,192]{0,1:T(8,128)(2,1)}, u32[]{:S(2)}) copy-start(bf16[512,192]{0,1:T(8,128)(2,1)} %fusion.16) | copy-start | bytes 589828
  220.7 6.9 %collective-permute-start.12 = (bf16[4,3,2,2,1408]{4,3,2,1,0:T(2,128)(2,1)S(1)}, bf16[4,3,2,2,1408]{4,3,2,1,0:T(2,128)(2,1)S(1)}, u32[]{:S(2)}, u32[]{:S(2)}) collective-permute-start(bf16[4,3,2,2,1408]{4,3,2,1,0:T(2,128)(2,1)S(1)} %bitcast.406), channel_id=1, source_target_pairs={{0,32},{8,40},{16,48},{24,56},{32,0},{40,8},{48,16},{56,24},{64,96... | collective-permute-start | bytes 405512 | tf_op jit(solution)/shard_map/ppermute | solution.py:152
  228.0 7.3 %collective-permute-start.13 = (bf16[4,3,2,1408]{3,2,1,0:T(2,128)(2,1)S(1)}, bf16[4,3,2,1408]{3,2,1,0:T(2,128)(2,1)S(1)}, u32[]{:S(2)}, u32[]{:S(2)}) collective-permute-start(bf16[4,3,2,1408]{3,2,1,0:T(2,128)(2,1)S(1)} %bitcast.407), channel_id=1, source_target_pairs={{0,64},{8,72},{16,80},{24,88},{32,96},{40,104},{48,112},{56,120},{... | collective-permute-start | bytes 202760 | tf_op jit(solution)/shard_map/ppermute | solution.py:152
  235.5 10.0 %collective-permute-start.14 = (bf16[4,3,1408]{2,0,1:T(4,128)(2,1)S(1)}, bf16[4,3,1408]{2,0,1:T(4,128)(2,1)S(1)}, u32[]{:S(2)}, u32[]{:S(2)}) collective-permute-start(bf16[4,3,1408]{2,0,1:T(4,128)(2,1)S(1)} %bitcast.408), channel_id=1, source_target_pairs={{0,128},{8,136},{16,144},{24,152},{32,160},{40,168},{48,176},{56,1... | collective-permute-start | bytes 101384 | tf_op jit(solution)/shard_map/ppermute | solution.py:152
  245.6 23.7 %collective-permute-start.15 = (bf16[3,1408]{1,0:T(4,128)(2,1)S(1)}, bf16[3,1408]{1,0:T(4,128)(2,1)S(1)}, u32[]{:S(2)}, u32[]{:S(2)}) collective-permute-start(bf16[3,1408]{1,0:T(4,128)(2,1)S(1)} %bitcast.409), channel_id=1, source_target_pairs={{0,2},{1,3},{2,4},{3,5},{4,6},{5,7},{6,0},{7,1},{8,10},{9,11},{10,... | collective-permute-start | bytes 25352 | tf_op jit(solution)/shard_map/ppermute | solution.py:152
  261.4 7.8 %collective-permute-start.16 = (bf16[3,1408]{1,0:T(4,128)(2,1)S(1)}, bf16[3,1408]{1,0:T(4,128)(2,1)S(1)}, u32[]{:S(2)}, u32[]{:S(2)}) collective-permute-start(bf16[3,1408]{1,0:T(4,128)(2,1)S(1)} %bitcast.410), channel_id=1, source_target_pairs={{0,6},{1,7},{2,0},{3,1},{4,2},{5,3},{6,4},{7,5},{8,14},{9,15},{10,... | collective-permute-start | bytes 25352 | tf_op jit(solution)/shard_map/ppermute | solution.py:152
  263.4 9.6 %collective-permute-start.17 = (bf16[3,1408]{1,0:T(4,128)(2,1)S(1)}, bf16[3,1408]{1,0:T(4,128)(2,1)S(1)}, u32[]{:S(2)}, u32[]{:S(2)}) collective-permute-start(bf16[3,1408]{1,0:T(4,128)(2,1)S(1)} %bitcast.411), channel_id=1, source_target_pairs={{0,4},{1,5},{2,6},{3,7},{4,0},{5,1},{6,2},{7,3},{8,12},{9,13},{10,... | collective-permute-start | bytes 25352 | tf_op jit(solution)/shard_map/ppermute | solution.py:152
  273.0 5.6 %collective-permute-start.18 = (bf16[3,1408]{1,0:T(4,128)(2,1)S(1)}, bf16[3,1408]{1,0:T(4,128)(2,1)S(1)}, u32[]{:S(2)}, u32[]{:S(2)}) collective-permute-start(bf16[3,1408]{1,0:T(4,128)(2,1)S(1)} %fusion.36), channel_id=1, source_target_pairs={{0,256},{8,264},{16,272},{24,280},{32,288},{40,296},{48,304},{56,3... | collective-permute-start | bytes 25352 | tf_op jit(solution)/shard_map/ppermute | solution.py:152
  278.6 9.5 %collective-permute-start.19 = (bf16[3,1408]{1,0:T(4,128)(2,1)S(1)}, bf16[3,1408]{1,0:T(4,128)(2,1)S(1)}, u32[]{:S(2)}, u32[]{:S(2)}) collective-permute-start(bf16[3,1408]{1,0:T(4,128)(2,1)S(1)} %add_convert_fusion), channel_id=1, source_target_pairs={{0,128},{8,136},{16,144},{24,152},{32,160},{40,168},{48,176},{56,1... | collective-permute-start | bytes 25352 | tf_op jit(solution)/shard_map/ppermute | solution.py:152
  288.1 6.6 %collective-permute-start.20 = (bf16[3,2,1408]{2,0,1:T(4,128)(2,1)S(1)}, bf16[3,2,1408]{2,0,1:T(4,128)(2,1)S(1)}, u32[]{:S(2)}, u32[]{:S(2)}) collective-permute-start(bf16[3,2,1408]{2,0,1:T(4,128)(2,1)S(1)} %pad_maximum_fusion.9), channel_id=1, source_target_pairs={{0,64},{8,72},{16,80},{24,88},{32,96},{40,104},{48,112},{56,120},{... | collective-permute-start | bytes 50696 | tf_op jit(solution)/shard_map/ppermute | solution.py:152
  294.8 5.9 %collective-permute-start.21 = (bf16[3,2,2,1408]{3,0,1,2:T(4,128)(2,1)S(1)}, bf16[3,2,2,1408]{3,0,1,2:T(4,128)(2,1)S(1)}, u32[]{:S(2)}, u32[]{:S(2)}) collective-permute-start(bf16[3,2,2,1408]{3,0,1,2:T(4,128)(2,1)S(1)} %pad_maximum_fusion.8), channel_id=1, source_target_pairs={{0,32},{8,40},{16,48},{24,56},{32,0},{40,8},{48,16},{56,24},{64,96... | collective-permute-start | bytes 101384 | tf_op jit(solution)/shard_map/ppermute | solution.py:152
  301.0 9.1 %collective-permute-start.22 = (bf16[24,1408]{1,0:T(8,128)(2,1)S(1)}, bf16[24,1408]{1,0:T(8,128)(2,1)S(1)}, u32[]{:S(2)}, u32[]{:S(2)}) collective-permute-start(bf16[24,1408]{1,0:T(8,128)(2,1)S(1)} %reshape.567), channel_id=1, source_target_pairs={{0,8},{8,16},{16,24},{24,0},{32,40},{40,48},{48,56},{56,32},{64,72... | collective-permute-start | bytes 202760 | tf_op jit(solution)/shard_map/ppermute | solution.py:152
  302.9 7.2 %collective-permute-start.23 = (bf16[24,1408]{1,0:T(8,128)(2,1)S(1)}, bf16[24,1408]{1,0:T(8,128)(2,1)S(1)}, u32[]{:S(2)}, u32[]{:S(2)}) collective-permute-start(bf16[24,1408]{1,0:T(8,128)(2,1)S(1)} %reshape.567), channel_id=1, source_target_pairs={{0,24},{8,0},{16,8},{24,16},{32,56},{40,32},{48,40},{56,48},{64,88... | collective-permute-start | bytes 202760 | tf_op jit(solution)/shard_map/ppermute | solution.py:152
  308.0 7.7 %collective-permute-start.24 = (bf16[24,1408]{1,0:T(8,128)(2,1)S(1)}, bf16[24,1408]{1,0:T(8,128)(2,1)S(1)}, u32[]{:S(2)}, u32[]{:S(2)}) collective-permute-start(bf16[24,1408]{1,0:T(8,128)(2,1)S(1)} %reshape.567), channel_id=1, source_target_pairs={{0,16},{8,24},{16,0},{24,8},{32,48},{40,56},{48,32},{56,40},{64,80... | collective-permute-start | bytes 202760 | tf_op jit(solution)/shard_map/ppermute | solution.py:152

commit v2 on v0

v2 whole, which is shorter than its diff:
```python
import functools

import jax
import jax.numpy as jnp
from jax import lax
from jax.experimental import pallas as pl
from jax.experimental.pallas import tpu as pltpu
from jax.sharding import PartitionSpec as P

CH = 192
META = 16
ROWS = CH + META
VOX = 512
OFFSETS = 27
TAPS = OFFSETS * CH
FACE = 128
SOURCES = 2 * VOX + 2 * FACE + 2 * 2 * FACE
PLANES = 10
ZH, CORES, ZL = 4, 2, 2
GROUP = 64
INTERPRET = False

F32 = jnp.float32
BF16 = jnp.bfloat16


def iota(shape, dim):
    return lax.broadcasted_iota(jnp.int32, shape, dim)


def ones_where(condition):
    return jnp.where(condition, 1.0, 0.0).astype(BF16)


def dot(left, right):
    return jnp.dot(left, right, preferred_element_type=F32)


def dot_nt(left, right):
    return lax.dot_general(left, right, (((1,), (1,)), ((), ())), preferred_element_type=F32)


def slot_scalars(fine, coarse, parents, slot):
    parent = parents[slot]
    position = [fine[slot, axis] for axis in range(3)]
    octant = [fine[slot, axis] - 2 * coarse[parent, axis] for axis in range(3)]
    return parent, position, octant


def occupied_of(counts, slot):
    return jnp.where(slot < counts[0], 1.0, 0.0).astype(F32)


def meta_rows(position):
    voxel = iota((META, VOX), 1)
    row = iota((META, VOX), 0)
    x = 8 * position[0] + (voxel >> 6)
    y = 8 * position[1] + ((voxel >> 3) & 7)
    z = 8 * position[2] + (voxel & 7)
    value = jnp.where(row == 0, x, jnp.where(row == 1, y, jnp.where(row == 2, z, 0)))
    return value.astype(F32).astype(BF16)


def face_columns(block, slot):
    lane = iota((1, 4 * FACE), 1)
    face = lane >> 7
    inner = lane & 63
    x_high = 448 + inner
    y_low = (inner >> 3) * 64 + (inner & 7)
    source = jnp.where(
        face == 0, x_high, jnp.where(face == 1, inner, jnp.where(face == 2, y_low + 56, y_low))
    )
    source = jnp.where(((lane >> 6) & 1) == slot, source, -1)
    return dot(block, ones_where(iota((VOX, 4 * FACE), 0) == source))


def store_faces(faces_ref, total):
    row = iota((ROWS, FACE), 0)
    shifts = ((CH, -16.0), (CH, 16.0), (CH + 1, -16.0), (CH + 1, 16.0))
    for face, (where, shift) in enumerate(shifts):
        part = total[:, face * FACE : (face + 1) * FACE]
        faces_ref[face] = (part + jnp.where(row == where, shift, 0.0)).astype(BF16)


def hidden_kernel(fine, coarse_pos, parents, counts, skip, coarse, up, own, faces, total):
    slot = pl.program_id(0)
    parent, position, octant = slot_scalars(fine, coarse_pos, parents, slot)
    voxel = iota((1, VOX), 1)
    p, q, s = voxel >> 6, (voxel >> 3) & 7, voxel & 7
    code = (
        (4 * octant[0] + (p >> 1)) * 64 + (4 * octant[1] + (q >> 1)) * 8 + 4 * octant[2] + (s >> 1)
    )
    spread = dot(coarse[parent], ones_where(iota((VOX, VOX), 0) == code)).astype(BF16)
    kind = 4 * (p & 1) + 2 * (q & 1) + (s & 1)
    lifted = jnp.zeros((CH, VOX), F32)
    for k in range(8):
        lifted = lifted + dot(up[k], spread * ones_where(kind == k))
    hidden = (lifted + skip[0].astype(F32)) * occupied_of(counts, slot)
    own[slot, 0:CH, :] = hidden.astype(BF16)
    own[slot, CH:ROWS, :] = meta_rows(position)
    columns = face_columns(own[slot], slot)

    @pl.when(slot == 0)
    def _():
        total[...] = columns

    @pl.when(slot == 1)
    def _():
        store_faces(faces, total[...] + columns)


def edges_kernel(faces, from_low, from_high, to_high, to_low):
    row = iota((ROWS, FACE), 0)
    lane = iota((1, FACE), 1)
    inside = lane & 15
    for target, face, edge, shift in ((to_high, 2, 56, -16.0), (to_low, 3, 0, 16.0)):
        source = (inside >> 3) * 64 + edge + (inside & 7)
        first = ones_where(iota((FACE, FACE), 0) == jnp.where(lane < 16, source, -1))
        second = ones_where(
            iota((FACE, FACE), 0) == jnp.where((lane >= 16) & (lane < 32), source, -1)
        )
        value = dot(from_low[...], first) + dot(from_high[...], second)
        value = value + jnp.where(row == CH + 1, shift, 0.0)
        target[:, 0:FACE] = faces[face]
        target[:, FACE : 2 * FACE] = value.astype(BF16)


def gather_sources(source, own, low_x, high_x, low_y, high_y):
    source[:, 0:VOX] = own[0]
    source[:, VOX : 2 * VOX] = own[1]
    start = 2 * VOX
    source[:, start : start + FACE] = low_x[...]
    source[:, start + FACE : start + 2 * FACE] = high_x[...]
    start = start + 2 * FACE
    source[:, start : start + 2 * FACE] = low_y[...]
    source[:, start + 2 * FACE : start + 4 * FACE] = high_y[...]


def fill_taps(source, frame, taps, position):
    meta = source[CH:ROWS, :].astype(F32).astype(jnp.int32)
    x = meta[0:1, :] - 8 * position[0] + 1
    y = meta[1:2, :] - 8 * position[1] + 1
    z = meta[2:3, :] - 8 * position[2] + 1
    near = (x >= 0) & (x < 10) & (y >= 0) & (y < 10) & (z >= 0) & (z < 10)
    code = jnp.where(near, x * 128 + y * 10 + z, -1)
    values = source[0:CH, :]
    for pair in range(PLANES // 2):
        place = ones_where(iota((256, SOURCES), 0) + 256 * pair == code)
        frame[:, 256 * pair : 256 * pair + 256] = dot_nt(values, place).astype(BF16)
    lane = iota((1, 9 * 128), 1)
    shift = lane >> 7
    inner = lane & 127
    step_y = jnp.where(shift >= 6, 2, jnp.where(shift >= 3, 1, 0))
    step_z = shift - 3 * step_y
    origin = (inner >> 6) * 128 + (((inner >> 3) & 7) + step_y) * 10 + (inner & 7) + step_z
    shifts = ones_where(iota((256, 9 * 128), 0) == origin)
    for plane in range(9):
        moved = dot(frame[:, 128 * plane : 128 * plane + 256], shifts).astype(BF16)
        for step_x in range(3):
            rest = plane - step_x
            if rest < 0 or rest % 2 or rest > 6:
                continue
            at = 64 * rest
            for g in range(9):
                row = (step_x * 9 + g) * CH
                taps[row : row + CH, at : at + 128] = moved[:, 128 * g : 128 * g + 128]


def forward_kernel(
    fine, counts, core, own, low_x, high_x, low_y, high_y, cot, weight,
    grad, faces, keep, send, source, frame, taps, total, sums,
):
    slot = pl.program_id(0)
    position = [fine[slot, axis] for axis in range(3)]

    @pl.when(slot == 0)
    def _():
        gather_sources(source, own, low_x, high_x, low_y, high_y)
        sums[...] = jnp.zeros_like(sums)

    fill_taps(source, frame, taps, position)
    occupied = occupied_of(counts, slot)
    for half in range(2):
        at = slice(256 * half, 256 * half + 256)
        pre = dot(weight[...], taps[:, at])
        sigma = jax.nn.sigmoid(pre)
        value = cot[0, :, at].astype(F32) * (sigma * (1.0 + pre * (1.0 - sigma))) * occupied
        grad[slot, 0:CH, at] = value.astype(BF16)
    grad[slot, CH:ROWS, :] = meta_rows(position)
    values = grad[slot, 0:CH, :]
    for start in range(0, TAPS, 512):
        size = min(512, TAPS - start)
        sums[:, start : start + size] += dot_nt(values, taps[start : start + size, :])
    columns = face_columns(grad[slot], slot)

    @pl.when(slot == 0)
    def _():
        total[...] = columns

    @pl.when(slot == 1)
    def _():
        store_faces(faces, total[...] + columns)
        part = CH // (ZH * CORES)
        mine = core[0]
        for high in range(ZH):
            own_start = pl.multiple_of((2 * high + mine) * part, 8)
            other_start = pl.multiple_of((2 * high + 1 - mine) * part, 8)
            keep[high] = sums[pl.ds(own_start, part), :]
            send[high] = sums[pl.ds(other_start, part), :].astype(BF16)


def backward_kernel(
    fine, coarse_pos, parents, counts, own, low_x, high_x, low_y, high_y, weight, up,
    skip_grad, coarse_grad, source, frame, taps,
):
    slot = pl.program_id(0)
    parent, position, octant = slot_scalars(fine, coarse_pos, parents, slot)

    @pl.when(slot == 0)
    def _():
        gather_sources(source, own, low_x, high_x, low_y, high_y)
        coarse_grad[...] = jnp.zeros_like(coarse_grad)

    fill_taps(source, frame, taps, position)
    occupied = occupied_of(counts, slot)
    for half in range(2):
        at = slice(256 * half, 256 * half + 256)
        skip_grad[0, :, at] = (dot(weight[...], taps[:, at]) * occupied).astype(BF16)
    lane = iota((1, 8 * 128), 1)
    kind = lane >> 7
    inner = lane & 127
    voxel = (
        (2 * (inner >> 4) + (kind >> 2)) * 64
        + (2 * ((inner >> 2) & 3) + ((kind >> 1) & 1)) * 8
        + 2 * (inner & 3)
        + (kind & 1)
    )
    voxel = jnp.where(inner < 64, voxel, -1)
    grouped = dot(skip_grad[0], ones_where(iota((VOX, 8 * 128), 0) == voxel)).astype(BF16)
    folded = jnp.zeros((CH, 128), F32)
    for k in range(8):
        folded = folded + dot(up[k], grouped[:, 128 * k : 128 * k + 128])
    cell = iota((1, VOX), 1)
    p, q, s = cell >> 6, (cell >> 3) & 7, cell & 7
    inside = ((p >> 2) == octant[0]) & ((q >> 2) == octant[1]) & ((s >> 2) == octant[2])
    code = jnp.where(inside, (p & 3) * 16 + (q & 3) * 4 + (s & 3), -1)
    placed = dot(folded.astype(BF16), ones_where(iota((128, VOX), 0) == code))
    coarse_grad[parent] = (coarse_grad[parent].astype(F32) + placed).astype(BF16)


SMEM = pl.BlockSpec(memory_space=pltpu.SMEM)


def whole(*shape):
    return pl.BlockSpec(shape, lambda slot: (0,) * len(shape))


def one_slot(*shape):
    return pl.BlockSpec((1,) + shape, lambda slot: (slot,) + (0,) * len(shape))


def shaped(shape, kind=BF16):
    return jax.ShapeDtypeStruct(shape, kind)


def cost(flops, moved):
    return pl.CostEstimate(flops=flops, bytes_accessed=moved, transcendentals=0)


SOURCE_SPECS = [
    whole(2, ROWS, VOX),
    whole(ROWS, FACE),
    whole(ROWS, FACE),
    whole(ROWS, 2 * FACE),
    whole(ROWS, 2 * FACE),
]
TAP_SCRATCH = [
    pltpu.VMEM((ROWS, SOURCES), BF16),
    pltpu.VMEM((CH, 128 * PLANES), BF16),
    pltpu.VMEM((TAPS, VOX), BF16),
]


def make_hidden(fine, coarse_pos, parents, counts, skip, coarse, up):
    return pl.pallas_call(
        hidden_kernel,
        grid=(2,),
        in_specs=[SMEM] * 4
        + [one_slot(CH, VOX), whole(2, CH, VOX), whole(8, CH, CH)],
        out_specs=[whole(2, ROWS, VOX), whole(4, ROWS, FACE)],
        out_shape=[shaped((2, ROWS, VOX)), shaped((4, ROWS, FACE))],
        scratch_shapes=[pltpu.VMEM((ROWS, 4 * FACE), F32)],
        cost_estimate=cost(2_000_000_000, 3_000_000),
        interpret=INTERPRET,
        name="hidden",
    )(fine, coarse_pos, parents, counts, skip, coarse, up)


def exchange(own, faces):
    def both(axis, to_high, to_low):
        count = lax.axis_size(axis)
        forward = [(i, i + 1) for i in range(count - 1)]
        backward = [(target, source) for source, target in forward]
        return lax.ppermute(to_high, axis, forward), lax.ppermute(to_low, axis, backward)

    low_x, high_x = both("gx", faces[0], faces[1])
    to_high, to_low = pl.pallas_call(
        edges_kernel,
        out_shape=[shaped((ROWS, 2 * FACE))] * 2,
        interpret=INTERPRET,
        name="edges",
    )(faces, low_x, high_x)
    low_y, high_y = both("gy", to_high, to_low)
    return own, low_x, high_x, low_y, high_y


def run_forward(fine, counts, core, sources, cot, weight):
    part = CH // (ZH * CORES)
    return pl.pallas_call(
        forward_kernel,
        grid=(2,),
        in_specs=[SMEM] * 3 + SOURCE_SPECS + [one_slot(CH, VOX), whole(CH, TAPS)],
        out_specs=[
            whole(2, ROWS, VOX),
            whole(4, ROWS, FACE),
            whole(ZH, part, TAPS),
            whole(ZH, part, TAPS),
        ],
        out_shape=[
            shaped((2, ROWS, VOX)),
            shaped((4, ROWS, FACE)),
            shaped((ZH, part, TAPS), F32),
            shaped((ZH, part, TAPS)),
        ],
        scratch_shapes=TAP_SCRATCH
        + [pltpu.VMEM((ROWS, 4 * FACE), F32), pltpu.VMEM((CH, TAPS), F32)],
        cost_estimate=cost(8_000_000_000, 8_000_000),
        interpret=INTERPRET,
        name="forward",
    )(fine, counts, core, *sources, cot, weight)


def run_backward(fine, coarse_pos, parents, counts, sources, weight, up):
    return pl.pallas_call(
        backward_kernel,
        grid=(2,),
        in_specs=[SMEM] * 4 + SOURCE_SPECS + [whole(CH, TAPS), whole(8, CH, CH)],
        out_specs=[one_slot(CH, VOX), whole(2, CH, VOX)],
        out_shape=[shaped((2, CH, VOX)), shaped((2, CH, VOX))],
        scratch_shapes=TAP_SCRATCH,
        cost_estimate=cost(6_000_000_000, 4_000_000),
        interpret=INTERPRET,
        name="backward",
    )(fine, coarse_pos, parents, counts, *sources, weight, up)


def gy_pairs(move):
    pairs = []
    for high in range(ZH):
        for core in range(CORES):
            to_high, to_core = move(high, core)
            pairs.append((high * CORES + core, to_high * CORES + to_core))
    return pairs


def pick(array, index):
    return lax.dynamic_index_in_dim(array, index, 0, keepdims=False)


def reduce_grad(keep, send):
    high = lax.axis_index("gy") // CORES
    other = lax.ppermute(send, "gy", gy_pairs(lambda h, c: (h, 1 - c)))
    held = keep + other.astype(F32)
    arrived = []
    for step in (1, 3, 2):
        piece = pick(held, (high + step) % ZH).astype(BF16)
        arrived.append(
            lax.ppermute(piece, "gy", gy_pairs(lambda h, c, s=step: ((h + s) % ZH, c)))
        )
    held = pick(held, high)
    for piece in arrived:
        held = held + piece.astype(F32)
    part, taps = held.shape
    pieces = held.astype(BF16).reshape(GROUP, part * taps // GROUP)
    pieces = lax.all_to_all(pieces, "gx", 0, 0, tiled=True)
    mine = jnp.sum(pieces.astype(F32), axis=0, keepdims=True).astype(BF16)
    spread = jnp.broadcast_to(mine, pieces.shape)
    return lax.all_to_all(spread, "gx", 0, 0, tiled=True).reshape(part, taps).astype(F32)


def local(
    skip_feature_rows,
    coarse_features,
    cotangent,
    fine_coords,
    coarse_coords,
    parents,
    counts,
    conv_weight,
    up_weight,
):
    core = (lax.axis_index("gy") % CORES).astype(jnp.int32).reshape(1)
    weight_flat = conv_weight.reshape(CH, TAPS)
    weight_back = jnp.transpose(conv_weight[:, ::-1, :], (2, 1, 0)).reshape(CH, TAPS)
    up_back = jnp.swapaxes(up_weight, 1, 2)
    own, faces = make_hidden(
        fine_coords, coarse_coords, parents, counts, skip_feature_rows, coarse_features, up_weight
    )
    sources = exchange(own, faces)
    grad, grad_faces, keep, send = run_forward(
        fine_coords, counts, core, sources, cotangent, weight_flat
    )
    grad_conv = reduce_grad(keep, send)
    grad_sources = exchange(grad, grad_faces)
    grad_skip, grad_coarse = run_backward(
        fine_coords, coarse_coords, parents, counts, grad_sources, weight_back, up_back
    )
    return (grad_skip, grad_coarse, grad_conv.reshape(grad_conv.shape[0], OFFSETS, CH))


def solution(mesh):
    in_specs = (
        P(("gx", "gy"), None, None),
        P(("gx", "gy"), None, None),
        P(("gx", "gy"), None, None),
        P(("gx", "gy"), None),
        P(("gx", "gy"), None),
        P(("gx", "gy")),
        P(("gx", "gy")),
        P(),
        P(),
    )
    out_specs = (P(("gx", "gy"), None, None), P(("gx", "gy"), None, None), P("gy", None, None))
    return jax.shard_map(local, mesh=mesh, in_specs=in_specs, out_specs=out_specs, check_vma=False)
```

time: 589 us -> 174 us (0.30)
  the two profiles are of different devices: /device:TPU:320 before, /device:TPU:1 now
where the time goes in v2:
time: 174 us; the launch traced here: 173 us
  starting transfers between devices  77.7 us (45%)
  Pallas kernels  37 us (21%)
  local copies, waits for them, and re-layouts  24 us (14%)
  waiting for transfers between devices  23.3 us (13%)
  other arithmetic  9.17 us (5%)
    ppermute x4, starting transfers between devices, both(): lax.ppermute(to_high, axis, forward)  20.6 us
    all_to_all x1, starting transfers between devices, reduce_grad(): pieces = lax.all_to_all(pieces, 'gx', 0, 0, tiled=True)  19.3 us
    ppermute x3, starting transfers between devices, reduce_grad(): lax.ppermute(piece, 'gy', gy_pairs(lambda h, c, s=step: ((h + s) % ZH, c)))  16.5 us
    pallas_call x1, Pallas kernels, run_forward(): pl.pallas_call(forward_kernel, grid=(2,), in_specs=[SMEM] * 3 + SOURCE_SP...  16.2 us
    all_to_all x1, starting transfers between devices, reduce_grad(): lax.all_to_all(spread, 'gx', 0, 0, tiled=True).reshape(part, taps)  12.8 us
    ppermute x3, waiting for transfers between devices, reduce_grad(): lax.ppermute(piece, 'gy', gy_pairs(lambda h, c, s=step: ((h + s) % ZH, c)))  12.8 us
    unnamed x25, local copies, waits for them, and re-layouts  12.7 us
    pallas_call x1, Pallas kernels, run_backward(): pl.pallas_call(backward_kernel, grid=(2,), in_specs=[SMEM] * 4 + SOURCE_S...  12.6 us
  transfers between devices with their start and end apart: 14, of which 5 were waited for; matrix products, arithmetic and copies ran while one was open for 11% of the time, Pallas kernels for 8%

profile of v2, /device:TPU:1, one launch (start us, length us, event | category | flops | bytes accessed | tf_op | source)
XLA Modules:
  0.0 172.9 jit_solution(11493308905191462670)
XLA Ops:
  1.3 4.5 %hidden.1 = (bf16[2,208,512]{2,1,0:T(8,128)(2,1)}, bf16[4,208,128]{2,1,0:T(8,128)(2,1)}) custom-call(s32[2,3]{1,0:T(2,128)} %fine.5, s32[2,3]{1,0:T(2,128)} %coarse_pos.3, s32[2]{0:T(128)} %parents.3, s32[1]{0:T(128)S(6)} %copy.26.counts, bf16[2,192,512]{2,1,0:T(8,128)(2,1)} %skip.1, bf16[2,192,512]{2,1,0:T(8,128)(2,1)} %coarse.1, bf16[8,192,192]{2,1,0:T(8,128)(2,1)} %up.1), custom_call_target="tpu_custom_call" | custom-call | flops 2000000000 | bytes 3000000 | tf_op jit(solution)/shard_map/hidden/pallas_call | solution.py:285
  5.8 0.8 slice_bitcast_fusion.2
  6.6 3.9 %collective-permute-start = (bf16[208,128]{1,0:T(8,128)(2,1)S(1)}, bf16[208,128]{1,0:T(8,128)(2,1)S(1)}, u32[]{:S(2)}, u32[]{:S(2)}) collective-permute-start(bf16[208,128]{1,0:T(8,128)(2,1)S(1)} %get-tuple-element.39), channel_id=1, source_target_pairs={{0,8},{8,16},{16,24},{24,32},{32,40},{40,48},{48,56},{56,64},{64,7... | collective-permute-start | bytes 159752 | tf_op jit(solution)/shard_map/ppermute | solution.py:304
  10.5 1.3 collective-permute-start.1
  11.8 0.0 collective-permute-done.from_low.low_x
  11.9 3.6 %collective-permute-done.1.from_high.high_x = bf16[208,128]{1,0:T(8,128)(2,1)S(1)} collective-permute-done((bf16[208,128]{1,0:T(8,128)(2,1)S(1)}, bf16[208,128]{1,0:T(8,128)(2,1)S(1)}, u32[]{:S(2)}, u32[]{:S(2)}) %collective-permute-start.1) | collective-permute-done | bytes 53280 | tf_op jit(solution)/shard_map/ppermute | solution.py:304
  15.4 0.0 copy-done.1
  15.4 0.6 copy-done.3
  16.0 1.9 %edges.2 = (bf16[208,256]{1,0:T(8,128)(2,1)}, bf16[208,256]{1,0:T(8,128)(2,1)}) custom-call(bf16[4,208,128]{2,1,0:T(8,128)(2,1)} %get-tuple-element.16.faces, bf16[208,128]{1,0:T(8,128)(2,1)} %copy-done.1, bf16[208,128]{1,0:T(8,128)(2,1)} %copy-done.3), custom_call_target="tpu_custom_call" | custom-call | tf_op jit(solution)/shard_map/edges/pallas_call | solution.py:307
  18.0 7.8 %collective-permute-start.2 = (bf16[208,256]{1,0:T(8,128)(2,1)}, bf16[208,256]{1,0:T(8,128)(2,1)S(1)}, u32[]{:S(2)}, u32[]{:S(2)}) collective-permute-start(bf16[208,256]{1,0:T(8,128)(2,1)} %get-tuple-element.17), channel_id=1, source_target_pairs={{0,1},{1,2},{2,3},{3,4},{4,5},{5,6},{6,7},{8,9},{9,10},{10,11},{11... | collective-permute-start | bytes 319496 | tf_op jit(solution)/shard_map/ppermute | solution.py:304
  25.7 1.9 %collective-permute-start.3 = (bf16[208,256]{1,0:T(8,128)(2,1)}, bf16[208,256]{1,0:T(8,128)(2,1)S(1)}, u32[]{:S(2)}, u32[]{:S(2)}) collective-permute-start(bf16[208,256]{1,0:T(8,128)(2,1)} %get-tuple-element.18), channel_id=1, source_target_pairs={{1,0},{2,1},{3,2},{4,3},{5,4},{6,5},{7,6},{9,8},{10,9},{11,10},{12... | collective-permute-start | bytes 319496 | tf_op jit(solution)/shard_map/ppermute | solution.py:304
  27.7 3.8 %copy.20 = bf16[192,27,192]{0,2,1:T(8,128)(2,1)S(1)} copy(bf16[192,27,192]{2,0,1:T(8,128)(2,1)} %param.16) | data formatting | bytes 3981312 | tf_op args[7]
  31.5 3.3 %copy.21.weight = bf16[192,5184]{1,0:T(8,128)(2,1)} copy(bf16[192,5184]{0,1:T(8,128)(2,1)S(1)} %bitcast.29) | data formatting | bytes 3981312 | tf_op jit(solution)/shard_map/reshape | solution.py:403
  34.8 0.0 collective-permute-done.2.low_y
  34.8 0.0 collective-permute-done.3.high_y
  34.8 0.6 copy-done.5
  35.4 0.0 copy-done.7
  35.5 16.2 %forward.1 = (bf16[2,208,512]{2,1,0:T(8,128)(2,1)}, bf16[4,208,128]{2,1,0:T(8,128)(2,1)}, f32[4,24,5184]{2,1,0:T(8,128)}, bf16[4,24,5184]{2,1,0:T(8,128)(2,1)}) custom-call(s32[2,3]{1,0:T(2,128)} %fine.5, s32[1]{0:T(128)S(6)} %copy.26.counts, s32[1]{0:T(128)} %bitcast.core, bf16[2,208,512]{2,1,0:T(8,128)(2,1)} %get-tuple-element.15.own, ...), custom_call_target="tpu_custom_call" | custom-call | flops 8000000000 | bytes 8000000 | tf_op jit(solution)/shard_map/forward/pallas_call | solution.py:319
  51.7 1.9 %collective-permute-start.8 = (bf16[4,24,5184]{2,1,0:T(8,128)(2,1)}, bf16[4,24,5184]{2,1,0:T(8,128)(2,1)S(1)}, u32[]{:S(2)}, u32[]{:S(2)}) collective-permute-start(bf16[4,24,5184]{2,1,0:T(8,128)(2,1)} %get-tuple-element.26), channel_id=1, source_target_pairs={{0,1},{1,0},{2,3},{3,2},{4,5},{5,4},{6,7},{7,6},{8,9},{9,8},{10,11... | collective-permute-start | bytes 2985992 | tf_op jit(solution)/shard_map/ppermute | solution.py:372
  53.7 2.7 %collective-permute-done.8 = bf16[4,24,5184]{2,1,0:T(8,128)(2,1)S(1)} collective-permute-done((bf16[4,24,5184]{2,1,0:T(8,128)(2,1)}, bf16[4,24,5184]{2,1,0:T(8,128)(2,1)S(1)}, u32[]{:S(2)}, u32[]{:S(2)}) %collective-permute-start.8) | collective-permute-done | bytes 995360 | tf_op jit(solution)/shard_map/ppermute | solution.py:372
  56.4 1.7 convert_add_fusion
  58.1 0.1 fusion.3
  58.2 9.1 %collective-permute-start.10 = (bf16[24,5184]{1,0:T(8,128)(2,1)S(1)}, bf16[24,5184]{1,0:T(8,128)(2,1)S(1)}, u32[]{:S(2)}, u32[]{:S(2)}) collective-permute-start(bf16[24,5184]{1,0:T(8,128)(2,1)S(1)} %get-tuple-element.35), channel_id=1, source_target_pairs={{0,6},{1,7},{2,0},{3,1},{4,2},{5,3},{6,4},{7,5},{8,14},{9,15},{10,... | collective-permute-start | bytes 746504 | tf_op jit(solution)/shard_map/ppermute | solution.py:378
  67.4 3.1 %collective-permute-start.11 = (bf16[24,5184]{1,0:T(8,128)(2,1)S(1)}, bf16[24,5184]{1,0:T(8,128)(2,1)S(1)}, u32[]{:S(2)}, u32[]{:S(2)}) collective-permute-start(bf16[24,5184]{1,0:T(8,128)(2,1)S(1)} %get-tuple-element.34), channel_id=1, source_target_pairs={{0,4},{1,5},{2,6},{3,7},{4,0},{5,1},{6,2},{7,3},{8,12},{9,13},{10,... | collective-permute-start | bytes 746504 | tf_op jit(solution)/shard_map/ppermute | solution.py:378
  70.5 4.3 %collective-permute-start.9 = (bf16[24,5184]{1,0:T(8,128)(2,1)S(1)}, bf16[24,5184]{1,0:T(8,128)(2,1)}, u32[]{:S(2)}, u32[]{:S(2)}) collective-permute-start(bf16[24,5184]{1,0:T(8,128)(2,1)S(1)} %get-tuple-element.33), channel_id=1, source_target_pairs={{0,2},{1,3},{2,4},{3,5},{4,6},{5,7},{6,0},{7,1},{8,10},{9,11},{10,... | collective-permute-start | bytes 746504 | tf_op jit(solution)/shard_map/ppermute | solution.py:378
  74.8 0.0 copy-start
  74.8 12.5 %collective-permute-done.10 = bf16[24,5184]{1,0:T(8,128)(2,1)S(1)} collective-permute-done((bf16[24,5184]{1,0:T(8,128)(2,1)S(1)}, bf16[24,5184]{1,0:T(8,128)(2,1)S(1)}, u32[]{:S(2)}, u32[]{:S(2)}) %collective-permute-start.10) | collective-permute-done | bytes 248864 | tf_op jit(solution)/shard_map/ppermute | solution.py:378
  87.3 0.0 collective-permute-done.11
  87.3 0.3 collective-permute-done.9
  87.5 1.1 fusion.2
  88.6 0.4 all_to_all.13
  89.0 0.5 broadcast.10
  89.5 2.2 %reduce.4 = bf16[64,1944]{1,0:T(8,128)(2,1)S(1)} reduce(bf16[64,1,1944]{2,1,0:T(2,128)(2,1)S(1)} %all_to_all.13, bf16[]{:T(256)} %broadcast.10), dimensions={1}, to_apply=%all_to_all.13.reduce_sub_computation | reduce | bytes 497666 | tf_op jit(solution)/shard_map/all_to_all | solution.py:385
  91.8 1.0 reshape.43
  92.8 19.3 %all-to-all-start = ((bf16[64,2,972]{2,1,0:T(2,128)(2,1)}), bf16[64,2,972]{2,1,0:T(2,128)(2,1)S(1)}, u32[]{:S(2)}, u32[]{:S(2)}) async-start(bf16[64,2,972]{2,1,0:T(2,128)(2,1)} %reshape.43), calls=%async_computation | async-start | bytes 524288 | tf_op jit(solution)/shard_map/all_to_all | solution.py:385
  112.1 0.0 copy-done
  112.1 2.9 %collective-permute-start.4 = (bf16[208,128]{1,0:T(8,128)(2,1)S(1)}, bf16[208,128]{1,0:T(8,128)(2,1)S(1)}, u32[]{:S(2)}, u32[]{:S(2)}) collective-permute-start(bf16[208,128]{1,0:T(8,128)(2,1)S(1)} %get-tuple-element.37), channel_id=1, source_target_pairs={{0,8},{8,16},{16,24},{24,32},{32,40},{40,48},{48,56},{56,64},{64,7... | collective-permute-start | bytes 159752 | tf_op jit(solution)/shard_map/ppermute | solution.py:304
  115.1 1.3 collective-permute-start.5
  116.4 0.0 collective-permute-done.4.from_low.low_x
  116.4 4.2 %collective-permute-done.5.from_high.high_x = bf16[208,128]{1,0:T(8,128)(2,1)S(1)} collective-permute-done((bf16[208,128]{1,0:T(8,128)(2,1)S(1)}, bf16[208,128]{1,0:T(8,128)(2,1)S(1)}, u32[]{:S(2)}, u32[]{:S(2)}) %collective-permute-start.5) | collective-permute-done | bytes 53280 | tf_op jit(solution)/shard_map/ppermute | solution.py:304
  120.6 0.6 copy-done.4
  121.2 1.9 %edges.3 = (bf16[208,256]{1,0:T(8,128)(2,1)}, bf16[208,256]{1,0:T(8,128)(2,1)}) custom-call(bf16[4,208,128]{2,1,0:T(8,128)(2,1)} %get-tuple-element.20.faces, bf16[208,128]{1,0:T(8,128)(2,1)} %copy-done.2, bf16[208,128]{1,0:T(8,128)(2,1)} %copy-done.4), custom_call_target="tpu_custom_call" | custom-call | tf_op jit(solution)/shard_map/edges/pallas_call | solution.py:307
  123.2 6.0 %collective-permute-start.6 = (bf16[208,256]{1,0:T(8,128)(2,1)}, bf16[208,256]{1,0:T(8,128)(2,1)S(1)}, u32[]{:S(2)}, u32[]{:S(2)}) collective-permute-start(bf16[208,256]{1,0:T(8,128)(2,1)} %get-tuple-element.21), channel_id=1, source_target_pairs={{0,1},{1,2},{2,3},{3,4},{4,5},{5,6},{6,7},{8,9},{9,10},{10,11},{11... | collective-permute-start | bytes 319496 | tf_op jit(solution)/shard_map/ppermute | solution.py:304
  129.2 2.1 %collective-permute-start.7 = (bf16[208,256]{1,0:T(8,128)(2,1)}, bf16[208,256]{1,0:T(8,128)(2,1)S(1)}, u32[]{:S(2)}, u32[]{:S(2)}) collective-permute-start(bf16[208,256]{1,0:T(8,128)(2,1)} %get-tuple-element.22), channel_id=1, source_target_pairs={{1,0},{2,1},{3,2},{4,3},{5,4},{6,5},{7,6},{9,8},{10,9},{11,10},{12... | collective-permute-start | bytes 319496 | tf_op jit(solution)/shard_map/ppermute | solution.py:304
  131.3 1.9 %rev.3 = bf16[192,27,192]{2,0,1:T(8,128)(2,1)S(1)} reverse(bf16[192,27,192]{2,0,1:T(8,128)(2,1)} %param.16), dimensions={1} | reverse | bytes 3981312 | tf_op jit(solution)/shard_map/rev | solution.py:404
  133.2 2.4 %copy.22 = bf16[8,192,192]{1,2,0:T(8,128)(2,1)} copy(bf16[8,192,192]{2,1,0:T(8,128)(2,1)} %up.1) | data formatting | bytes 1179648 | tf_op args[8]
  135.6 3.3 %copy.23.weight = bf16[192,5184]{1,0:T(8,128)(2,1)} copy(bf16[192,5184]{0,1:T(8,128)(2,1)S(1)} %bitcast.28) | data formatting | bytes 3981312 | tf_op jit(solution)/shard_map/reshape | solution.py:404
  138.9 0.0 all-to-all-done
  138.9 0.4 reshape.44
  139.2 0.5 reduce_sum.12
  139.7 0.3 broadcast_in_dim.2
  140.0 2.2 %reduce.5 = bf16[64,1944]{1,0:T(8,128)(2,1)S(1)} reduce(bf16[64,1,1944]{2,1,0:T(2,128)(2,1)S(1)} %broadcast_in_dim.2, bf16[]{:T(256)} %broadcast.10), dimensions={1}, to_apply=%broadcast_in_dim.2.reduce_sub_computation | reduce | bytes 497666 | tf_op jit(solution)/shard_map/broadcast_in_dim | solution.py:387
  142.2 1.0 reshape.45
  143.2 12.8 %all-to-all-start.1 = ((bf16[64,2,972]{2,1,0:T(2,128)(2,1)}), bf16[64,2,972]{2,1,0:T(2,128)(2,1)S(1)}, u32[]{:S(2)}, u32[]{:S(2)}) async-start(bf16[64,2,972]{2,1,0:T(2,128)(2,1)} %reshape.45), calls=%async_computation.1 | async-start | bytes 524288 | tf_op jit(solution)/shard_map/all_to_all | solution.py:388
  156.0 0.0 collective-permute-done.6.low_y
  156.0 0.0 collective-permute-done.7.high_y
  156.0 0.6 copy-done.6
  156.7 0.0 copy-done.8
  156.7 12.6 %backward.1 = (bf16[2,192,512]{2,1,0:T(8,128)(2,1)}, bf16[2,192,512]{2,1,0:T(8,128)(2,1)}) custom-call(s32[2,3]{1,0:T(2,128)} %fine.5, s32[2,3]{1,0:T(2,128)} %coarse_pos.3, s32[2]{0:T(128)} %parents.3, s32[1]{0:T(128)S(6)} %copy.26.counts, bf16[2,208,512]{2,1,0:T(8,128)(2,1)} %get-tuple-element.19.own, bf16[208,128]{1,0:T(8,128)(2,1)} %copy-done.2, ...), custom_call_target="tpu_custom_call" | custom-call | flops 6000000000 | bytes 4000000 | tf_op jit(solution)/shard_map/backward/pallas_call | solution.py:344
  169.3 0.0 all-to-all-done.1
  169.3 0.4 reshape.46
  169.6 1.5 convert_reduce_fusion
  171.1 0.5 reshape.41
  171.7 1.2 copy.25
  (10 shorter events, 0.0 us)
Async XLA Ops:
  6.6 5.2 %collective-permute-start = (bf16[208,128]{1,0:T(8,128)(2,1)S(1)}, bf16[208,128]{1,0:T(8,128)(2,1)S(1)}, u32[]{:S(2)}, u32[]{:S(2)}) collective-permute-start(bf16[208,128]{1,0:T(8,128)(2,1)S(1)} %get-tuple-element.39), channel_id=1, source_target_pairs={{0,8},{8,16},{16,24},{24,32},{32,40},{40,48},{48,56},{56,64},{64,7... | collective-permute-start | bytes 159752 | tf_op jit(solution)/shard_map/ppermute | solution.py:304
  10.5 4.9 %collective-permute-start.1 = (bf16[208,128]{1,0:T(8,128)(2,1)S(1)}, bf16[208,128]{1,0:T(8,128)(2,1)S(1)}, u32[]{:S(2)}, u32[]{:S(2)}) collective-permute-start(bf16[208,128]{1,0:T(8,128)(2,1)S(1)} %get-tuple-element.38), channel_id=1, source_target_pairs={{8,0},{16,8},{24,16},{32,24},{40,32},{48,40},{56,48},{64,56},{72,6... | collective-permute-start | bytes 159752 | tf_op jit(solution)/shard_map/ppermute | solution.py:304
  11.8 3.6 %copy-start.1 = (bf16[208,128]{1,0:T(8,128)(2,1)}, bf16[208,128]{1,0:T(8,128)(2,1)S(1)}, u32[]{:S(2)}) copy-start(bf16[208,128]{1,0:T(8,128)(2,1)S(1)} %collective-permute-done.from_low.low_x) | copy-start | bytes 159748
  15.4 0.6 copy-start.3
  18.0 16.8 %collective-permute-start.2 = (bf16[208,256]{1,0:T(8,128)(2,1)}, bf16[208,256]{1,0:T(8,128)(2,1)S(1)}, u32[]{:S(2)}, u32[]{:S(2)}) collective-permute-start(bf16[208,256]{1,0:T(8,128)(2,1)} %get-tuple-element.17), channel_id=1, source_target_pairs={{0,1},{1,2},{2,3},{3,4},{4,5},{5,6},{6,7},{8,9},{9,10},{10,11},{11... | collective-permute-start | bytes 319496 | tf_op jit(solution)/shard_map/ppermute | solution.py:304
  25.7 9.1 %collective-permute-start.3 = (bf16[208,256]{1,0:T(8,128)(2,1)}, bf16[208,256]{1,0:T(8,128)(2,1)S(1)}, u32[]{:S(2)}, u32[]{:S(2)}) collective-permute-start(bf16[208,256]{1,0:T(8,128)(2,1)} %get-tuple-element.18), channel_id=1, source_target_pairs={{1,0},{2,1},{3,2},{4,3},{5,4},{6,5},{7,6},{9,8},{10,9},{11,10},{12... | collective-permute-start | bytes 319496 | tf_op jit(solution)/shard_map/ppermute | solution.py:304
  34.8 0.6 copy-start.5
  34.8 0.7 copy-start.7
  51.7 4.7 %collective-permute-start.8 = (bf16[4,24,5184]{2,1,0:T(8,128)(2,1)}, bf16[4,24,5184]{2,1,0:T(8,128)(2,1)S(1)}, u32[]{:S(2)}, u32[]{:S(2)}) collective-permute-start(bf16[4,24,5184]{2,1,0:T(8,128)(2,1)} %get-tuple-element.26), channel_id=1, source_target_pairs={{0,1},{1,0},{2,3},{3,2},{4,5},{5,4},{6,7},{7,6},{8,9},{9,8},{10,11... | collective-permute-start | bytes 2985992 | tf_op jit(solution)/shard_map/ppermute | solution.py:372
  58.2 29.1 %collective-permute-start.10 = (bf16[24,5184]{1,0:T(8,128)(2,1)S(1)}, bf16[24,5184]{1,0:T(8,128)(2,1)S(1)}, u32[]{:S(2)}, u32[]{:S(2)}) collective-permute-start(bf16[24,5184]{1,0:T(8,128)(2,1)S(1)} %get-tuple-element.35), channel_id=1, source_target_pairs={{0,6},{1,7},{2,0},{3,1},{4,2},{5,3},{6,4},{7,5},{8,14},{9,15},{10,... | collective-permute-start | bytes 746504 | tf_op jit(solution)/shard_map/ppermute | solution.py:378
  67.4 19.9 %collective-permute-start.11 = (bf16[24,5184]{1,0:T(8,128)(2,1)S(1)}, bf16[24,5184]{1,0:T(8,128)(2,1)S(1)}, u32[]{:S(2)}, u32[]{:S(2)}) collective-permute-start(bf16[24,5184]{1,0:T(8,128)(2,1)S(1)} %get-tuple-element.34), channel_id=1, source_target_pairs={{0,4},{1,5},{2,6},{3,7},{4,0},{5,1},{6,2},{7,3},{8,12},{9,13},{10,... | collective-permute-start | bytes 746504 | tf_op jit(solution)/shard_map/ppermute | solution.py:378
  70.5 17.1 %collective-permute-start.9 = (bf16[24,5184]{1,0:T(8,128)(2,1)S(1)}, bf16[24,5184]{1,0:T(8,128)(2,1)}, u32[]{:S(2)}, u32[]{:S(2)}) collective-permute-start(bf16[24,5184]{1,0:T(8,128)(2,1)S(1)} %get-tuple-element.33), channel_id=1, source_target_pairs={{0,2},{1,3},{2,4},{3,5},{4,6},{5,7},{6,0},{7,1},{8,10},{9,11},{10,... | collective-permute-start | bytes 746504 | tf_op jit(solution)/shard_map/ppermute | solution.py:378
  74.8 37.4 %copy-start = (bf16[4,208,128]{2,1,0:T(8,128)(2,1)S(1)}, bf16[4,208,128]{2,1,0:T(8,128)(2,1)}, u32[]{:S(2)}) copy-start(bf16[4,208,128]{2,1,0:T(8,128)(2,1)} %get-tuple-element.20.faces) | copy-start | bytes 638980
  92.8 46.1 %all-to-all-start = ((bf16[64,2,972]{2,1,0:T(2,128)(2,1)}), bf16[64,2,972]{2,1,0:T(2,128)(2,1)S(1)}, u32[]{:S(2)}, u32[]{:S(2)}) async-start(bf16[64,2,972]{2,1,0:T(2,128)(2,1)} %reshape.43), calls=%async_computation | async-start | bytes 524288 | tf_op jit(solution)/shard_map/all_to_all | solution.py:385
  112.1 4.3 %collective-permute-start.4 = (bf16[208,128]{1,0:T(8,128)(2,1)S(1)}, bf16[208,128]{1,0:T(8,128)(2,1)S(1)}, u32[]{:S(2)}, u32[]{:S(2)}) collective-permute-start(bf16[208,128]{1,0:T(8,128)(2,1)S(1)} %get-tuple-element.37), channel_id=1, source_target_pairs={{0,8},{8,16},{16,24},{24,32},{32,40},{40,48},{48,56},{56,64},{64,7... | collective-permute-start | bytes 159752 | tf_op jit(solution)/shard_map/ppermute | solution.py:304
  115.1 5.6 %collective-permute-start.5 = (bf16[208,128]{1,0:T(8,128)(2,1)S(1)}, bf16[208,128]{1,0:T(8,128)(2,1)S(1)}, u32[]{:S(2)}, u32[]{:S(2)}) collective-permute-start(bf16[208,128]{1,0:T(8,128)(2,1)S(1)} %get-tuple-element.36), channel_id=1, source_target_pairs={{8,0},{16,8},{24,16},{32,24},{40,32},{48,40},{56,48},{64,56},{72,6... | collective-permute-start | bytes 159752 | tf_op jit(solution)/shard_map/ppermute | solution.py:304
  116.4 4.2 %copy-start.2 = (bf16[208,128]{1,0:T(8,128)(2,1)}, bf16[208,128]{1,0:T(8,128)(2,1)S(1)}, u32[]{:S(2)}) copy-start(bf16[208,128]{1,0:T(8,128)(2,1)S(1)} %collective-permute-done.4.from_low.low_x) | copy-start | bytes 159748
  120.6 0.6 copy-start.4
  123.2 32.8 %collective-permute-start.6 = (bf16[208,256]{1,0:T(8,128)(2,1)}, bf16[208,256]{1,0:T(8,128)(2,1)S(1)}, u32[]{:S(2)}, u32[]{:S(2)}) collective-permute-start(bf16[208,256]{1,0:T(8,128)(2,1)} %get-tuple-element.21), channel_id=1, source_target_pairs={{0,1},{1,2},{2,3},{3,4},{4,5},{5,6},{6,7},{8,9},{9,10},{10,11},{11... | collective-permute-start | bytes 319496 | tf_op jit(solution)/shard_map/ppermute | solution.py:304
  129.2 26.9 %collective-permute-start.7 = (bf16[208,256]{1,0:T(8,128)(2,1)}, bf16[208,256]{1,0:T(8,128)(2,1)S(1)}, u32[]{:S(2)}, u32[]{:S(2)}) collective-permute-start(bf16[208,256]{1,0:T(8,128)(2,1)} %get-tuple-element.22), channel_id=1, source_target_pairs={{1,0},{2,1},{3,2},{4,3},{5,4},{6,5},{7,6},{9,8},{10,9},{11,10},{12... | collective-permute-start | bytes 319496 | tf_op jit(solution)/shard_map/ppermute | solution.py:304
  143.2 26.1 %all-to-all-start.1 = ((bf16[64,2,972]{2,1,0:T(2,128)(2,1)}), bf16[64,2,972]{2,1,0:T(2,128)(2,1)S(1)}, u32[]{:S(2)}, u32[]{:S(2)}) async-start(bf16[64,2,972]{2,1,0:T(2,128)(2,1)} %reshape.45), calls=%async_computation.1 | async-start | bytes 524288 | tf_op jit(solution)/shard_map/all_to_all | solution.py:388
  156.0 0.6 copy-start.6
  156.0 0.7 copy-start.8

commit v3 on v2

--- a/solution.py
+++ b/solution.py
@@ -1,5 +1,3 @@
-import functools
-
 import jax
 import jax.numpy as jnp
 from jax import lax
@@ -7,17 +5,21 @@
 from jax.experimental.pallas import tpu as pltpu
 from jax.sharding import PartitionSpec as P
 
+
 CH = 192
 META = 16
 ROWS = CH + META
 VOX = 512
 OFFSETS = 27
 TAPS = OFFSETS * CH
+TILES = 41
+PADDED = 128 * TILES
 FACE = 128
 SOURCES = 2 * VOX + 2 * FACE + 2 * 2 * FACE
 PLANES = 10
-ZH, CORES, ZL = 4, 2, 2
+ZH, CORES = 4, 2
 GROUP = 64
+SMALL = 24 * 1024 * 1024
 INTERPRET = False
 
 F32 = jnp.float32
@@ -248,6 +250,68 @@
     coarse_grad[parent] = (coarse_grad[parent].astype(F32) + placed).astype(BF16)
 
 
+def flatten_kernel(weight, flat):
+    for pair in range(OFFSETS // 2):
+        flat[:, 384 * pair : 384 * pair + 384] = jnp.concatenate(
+            [weight[2 * pair], weight[2 * pair + 1]], axis=1
+        )
+    flat[:, TAPS - CH : TAPS] = weight[OFFSETS - 1]
+
+
+def flatten_back_kernel(weight, up, flat, up_back):
+    last = OFFSETS - 1
+    for pair in range(OFFSETS // 2):
+        flat[:, 384 * pair : 384 * pair + 384] = jnp.concatenate(
+            [weight[last - 2 * pair].T, weight[last - 2 * pair - 1].T], axis=1
+        )
+    flat[:, TAPS - CH : TAPS] = weight[0].T
+    for k in range(8):
+        up_back[k] = up[k].T
+
+
+def pack_kernel(own, first, second, third, packed):
+    def tile(index):
+        at = slice(128 * index, 128 * index + 128)
+        value = own[:, at]
+        for piece in (first, second, third):
+            value = value + piece[:, at].astype(F32)
+        return value
+
+    part = own.shape[0]
+    for pair in range(TILES // 2):
+        both = jnp.concatenate([tile(2 * pair), tile(2 * pair + 1)], axis=0)
+        packed[2 * part * pair : 2 * part * pair + 2 * part, :] = both.astype(BF16)
+    start = part * (TILES - 1)
+    rest = packed.shape[0] - start - part
+    tail = jnp.concatenate([tile(TILES - 1), jnp.zeros((rest, 128), F32)], axis=0)
+    packed[start:, :] = tail.astype(BF16)
+
+
+def total_kernel(pieces, spread):
+    total = jnp.sum(pieces[...].astype(F32), axis=0, keepdims=True).astype(BF16)
+    spread[...] = jnp.broadcast_to(total, spread.shape)
+
+
+def unpack_kernel(packed, out):
+    part = out.shape[1]
+
+    def tiles(index):
+        both = packed[2 * part * index : 2 * part * index + 2 * part, :].astype(F32)
+        return both[0:part], both[part : 2 * part]
+
+    loaded = []
+    for index in range(TILES // 2):
+        loaded.extend(tiles(index))
+    start = part * (TILES - 1)
+    loaded.append(packed[start : start + 2 * part - 8 - 8, :].astype(F32)[0:part])
+    for pair in range(OFFSETS // 2):
+        wide = jnp.concatenate(loaded[3 * pair : 3 * pair + 3], axis=1)
+        out[2 * pair] = wide[:, 0:CH]
+        out[2 * pair + 1] = wide[:, CH : 2 * CH]
+    wide = jnp.concatenate(loaded[TILES - 2 : TILES], axis=1)
+    out[OFFSETS - 1] = wide[:, 0:CH]
+
+
 SMEM = pl.BlockSpec(memory_space=pltpu.SMEM)
 
 
@@ -296,22 +360,31 @@
     )(fine, coarse_pos, parents, counts, skip, coarse, up)
 
 
-def exchange(own, faces):
-    def both(axis, to_high, to_low):
-        count = lax.axis_size(axis)
-        forward = [(i, i + 1) for i in range(count - 1)]
-        backward = [(target, source) for source, target in forward]
-        return lax.ppermute(to_high, axis, forward), lax.ppermute(to_low, axis, backward)
-
-    low_x, high_x = both("gx", faces[0], faces[1])
-    to_high, to_low = pl.pallas_call(
-        edges_kernel,
-        out_shape=[shaped((ROWS, 2 * FACE))] * 2,
+def small_kernel(body, outs, vmem=None):
+    return pl.pallas_call(
+        body,
+        out_shape=outs,
+        compiler_params=pltpu.CompilerParams(vmem_limit_bytes=vmem),
+        cost_estimate=cost(1_000_000, 3_000_000),
         interpret=INTERPRET,
-        name="edges",
-    )(faces, low_x, high_x)
-    low_y, high_y = both("gy", to_high, to_low)
-    return own, low_x, high_x, low_y, high_y
+    )
+
+
+def both_ways(axis, to_high, to_low):
+    count = lax.axis_size(axis)
+    forward = [(i, i + 1) for i in range(count - 1)]
+    backward = [(target, source) for source, target in forward]
+    return lax.ppermute(to_high, axis, forward), lax.ppermute(to_low, axis, backward)
+
+
+def exchange(own, faces, beside_x=()):
+    low_x, high_x = both_ways("gx", faces[0], faces[1])
+    low_x, high_x, beside_x = lax.optimization_barrier((low_x, high_x, beside_x))
+    to_high, to_low = small_kernel(edges_kernel, [shaped((ROWS, 2 * FACE))] * 2, SMALL)(
+        faces, low_x, high_x
+    )
+    low_y, high_y = both_ways("gy", to_high, to_low)
+    return (own, low_x, high_x, low_y, high_y), beside_x
 
 
 def run_forward(fine, counts, core, sources, cot, weight):
@@ -323,17 +396,17 @@
         out_specs=[
             whole(2, ROWS, VOX),
             whole(4, ROWS, FACE),
-            whole(ZH, part, TAPS),
-            whole(ZH, part, TAPS),
+            whole(ZH, part, PADDED),
+            whole(ZH, part, PADDED),
         ],
         out_shape=[
             shaped((2, ROWS, VOX)),
             shaped((4, ROWS, FACE)),
-            shaped((ZH, part, TAPS), F32),
-            shaped((ZH, part, TAPS)),
+            shaped((ZH, part, PADDED), F32),
+            shaped((ZH, part, PADDED)),
         ],
         scratch_shapes=TAP_SCRATCH
-        + [pltpu.VMEM((ROWS, 4 * FACE), F32), pltpu.VMEM((CH, TAPS), F32)],
+        + [pltpu.VMEM((ROWS, 4 * FACE), F32), pltpu.VMEM((CH, PADDED), F32)],
         cost_estimate=cost(8_000_000_000, 8_000_000),
         interpret=INTERPRET,
         name="forward",
@@ -367,25 +440,24 @@
     return lax.dynamic_index_in_dim(array, index, 0, keepdims=False)
 
 
-def reduce_grad(keep, send):
+def reduce_first(keep, send):
     high = lax.axis_index("gy") // CORES
     other = lax.ppermute(send, "gy", gy_pairs(lambda h, c: (h, 1 - c)))
     held = keep + other.astype(F32)
     arrived = []
     for step in (1, 3, 2):
         piece = pick(held, (high + step) % ZH).astype(BF16)
-        arrived.append(
-            lax.ppermute(piece, "gy", gy_pairs(lambda h, c, s=step: ((h + s) % ZH, c)))
-        )
-    held = pick(held, high)
-    for piece in arrived:
-        held = held + piece.astype(F32)
-    part, taps = held.shape
-    pieces = held.astype(BF16).reshape(GROUP, part * taps // GROUP)
-    pieces = lax.all_to_all(pieces, "gx", 0, 0, tiled=True)
-    mine = jnp.sum(pieces.astype(F32), axis=0, keepdims=True).astype(BF16)
-    spread = jnp.broadcast_to(mine, pieces.shape)
-    return lax.all_to_all(spread, "gx", 0, 0, tiled=True).reshape(part, taps).astype(F32)
+        arrived.append(lax.ppermute(piece, "gy", gy_pairs(lambda h, c, s=step: ((h + s) % ZH, c))))
+    return (pick(held, high), *arrived)
+
+
+def reduce_second(terms):
+    packed = small_kernel(pack_kernel, shaped((GROUP * 16, 128)), SMALL)(*terms)
+    pieces = lax.all_to_all(packed.reshape(GROUP, 16, 128), "gx", 0, 0, tiled=True)
+    spread = small_kernel(total_kernel, shaped((GROUP, 16, 128)), SMALL)(pieces)
+    packed = lax.all_to_all(spread, "gx", 0, 0, tiled=True).reshape(GROUP * 16, 128)
+    part = terms[0].shape[0]
+    return small_kernel(unpack_kernel, shaped((OFFSETS, part, CH), F32), SMALL)(packed)
 
 
 def local(
@@ -400,22 +472,26 @@
     up_weight,
 ):
     core = (lax.axis_index("gy") % CORES).astype(jnp.int32).reshape(1)
-    weight_flat = conv_weight.reshape(CH, TAPS)
-    weight_back = jnp.transpose(conv_weight[:, ::-1, :], (2, 1, 0)).reshape(CH, TAPS)
-    up_back = jnp.swapaxes(up_weight, 1, 2)
+    by_offset = jnp.transpose(conv_weight, (1, 0, 2))
+    weight_flat = small_kernel(flatten_kernel, shaped((CH, TAPS)))(by_offset)
+    backs = small_kernel(
+        flatten_back_kernel, [shaped((CH, TAPS)), shaped((8, CH, CH))]
+    )(by_offset, up_weight)
     own, faces = make_hidden(
         fine_coords, coarse_coords, parents, counts, skip_feature_rows, coarse_features, up_weight
     )
-    sources = exchange(own, faces)
+    sources, (weight_back, up_back) = exchange(own, faces, tuple(backs))
     grad, grad_faces, keep, send = run_forward(
         fine_coords, counts, core, sources, cotangent, weight_flat
     )
-    grad_conv = reduce_grad(keep, send)
-    grad_sources = exchange(grad, grad_faces)
+    terms = reduce_first(keep, send)
+    grad_sources, _ = exchange(grad, grad_faces)
     grad_skip, grad_coarse = run_backward(
         fine_coords, coarse_coords, parents, counts, grad_sources, weight_back, up_back
     )
-    return (grad_skip, grad_coarse, grad_conv.reshape(grad_conv.shape[0], OFFSETS, CH))
+    terms, grad_skip = lax.optimization_barrier((terms, grad_skip))
+    grad_conv = reduce_second(terms)
+    return (grad_skip, grad_coarse, jnp.transpose(grad_conv, (1, 0, 2)))
 
 
 def solution(mesh):

time: 174 us -> 168 us (0.966)
  the two profiles are of different devices: /device:TPU:1 before, /device:TPU:8 now
where the time goes in v3:
time: 168 us; the launch traced here: 167 us
  Pallas kernels  43.3 us (26%)
  blocking collectives  43.1 us (26%)
  starting transfers between devices  41 us (24%)
  waiting for transfers between devices  33.9 us (20%)
  local copies, waits for them, and re-layouts  4.14 us (2%)
    all_to_all x1, blocking collectives, reduce_second(): lax.all_to_all(packed.reshape(GROUP, 16, 128), 'gx', 0, 0, tiled=True)  25.8 us
    all_to_all x1, blocking collectives, reduce_second(): lax.all_to_all(spread, 'gx', 0, 0, tiled=True).reshape(GROUP * 16, 128)  17.3 us
    ppermute x3, starting transfers between devices, reduce_first(): lax.ppermute(piece, 'gy', gy_pairs(lambda h, c, s=step: ((h + s) % ZH, c)))  16.6 us
    pallas_call x1, Pallas kernels, run_forward(): pl.pallas_call(forward_kernel, grid=(2,), in_specs=[SMEM] * 3 + SOURCE_SP...  16.2 us
    ppermute x3, waiting for transfers between devices, reduce_first(): lax.ppermute(piece, 'gy', gy_pairs(lambda h, c, s=step: ((h + s) % ZH, c)))  15 us
    pallas_call x1, Pallas kernels, run_backward(): pl.pallas_call(backward_kernel, grid=(2,), in_specs=[SMEM] * 4 + SOURCE_S...  12.7 us
    ppermute x4, starting transfers between devices, both_ways(): lax.ppermute(to_low, axis, backward)  11.9 us
    ppermute x4, waiting for transfers between devices, both_ways(): lax.ppermute(to_low, axis, backward)  11.3 us
  transfers between devices with their start and end apart: 12, of which 6 were waited for; matrix products, arithmetic and copies ran while one was open for 1% of the time, Pallas kernels for 13%

profile of v3, /device:TPU:8, one launch (start us, length us, event | category | flops | bytes accessed | tf_op | source)
XLA Modules:
  0.0 167.2 jit_solution(6718371207308584894)
XLA Ops:
  1.3 4.5 %hidden.1 = (bf16[2,208,512]{2,1,0:T(8,128)(2,1)}, bf16[4,208,128]{2,1,0:T(8,128)(2,1)}) custom-call(s32[2,3]{1,0:T(2,128)} %fine.5, s32[2,3]{1,0:T(2,128)} %coarse_pos.3, s32[2]{0:T(128)} %parents.3, s32[1]{0:T(128)S(6)} %copy.12.counts, bf16[2,192,512]{2,1,0:T(8,128)(2,1)} %skip.1, bf16[2,192,512]{2,1,0:T(8,128)(2,1)} %coarse.1, bf16[8,192,192]{2,1,0:T(8,128)(2,1)} %up.3), custom_call_target="tpu_custom_call" | custom-call | flops 2000000000 | bytes 3000000 | tf_op jit(solution)/shard_map/hidden/pallas_call | solution.py:349
  5.8 0.0 copy-start.1
  5.8 0.9 slice_bitcast_fusion.2
  6.7 4.6 %collective-permute-start.1 = (bf16[208,128]{1,0:T(8,128)(2,1)S(1)}, bf16[208,128]{1,0:T(8,128)(2,1)S(1)}, u32[]{:S(2)}, u32[]{:S(2)}) collective-permute-start(bf16[208,128]{1,0:T(8,128)(2,1)S(1)} %get-tuple-element.58), channel_id=1, source_target_pairs={{8,0},{16,8},{24,16},{32,24},{40,32},{48,40},{56,48},{64,56},{72,6... | collective-permute-start | bytes 159752 | tf_op jit(solution)/shard_map/ppermute | solution.py:377
  11.2 1.9 %collective-permute-start = (bf16[208,128]{1,0:T(8,128)(2,1)S(1)}, bf16[208,128]{1,0:T(8,128)(2,1)S(1)}, u32[]{:S(2)}, u32[]{:S(2)}) collective-permute-start(bf16[208,128]{1,0:T(8,128)(2,1)S(1)} %get-tuple-element.59), channel_id=1, source_target_pairs={{0,8},{8,16},{16,24},{24,32},{32,40},{40,48},{48,56},{56,64},{64,7... | collective-permute-start | bytes 159752 | tf_op jit(solution)/shard_map/ppermute | solution.py:377
  13.1 4.7 %shard_map.112 = (bf16[192,5184]{1,0:T(8,128)(2,1)}, bf16[8,192,192]{2,1,0:T(8,128)(2,1)}) custom-call(bf16[27,192,192]{2,1,0:T(8,128)(2,1)} %bitcast.23, bf16[8,192,192]{2,1,0:T(8,128)(2,1)} %up.3), custom_call_target="tpu_custom_call" | custom-call | flops 1000000 | bytes 3000000 | tf_op jit(solution)/shard_map/pallas_call | solution.py:477
  17.9 0.0 collective-permute-done.1.from_high.high_x
  17.9 0.0 copy-start.4
  17.9 1.5 collective-permute-done.from_low.low_x
  19.4 0.0 copy-start.5
  19.4 0.0 copy-done.1
  19.4 0.3 shard_map.113
  19.6 1.3 collective-permute-start.2
  20.9 1.3 collective-permute-start.3
  22.2 3.5 %shard_map.114.weight = bf16[192,5184]{1,0:T(8,128)(2,1)} custom-call(bf16[27,192,192]{2,1,0:T(8,128)(2,1)} %bitcast.24), custom_call_target="tpu_custom_call" | custom-call | flops 1000000 | bytes 3000000 | tf_op jit(solution)/shard_map/pallas_call | solution.py:476
  25.7 0.0 copy-done.4
  25.7 0.0 copy-done.5
  25.7 0.0 collective-permute-done.2.low_y
  25.7 0.0 copy-start.9
  25.8 2.8 %collective-permute-done.3.high_y = bf16[208,256]{1,0:T(8,128)(2,1)S(1)} collective-permute-done((bf16[208,256]{1,0:T(8,128)(2,1)S(1)}, bf16[208,256]{1,0:T(8,128)(2,1)S(1)}, u32[]{:S(2)}, u32[]{:S(2)}) %collective-permute-start.3) | collective-permute-done | bytes 106528 | tf_op jit(solution)/shard_map/ppermute | solution.py:377
  28.5 0.0 copy-start.10
  28.5 0.0 copy-done.9
  28.5 0.6 copy-done.10
  29.2 16.2 %forward.1 = (bf16[2,208,512]{2,1,0:T(8,128)(2,1)}, bf16[4,208,128]{2,1,0:T(8,128)(2,1)}, f32[4,24,5248]{2,1,0:T(8,128)}, bf16[4,24,5248]{2,1,0:T(8,128)(2,1)}) custom-call(s32[2,3]{1,0:T(2,128)} %fine.5, s32[1]{0:T(128)S(6)} %copy.12.counts, s32[1]{0:T(128)} %bitcast.core, bf16[2,208,512]{2,1,0:T(8,128)(2,1)} %get-tuple-element.28.own, ...), custom_call_target="tpu_custom_call" | custom-call | flops 8000000000 | bytes 8000000 | tf_op jit(solution)/shard_map/forward/pallas_call | solution.py:392
  45.4 6.1 %collective-permute-start.4 = (bf16[4,24,5248]{2,1,0:T(8,128)(2,1)}, bf16[4,24,5248]{2,1,0:T(8,128)(2,1)S(1)}, u32[]{:S(2)}, u32[]{:S(2)}) collective-permute-start(bf16[4,24,5248]{2,1,0:T(8,128)(2,1)} %get-tuple-element.37), channel_id=1, source_target_pairs={{0,1},{1,0},{2,3},{3,2},{4,5},{5,4},{6,7},{7,6},{8,9},{9,8},{10,11... | collective-permute-start | bytes 3022856 | tf_op jit(solution)/shard_map/ppermute | solution.py:445
  51.5 0.8 slice_bitcast_fusion
  52.4 4.6 %collective-permute-start.9 = (bf16[208,128]{1,0:T(8,128)(2,1)S(1)}, bf16[208,128]{1,0:T(8,128)(2,1)S(1)}, u32[]{:S(2)}, u32[]{:S(2)}) collective-permute-start(bf16[208,128]{1,0:T(8,128)(2,1)S(1)} %get-tuple-element.56), channel_id=1, source_target_pairs={{8,0},{16,8},{24,16},{32,24},{40,32},{48,40},{56,48},{64,56},{72,6... | collective-permute-start | bytes 159752 | tf_op jit(solution)/shard_map/ppermute | solution.py:377
  57.0 1.9 %collective-permute-start.8 = (bf16[208,128]{1,0:T(8,128)(2,1)S(1)}, bf16[208,128]{1,0:T(8,128)(2,1)S(1)}, u32[]{:S(2)}, u32[]{:S(2)}) collective-permute-start(bf16[208,128]{1,0:T(8,128)(2,1)S(1)} %get-tuple-element.57), channel_id=1, source_target_pairs={{0,8},{8,16},{16,24},{24,32},{32,40},{40,48},{48,56},{56,64},{64,7... | collective-permute-start | bytes 159752 | tf_op jit(solution)/shard_map/ppermute | solution.py:377
  58.9 0.0 collective-permute-done.9.from_high.high_x
  58.9 0.0 copy-start.2
  58.9 6.2 %collective-permute-done.8.from_low.low_x = bf16[208,128]{1,0:T(8,128)(2,1)S(1)} collective-permute-done((bf16[208,128]{1,0:T(8,128)(2,1)S(1)}, bf16[208,128]{1,0:T(8,128)(2,1)S(1)}, u32[]{:S(2)}, u32[]{:S(2)}) %collective-permute-start.8) | collective-permute-done | bytes 53280 | tf_op jit(solution)/shard_map/ppermute | solution.py:377
  65.1 0.0 copy-start
  65.1 0.9 copy-done
  66.0 0.0 copy-start.3
  66.0 0.3 shard_map.115
  66.3 1.3 collective-permute-start.10
  67.6 1.5 collective-permute-start.11
  69.2 0.0 collective-permute-done.10.low_y
  69.2 0.0 copy-start.7
  69.2 8.5 %collective-permute-done.11.high_y = bf16[208,256]{1,0:T(8,128)(2,1)S(1)} collective-permute-done((bf16[208,256]{1,0:T(8,128)(2,1)S(1)}, bf16[208,256]{1,0:T(8,128)(2,1)S(1)}, u32[]{:S(2)}, u32[]{:S(2)}) %collective-permute-start.11) | collective-permute-done | bytes 106528 | tf_op jit(solution)/shard_map/ppermute | solution.py:377
  77.7 0.0 copy-start.8
  77.7 0.0 copy-done.2
  77.7 0.0 copy-done.3
  77.7 0.0 copy-done.7
  77.7 0.6 copy-done.8
  78.3 0.0 copy-start.6
  78.3 12.7 %backward.1 = (bf16[2,192,512]{2,1,0:T(8,128)(2,1)}, bf16[2,192,512]{2,1,0:T(8,128)(2,1)}) custom-call(s32[2,3]{1,0:T(2,128)} %fine.5, s32[2,3]{1,0:T(2,128)} %coarse_pos.3, s32[2]{0:T(128)} %parents.3, s32[1]{0:T(128)S(6)} %copy.12.counts, bf16[2,208,512]{2,1,0:T(8,128)(2,1)} %get-tuple-element.38.own, bf16[208,128]{1,0:T(8,128)(2,1)} %copy-done.3, ...), custom_call_target="tpu_custom_call" | custom-call | flops 6000000000 | bytes 4000000 | tf_op jit(solution)/shard_map/backward/pallas_call | solution.py:417
  91.0 0.0 collective-permute-done.4
  91.0 0.0 copy-done.6
  91.0 0.2 convert_add_fusion
  91.2 0.1 fusion.2
  91.3 9.8 %collective-permute-start.7 = (bf16[24,5248]{1,0:T(8,128)(2,1)S(1)}, bf16[24,5248]{1,0:T(8,128)(2,1)S(1)}, u32[]{:S(2)}, u32[]{:S(2)}) collective-permute-start(bf16[24,5248]{1,0:T(8,128)(2,1)S(1)} %get-tuple-element.53), channel_id=1, source_target_pairs={{0,4},{1,5},{2,6},{3,7},{4,0},{5,1},{6,2},{7,3},{8,12},{9,13},{10,... | collective-permute-start | bytes 755720 | tf_op jit(solution)/shard_map/ppermute | solution.py:450
  101.2 1.9 %collective-permute-start.6 = (bf16[24,5248]{1,0:T(8,128)(2,1)S(1)}, bf16[24,5248]{1,0:T(8,128)(2,1)S(1)}, u32[]{:S(2)}, u32[]{:S(2)}) collective-permute-start(bf16[24,5248]{1,0:T(8,128)(2,1)S(1)} %get-tuple-element.54), channel_id=1, source_target_pairs={{0,6},{1,7},{2,0},{3,1},{4,2},{5,3},{6,4},{7,5},{8,14},{9,15},{10,... | collective-permute-start | bytes 755720 | tf_op jit(solution)/shard_map/ppermute | solution.py:450
  103.1 4.8 %collective-permute-start.5 = (bf16[24,5248]{1,0:T(8,128)(2,1)S(1)}, bf16[24,5248]{1,0:T(8,128)(2,1)S(1)}, u32[]{:S(2)}, u32[]{:S(2)}) collective-permute-start(bf16[24,5248]{1,0:T(8,128)(2,1)S(1)} %get-tuple-element.55), channel_id=1, source_target_pairs={{0,2},{1,3},{2,4},{3,5},{4,6},{5,7},{6,0},{7,1},{8,10},{9,11},{10,... | collective-permute-start | bytes 755720 | tf_op jit(solution)/shard_map/ppermute | solution.py:450
  108.0 5.0 %collective-permute-done.7.third = bf16[24,5248]{1,0:T(8,128)(2,1)S(1)} collective-permute-done((bf16[24,5248]{1,0:T(8,128)(2,1)S(1)}, bf16[24,5248]{1,0:T(8,128)(2,1)S(1)}, u32[]{:S(2)}, u32[]{:S(2)}) %collective-permute-start.7) | collective-permute-done | bytes 251936 | tf_op jit(solution)/shard_map/ppermute | solution.py:450
  113.0 10.0 %collective-permute-done.6.second = bf16[24,5248]{1,0:T(8,128)(2,1)S(1)} collective-permute-done((bf16[24,5248]{1,0:T(8,128)(2,1)S(1)}, bf16[24,5248]{1,0:T(8,128)(2,1)S(1)}, u32[]{:S(2)}, u32[]{:S(2)}) %collective-permute-start.6) | collective-permute-done | bytes 251936 | tf_op jit(solution)/shard_map/ppermute | solution.py:450
  122.9 0.0 collective-permute-done.5.first
  122.9 0.1 shard_map.116
  123.1 25.8 %all_to_all.10.pieces = bf16[64,16,128]{2,1,0:T(8,128)(2,1)S(1)} all-to-all(bf16[64,16,128]{2,1,0:T(8,128)(2,1)S(1)} %bitcast.22), channel_id=1, replica_groups=mesh['gx'=64,'gy'=8] {'gx'}, dimensions={0} | all-to-all | bytes 524288 | tf_op jit(solution)/shard_map/all_to_all | solution.py:456
  148.9 0.1 shard_map.117
  149.0 17.3 %all_to_all.11 = bf16[64,16,128]{2,1,0:T(8,128)(2,1)S(1)} all-to-all(bf16[64,16,128]{2,1,0:T(8,128)(2,1)S(1)} %shard_map.117), channel_id=1, replica_groups=mesh['gx'=64,'gy'=8] {'gx'}, dimensions={0} | all-to-all | bytes 524288 | tf_op jit(solution)/shard_map/all_to_all | solution.py:458
  166.2 1.0 shard_map.118
  (1 shorter events, 0.0 us)
Async XLA Ops:
  5.8 13.6 %copy-start.1 = (bf16[4,208,128]{2,1,0:T(8,128)(2,1)S(1)}, bf16[4,208,128]{2,1,0:T(8,128)(2,1)}, u32[]{:S(2)}) copy-start(bf16[4,208,128]{2,1,0:T(8,128)(2,1)} %get-tuple-element.29.faces) | copy-start | bytes 638980
  6.7 11.2 %collective-permute-start.1 = (bf16[208,128]{1,0:T(8,128)(2,1)S(1)}, bf16[208,128]{1,0:T(8,128)(2,1)S(1)}, u32[]{:S(2)}, u32[]{:S(2)}) collective-permute-start(bf16[208,128]{1,0:T(8,128)(2,1)S(1)} %get-tuple-element.58), channel_id=1, source_target_pairs={{8,0},{16,8},{24,16},{32,24},{40,32},{48,40},{56,48},{64,56},{72,6... | collective-permute-start | bytes 159752 | tf_op jit(solution)/shard_map/ppermute | solution.py:377
  11.2 8.1 %collective-permute-start = (bf16[208,128]{1,0:T(8,128)(2,1)S(1)}, bf16[208,128]{1,0:T(8,128)(2,1)S(1)}, u32[]{:S(2)}, u32[]{:S(2)}) collective-permute-start(bf16[208,128]{1,0:T(8,128)(2,1)S(1)} %get-tuple-element.59), channel_id=1, source_target_pairs={{0,8},{8,16},{16,24},{24,32},{32,40},{40,48},{48,56},{56,64},{64,7... | collective-permute-start | bytes 159752 | tf_op jit(solution)/shard_map/ppermute | solution.py:377
  17.9 7.8 %copy-start.4 = (bf16[208,128]{1,0:T(8,128)(2,1)}, bf16[208,128]{1,0:T(8,128)(2,1)S(1)}, u32[]{:S(2)}) copy-start(bf16[208,128]{1,0:T(8,128)(2,1)S(1)} %collective-permute-done.1.from_high.high_x) | copy-start | bytes 159748
  19.4 6.4 %copy-start.5 = (bf16[208,128]{1,0:T(8,128)(2,1)}, bf16[208,128]{1,0:T(8,128)(2,1)S(1)}, u32[]{:S(2)}) copy-start(bf16[208,128]{1,0:T(8,128)(2,1)S(1)} %collective-permute-done.from_low.low_x) | copy-start | bytes 159748
  19.6 6.1 %collective-permute-start.2 = (bf16[208,256]{1,0:T(8,128)(2,1)S(1)}, bf16[208,256]{1,0:T(8,128)(2,1)S(1)}, u32[]{:S(2)}, u32[]{:S(2)}) collective-permute-start(bf16[208,256]{1,0:T(8,128)(2,1)S(1)} %get-tuple-element.34), channel_id=1, source_target_pairs={{0,1},{1,2},{2,3},{3,4},{4,5},{5,6},{6,7},{8,9},{9,10},{10,11},{11... | collective-permute-start | bytes 319496 | tf_op jit(solution)/shard_map/ppermute | solution.py:377
  20.9 7.6 %collective-permute-start.3 = (bf16[208,256]{1,0:T(8,128)(2,1)S(1)}, bf16[208,256]{1,0:T(8,128)(2,1)S(1)}, u32[]{:S(2)}, u32[]{:S(2)}) collective-permute-start(bf16[208,256]{1,0:T(8,128)(2,1)S(1)} %get-tuple-element.35), channel_id=1, source_target_pairs={{1,0},{2,1},{3,2},{4,3},{5,4},{6,5},{7,6},{9,8},{10,9},{11,10},{12... | collective-permute-start | bytes 319496 | tf_op jit(solution)/shard_map/ppermute | solution.py:377
  25.7 2.8 %copy-start.9 = (bf16[208,256]{1,0:T(8,128)(2,1)}, bf16[208,256]{1,0:T(8,128)(2,1)S(1)}, u32[]{:S(2)}) copy-start(bf16[208,256]{1,0:T(8,128)(2,1)S(1)} %collective-permute-done.2.low_y) | copy-start | bytes 319492
  28.5 0.6 copy-start.10
  45.4 45.6 %collective-permute-start.4 = (bf16[4,24,5248]{2,1,0:T(8,128)(2,1)}, bf16[4,24,5248]{2,1,0:T(8,128)(2,1)S(1)}, u32[]{:S(2)}, u32[]{:S(2)}) collective-permute-start(bf16[4,24,5248]{2,1,0:T(8,128)(2,1)} %get-tuple-element.37), channel_id=1, source_target_pairs={{0,1},{1,0},{2,3},{3,2},{4,5},{5,4},{6,7},{7,6},{8,9},{9,8},{10,11... | collective-permute-start | bytes 3022856 | tf_op jit(solution)/shard_map/ppermute | solution.py:445
  52.4 6.5 %collective-permute-start.9 = (bf16[208,128]{1,0:T(8,128)(2,1)S(1)}, bf16[208,128]{1,0:T(8,128)(2,1)S(1)}, u32[]{:S(2)}, u32[]{:S(2)}) collective-permute-start(bf16[208,128]{1,0:T(8,128)(2,1)S(1)} %get-tuple-element.56), channel_id=1, source_target_pairs={{8,0},{16,8},{24,16},{32,24},{40,32},{48,40},{56,48},{64,56},{72,6... | collective-permute-start | bytes 159752 | tf_op jit(solution)/shard_map/ppermute | solution.py:377
  57.0 8.1 %collective-permute-start.8 = (bf16[208,128]{1,0:T(8,128)(2,1)S(1)}, bf16[208,128]{1,0:T(8,128)(2,1)S(1)}, u32[]{:S(2)}, u32[]{:S(2)}) collective-permute-start(bf16[208,128]{1,0:T(8,128)(2,1)S(1)} %get-tuple-element.57), channel_id=1, source_target_pairs={{0,8},{8,16},{16,24},{24,32},{32,40},{40,48},{48,56},{56,64},{64,7... | collective-permute-start | bytes 159752 | tf_op jit(solution)/shard_map/ppermute | solution.py:377
  58.9 18.8 %copy-start.2 = (bf16[208,128]{1,0:T(8,128)(2,1)}, bf16[208,128]{1,0:T(8,128)(2,1)S(1)}, u32[]{:S(2)}) copy-start(bf16[208,128]{1,0:T(8,128)(2,1)S(1)} %collective-permute-done.9.from_high.high_x) | copy-start | bytes 159748
  65.1 0.9 copy-start
  66.0 11.7 %copy-start.3 = (bf16[208,128]{1,0:T(8,128)(2,1)}, bf16[208,128]{1,0:T(8,128)(2,1)S(1)}, u32[]{:S(2)}) copy-start(bf16[208,128]{1,0:T(8,128)(2,1)S(1)} %collective-permute-done.8.from_low.low_x) | copy-start | bytes 159748
  66.3 2.9 %collective-permute-start.10 = (bf16[208,256]{1,0:T(8,128)(2,1)S(1)}, bf16[208,256]{1,0:T(8,128)(2,1)S(1)}, u32[]{:S(2)}, u32[]{:S(2)}) collective-permute-start(bf16[208,256]{1,0:T(8,128)(2,1)S(1)} %get-tuple-element.42), channel_id=1, source_target_pairs={{0,1},{1,2},{2,3},{3,4},{4,5},{5,6},{6,7},{8,9},{9,10},{10,11},{11... | collective-permute-start | bytes 319496 | tf_op jit(solution)/shard_map/ppermute | solution.py:377
  67.6 10.1 %collective-permute-start.11 = (bf16[208,256]{1,0:T(8,128)(2,1)S(1)}, bf16[208,256]{1,0:T(8,128)(2,1)S(1)}, u32[]{:S(2)}, u32[]{:S(2)}) collective-permute-start(bf16[208,256]{1,0:T(8,128)(2,1)S(1)} %get-tuple-element.43), channel_id=1, source_target_pairs={{1,0},{2,1},{3,2},{4,3},{5,4},{6,5},{7,6},{9,8},{10,9},{11,10},{12... | collective-permute-start | bytes 319496 | tf_op jit(solution)/shard_map/ppermute | solution.py:377
  69.2 8.5 %copy-start.7 = (bf16[208,256]{1,0:T(8,128)(2,1)}, bf16[208,256]{1,0:T(8,128)(2,1)S(1)}, u32[]{:S(2)}) copy-start(bf16[208,256]{1,0:T(8,128)(2,1)S(1)} %collective-permute-done.10.low_y) | copy-start | bytes 319492
  77.7 0.6 copy-start.8
  78.3 12.7 %copy-start.6 = (f32[4,24,5248]{2,1,0:T(8,128)S(1)}, f32[4,24,5248]{2,1,0:T(8,128)}, u32[]{:S(2)}) copy-start(f32[4,24,5248]{2,1,0:T(8,128)} %get-tuple-element.36) | copy-start | bytes 6045700
  91.3 21.6 %collective-permute-start.7 = (bf16[24,5248]{1,0:T(8,128)(2,1)S(1)}, bf16[24,5248]{1,0:T(8,128)(2,1)S(1)}, u32[]{:S(2)}, u32[]{:S(2)}) collective-permute-start(bf16[24,5248]{1,0:T(8,128)(2,1)S(1)} %get-tuple-element.53), channel_id=1, source_target_pairs={{0,4},{1,5},{2,6},{3,7},{4,0},{5,1},{6,2},{7,3},{8,12},{9,13},{10,... | collective-permute-start | bytes 755720 | tf_op jit(solution)/shard_map/ppermute | solution.py:450
  101.2 21.8 %collective-permute-start.6 = (bf16[24,5248]{1,0:T(8,128)(2,1)S(1)}, bf16[24,5248]{1,0:T(8,128)(2,1)S(1)}, u32[]{:S(2)}, u32[]{:S(2)}) collective-permute-start(bf16[24,5248]{1,0:T(8,128)(2,1)S(1)} %get-tuple-element.54), channel_id=1, source_target_pairs={{0,6},{1,7},{2,0},{3,1},{4,2},{5,3},{6,4},{7,5},{8,14},{9,15},{10,... | collective-permute-start | bytes 755720 | tf_op jit(solution)/shard_map/ppermute | solution.py:450
  103.1 19.9 %collective-permute-start.5 = (bf16[24,5248]{1,0:T(8,128)(2,1)S(1)}, bf16[24,5248]{1,0:T(8,128)(2,1)S(1)}, u32[]{:S(2)}, u32[]{:S(2)}) collective-permute-start(bf16[24,5248]{1,0:T(8,128)(2,1)S(1)} %get-tuple-element.55), channel_id=1, source_target_pairs={{0,2},{1,3},{2,4},{3,5},{4,6},{5,7},{6,0},{7,1},{8,10},{9,11},{10,... | collective-permute-start | bytes 755720 | tf_op jit(solution)/shard_map/ppermute | solution.py:450

commit v4 on v3

--- a/solution.py
+++ b/solution.py
@@ -17,8 +17,8 @@
 FACE = 128
 SOURCES = 2 * VOX + 2 * FACE + 2 * 2 * FACE
 PLANES = 10
-ZH, CORES = 4, 2
-GROUP = 64
+ZH, CORES, ZL = 4, 2, 2
+GROUP, SIDE, XS = 64, 8, 4
 SMALL = 24 * 1024 * 1024
 INTERPRET = False
 
@@ -156,16 +156,19 @@
     step_z = shift - 3 * step_y
     origin = (inner >> 6) * 128 + (((inner >> 3) & 7) + step_y) * 10 + (inner & 7) + step_z
     shifts = ones_where(iota((256, 9 * 128), 0) == origin)
-    for plane in range(9):
-        moved = dot(frame[:, 128 * plane : 128 * plane + 256], shifts).astype(BF16)
-        for step_x in range(3):
-            rest = plane - step_x
-            if rest < 0 or rest % 2 or rest > 6:
-                continue
-            at = 64 * rest
-            for g in range(9):
-                row = (step_x * 9 + g) * CH
-                taps[row : row + CH, at : at + 128] = moved[:, 128 * g : 128 * g + 128]
+    for pair in range(PLANES // 2):
+        moved = dot(frame[:, 256 * pair : 256 * pair + 256], shifts).astype(BF16)
+        for g in range(9):
+            part = moved[:, 128 * g : 128 * g + 128]
+            first, middle, last = (slice((9 * k + g) * CH, (9 * k + g + 1) * CH) for k in range(3))
+            if pair < 4:
+                taps[first, 128 * pair : 128 * pair + 128] = part
+            if pair > 0:
+                at = slice(128 * pair - 128, 128 * pair)
+                taps[last, at] = part
+                taps[middle, at] = jnp.concatenate(
+                    [taps[first, at][:, 64:128], part[:, 0:64]], axis=1
+                )
 
 
 def forward_kernel(
@@ -269,12 +272,14 @@
         up_back[k] = up[k].T
 
 
-def pack_kernel(own, first, second, third, packed):
+def pack_kernel(high, own, arrived, packed):
+    weights = [jnp.where(high[0] == h, 0.0, 1.0).astype(F32) for h in range(ZH)]
+
     def tile(index):
         at = slice(128 * index, 128 * index + 128)
         value = own[:, at]
-        for piece in (first, second, third):
-            value = value + piece[:, at].astype(F32)
+        for h in range(ZH):
+            value = value + weights[h] * arrived[h, :, at].astype(F32)
         return value
 
     part = own.shape[0]
@@ -285,6 +290,10 @@
     rest = packed.shape[0] - start - part
     tail = jnp.concatenate([tile(TILES - 1), jnp.zeros((rest, 128), F32)], axis=0)
     packed[start:, :] = tail.astype(BF16)
+
+
+def sum_kernel(pieces, out):
+    out[...] = jnp.sum(pieces[...].astype(F32), axis=0).astype(BF16)
 
 
 def total_kernel(pieces, spread):
@@ -313,6 +322,7 @@
 
 
 SMEM = pl.BlockSpec(memory_space=pltpu.SMEM)
+WHOLE = pl.BlockSpec(memory_space=pltpu.VMEM)
 
 
 def whole(*shape):
@@ -444,20 +454,44 @@
     high = lax.axis_index("gy") // CORES
     other = lax.ppermute(send, "gy", gy_pairs(lambda h, c: (h, 1 - c)))
     held = keep + other.astype(F32)
-    arrived = []
-    for step in (1, 3, 2):
-        piece = pick(held, (high + step) % ZH).astype(BF16)
-        arrived.append(lax.ppermute(piece, "gy", gy_pairs(lambda h, c, s=step: ((h + s) % ZH, c))))
-    return (pick(held, high), *arrived)
-
-
-def reduce_second(terms):
-    packed = small_kernel(pack_kernel, shaped((GROUP * 16, 128)), SMALL)(*terms)
-    pieces = lax.all_to_all(packed.reshape(GROUP, 16, 128), "gx", 0, 0, tiled=True)
-    spread = small_kernel(total_kernel, shaped((GROUP, 16, 128)), SMALL)(pieces)
-    packed = lax.all_to_all(spread, "gx", 0, 0, tiled=True).reshape(GROUP * 16, 128)
-    part = terms[0].shape[0]
-    return small_kernel(unpack_kernel, shaped((OFFSETS, part, CH), F32), SMALL)(packed)
+    groups = [[h * CORES + c for h in range(ZH)] for c in range(CORES)]
+    arrived = lax.all_to_all(held.astype(BF16), "gy", 0, 0, axis_index_groups=groups, tiled=True)
+    return pick(held, high), arrived, high.astype(jnp.int32).reshape(1)
+
+
+def gx_groups():
+    count = GROUP // SIDE
+    rows = [[(z * SIDE + y) * XS + x for y in range(SIDE)] for z in range(ZL) for x in range(XS)]
+    squares = [[(z * SIDE + y) * XS + x for z in range(ZL) for x in range(XS)] for y in range(SIDE)]
+    assert len(rows) == count
+    return rows, squares
+
+
+def among(pieces, groups):
+    return lax.all_to_all(pieces, "gx", 0, 0, axis_index_groups=groups, tiled=True)
+
+
+def reduce_second(own, arrived, high):
+    rows, squares = gx_groups()
+    packed = pl.pallas_call(
+        pack_kernel,
+        in_specs=[SMEM, WHOLE, WHOLE],
+        out_specs=WHOLE,
+        out_shape=shaped((GROUP * 16, 128)),
+        compiler_params=pltpu.CompilerParams(vmem_limit_bytes=SMALL),
+        interpret=INTERPRET,
+        name="pack",
+    )(high, own, arrived)
+    pieces = among(packed.reshape(SIDE, SIDE * 16, 128), rows)
+    pieces = small_kernel(sum_kernel, shaped((SIDE * 16, 128)), SMALL)(pieces)
+    pieces = among(pieces.reshape(SIDE, 16, 128), squares)
+    spread = small_kernel(total_kernel, shaped((SIDE, 16, 128)), SMALL)(pieces)
+    pieces = among(spread, squares).reshape(1, SIDE * 16, 128)
+    pieces = among(jnp.broadcast_to(pieces, (SIDE, SIDE * 16, 128)), rows)
+    part = own.shape[0]
+    return small_kernel(unpack_kernel, shaped((OFFSETS, part, CH), F32), SMALL)(
+        pieces.reshape(GROUP * 16, 128)
+    )
 
 
 def local(
@@ -490,7 +524,7 @@
         fine_coords, coarse_coords, parents, counts, grad_sources, weight_back, up_back
     )
     terms, grad_skip = lax.optimization_barrier((terms, grad_skip))
-    grad_conv = reduce_second(terms)
+    grad_conv = reduce_second(*terms)
     return (grad_skip, grad_coarse, jnp.transpose(grad_conv, (1, 0, 2)))
 
 

time: 168 us -> 157 us (0.935)
  the two profiles are of different devices: /device:TPU:8 before, /device:TPU:128 now
where the time goes in v4:
time: 157 us; the launch traced here: 156 us
  blocking collectives  54.7 us (35%)
  Pallas kernels  42.4 us (27%)
  starting transfers between devices  37.3 us (24%)
  waiting for transfers between devices  15 us (10%)
  other arithmetic  2.76 us (2%)
  local copies, waits for them, and re-layouts  2.28 us (1%)
    all_to_all x4, blocking collectives, among(): lax.all_to_all(pieces, 'gx', 0, 0, axis_index_groups=groups, tiled=True)  54.7 us
    pallas_call x1, Pallas kernels, run_forward(): pl.pallas_call(forward_kernel, grid=(2,), in_specs=[SMEM] * 3 + SOURCE_SP...  15.9 us
    ppermute x4, starting transfers between devices, both_ways(): lax.ppermute(to_high, axis, forward)  12.9 us
    pallas_call x1, Pallas kernels, run_backward(): pl.pallas_call(backward_kernel, grid=(2,), in_specs=[SMEM] * 4 + SOURCE_S...  12.1 us
    ppermute x4, starting transfers between devices, both_ways(): lax.ppermute(to_low, axis, backward)  11.8 us
    ppermute x4, waiting for transfers between devices, both_ways(): lax.ppermute(to_low, axis, backward)  9.77 us
    ppermute x1, starting transfers between devices, reduce_first(): other = lax.ppermute(send, 'gy', gy_pairs(lambda h, c: (h, 1 - c)))  7.32 us
    all_to_all x1, starting transfers between devices, reduce_first(): lax.all_to_all(held.astype(BF16), 'gy', 0, 0, axis_index_groups=groups, t...  5.17 us
  transfers between devices with their start and end apart: 10, of which 6 were waited for; matrix products, arithmetic and copies ran while one was open for 0% of the time, Pallas kernels for 13%

profile of v4, /device:TPU:128, one launch (start us, length us, event | category | flops | bytes accessed | tf_op | source)
XLA Modules:
  0.0 155.9 jit_solution(11616640504405659017)
XLA Ops:
  1.3 4.5 %hidden.1 = (bf16[2,208,512]{2,1,0:T(8,128)(2,1)}, bf16[4,208,128]{2,1,0:T(8,128)(2,1)}) custom-call(s32[2,3]{1,0:T(2,128)} %fine.5, s32[2,3]{1,0:T(2,128)} %coarse_pos.3, s32[2]{0:T(128)} %parents.3, s32[1]{0:T(128)S(6)} %copy.12.counts, bf16[2,192,512]{2,1,0:T(8,128)(2,1)} %skip.1, bf16[2,192,512]{2,1,0:T(8,128)(2,1)} %coarse.1, bf16[8,192,192]{2,1,0:T(8,128)(2,1)} %up.3), custom_call_target="tpu_custom_call" | custom-call | flops 2000000000 | bytes 3000000 | tf_op jit(solution)/shard_map/hidden/pallas_call | solution.py:359
  5.8 0.0 copy-start.1
  5.8 0.9 slice_bitcast_fusion.2
  6.6 1.3 collective-permute-start.1
  7.9 4.5 %collective-permute-start = (bf16[208,128]{1,0:T(8,128)(2,1)S(1)}, bf16[208,128]{1,0:T(8,128)(2,1)S(1)}, u32[]{:S(2)}, u32[]{:S(2)}) collective-permute-start(bf16[208,128]{1,0:T(8,128)(2,1)S(1)} %get-tuple-element.56), channel_id=1, source_target_pairs={{0,8},{8,16},{16,24},{24,32},{32,40},{40,48},{48,56},{56,64},{64,7... | collective-permute-start | bytes 159752 | tf_op jit(solution)/shard_map/ppermute | solution.py:387
  12.5 4.8 %shard_map.112 = (bf16[192,5184]{1,0:T(8,128)(2,1)}, bf16[8,192,192]{2,1,0:T(8,128)(2,1)}) custom-call(bf16[27,192,192]{2,1,0:T(8,128)(2,1)} %bitcast.21, bf16[8,192,192]{2,1,0:T(8,128)(2,1)} %up.3), custom_call_target="tpu_custom_call" | custom-call | flops 1000000 | bytes 3000000 | tf_op jit(solution)/shard_map/pallas_call | solution.py:511
  17.3 0.0 collective-permute-done.1.from_high.high_x
  17.3 0.0 copy-start.2
  17.3 0.0 collective-permute-done.from_low.low_x
  17.3 0.0 copy-start.4
  17.3 0.0 copy-done.1
  17.3 0.3 shard_map.113
  17.6 1.9 %collective-permute-start.2 = (bf16[208,256]{1,0:T(8,128)(2,1)S(1)}, bf16[208,256]{1,0:T(8,128)(2,1)S(1)}, u32[]{:S(2)}, u32[]{:S(2)}) collective-permute-start(bf16[208,256]{1,0:T(8,128)(2,1)S(1)} %get-tuple-element.33), channel_id=1, source_target_pairs={{0,1},{1,2},{2,3},{3,4},{4,5},{5,6},{6,7},{8,9},{9,10},{10,11},{11... | collective-permute-start | bytes 319496 | tf_op jit(solution)/shard_map/ppermute | solution.py:387
  19.5 4.5 %collective-permute-start.3 = (bf16[208,256]{1,0:T(8,128)(2,1)S(1)}, bf16[208,256]{1,0:T(8,128)(2,1)S(1)}, u32[]{:S(2)}, u32[]{:S(2)}) collective-permute-start(bf16[208,256]{1,0:T(8,128)(2,1)S(1)} %get-tuple-element.34), channel_id=1, source_target_pairs={{1,0},{2,1},{3,2},{4,3},{5,4},{6,5},{7,6},{9,8},{10,9},{11,10},{12... | collective-permute-start | bytes 319496 | tf_op jit(solution)/shard_map/ppermute | solution.py:387
  24.1 3.5 %shard_map.114.weight = bf16[192,5184]{1,0:T(8,128)(2,1)} custom-call(bf16[27,192,192]{2,1,0:T(8,128)(2,1)} %bitcast.22), custom_call_target="tpu_custom_call" | custom-call | flops 1000000 | bytes 3000000 | tf_op jit(solution)/shard_map/pallas_call | solution.py:510
  27.5 0.0 copy-done.2
  27.5 0.0 copy-done.4
  27.5 0.0 collective-permute-done.2.low_y
  27.5 0.0 copy-start.7
  27.5 0.2 collective-permute-done.3.high_y
  27.7 0.0 copy-start.9
  27.7 0.5 copy-done.7
  28.2 0.2 copy-done.9
  28.4 15.9 %forward.1 = (bf16[2,208,512]{2,1,0:T(8,128)(2,1)}, bf16[4,208,128]{2,1,0:T(8,128)(2,1)}, f32[4,24,5248]{2,1,0:T(8,128)}, bf16[4,24,5248]{2,1,0:T(8,128)(2,1)}) custom-call(s32[2,3]{1,0:T(2,128)} %fine.5, s32[1]{0:T(128)S(6)} %copy.12.counts, s32[1]{0:T(128)} %bitcast.core, bf16[2,208,512]{2,1,0:T(8,128)(2,1)} %get-tuple-element.27.own, ...), custom_call_target="tpu_custom_call" | custom-call | flops 8000000000 | bytes 8000000 | tf_op jit(solution)/shard_map/forward/pallas_call | solution.py:402
  44.3 7.3 %collective-permute-start.4 = (bf16[4,24,5248]{2,1,0:T(8,128)(2,1)}, bf16[4,24,5248]{2,1,0:T(8,128)(2,1)S(1)}, u32[]{:S(2)}, u32[]{:S(2)}) collective-permute-start(bf16[4,24,5248]{2,1,0:T(8,128)(2,1)} %get-tuple-element.36), channel_id=1, source_target_pairs={{0,1},{1,0},{2,3},{3,2},{4,5},{5,4},{6,7},{7,6},{8,9},{9,8},{10,11... | collective-permute-start | bytes 3022856 | tf_op jit(solution)/shard_map/ppermute | solution.py:455
  51.6 2.4 %collective-permute-done.4 = bf16[4,24,5248]{2,1,0:T(8,128)(2,1)S(1)} collective-permute-done((bf16[4,24,5248]{2,1,0:T(8,128)(2,1)}, bf16[4,24,5248]{2,1,0:T(8,128)(2,1)S(1)}, u32[]{:S(2)}, u32[]{:S(2)}) %collective-permute-start.4) | collective-permute-done | bytes 1007648 | tf_op jit(solution)/shard_map/ppermute | solution.py:455
  54.0 2.8 %fusion = (bf16[4,24,5248]{2,1,0:T(8,128)(2,1)}, f32[4,24,5248]{2,1,0:T(8,128)S(1)}) fusion(f32[4,24,5248]{2,1,0:T(8,128)} %get-tuple-element.35, bf16[4,24,5248]{2,1,0:T(8,128)(2,1)S(1)} %collective-permute-done.4), kind=kLoop, calls=%fused_computation.6 | loop fusion | flops 1511424 | bytes 6045696 | tf_op jit(solution)/shard_map/convert_element_type | solution.py:458
  56.8 0.0 copy-start
  56.8 5.2 %all-to-all-start = ((bf16[4,24,5248]{2,1,0:T(8,128)(2,1)}), bf16[4,24,5248]{2,1,0:T(8,128)(2,1)S(1)}, u32[]{:S(2)}, u32[]{:S(2)}) async-start(bf16[4,24,5248]{2,1,0:T(8,128)(2,1)} %get-tuple-element.51), calls=%async_computation | async-start | bytes 2015232 | tf_op jit(solution)/shard_map/all_to_all | solution.py:458
  61.9 0.0 copy-done
  62.0 1.3 collective-permute-start.6
  63.3 4.5 %collective-permute-start.5 = (bf16[208,128]{1,0:T(8,128)(2,1)S(1)}, bf16[208,128]{1,0:T(8,128)(2,1)S(1)}, u32[]{:S(2)}, u32[]{:S(2)}) collective-permute-start(bf16[208,128]{1,0:T(8,128)(2,1)S(1)} %get-tuple-element.54), channel_id=1, source_target_pairs={{0,8},{8,16},{16,24},{24,32},{32,40},{40,48},{48,56},{56,64},{64,7... | collective-permute-start | bytes 159752 | tf_op jit(solution)/shard_map/ppermute | solution.py:387
  67.8 0.2 collective-permute-done.6.from_high.high_x
  68.0 0.0 copy-start.3
  68.0 1.6 %collective-permute-done.5.from_low.low_x = bf16[208,128]{1,0:T(8,128)(2,1)S(1)} collective-permute-done((bf16[208,128]{1,0:T(8,128)(2,1)S(1)}, bf16[208,128]{1,0:T(8,128)(2,1)S(1)}, u32[]{:S(2)}, u32[]{:S(2)}) %collective-permute-start.5) | collective-permute-done | bytes 53280 | tf_op jit(solution)/shard_map/ppermute | solution.py:387
  69.6 0.0 copy-start.5
  69.6 0.3 shard_map.115
  69.9 1.9 %collective-permute-start.7 = (bf16[208,256]{1,0:T(8,128)(2,1)S(1)}, bf16[208,256]{1,0:T(8,128)(2,1)S(1)}, u32[]{:S(2)}, u32[]{:S(2)}) collective-permute-start(bf16[208,256]{1,0:T(8,128)(2,1)S(1)} %get-tuple-element.41), channel_id=1, source_target_pairs={{0,1},{1,2},{2,3},{3,4},{4,5},{5,6},{6,7},{8,9},{9,10},{10,11},{11... | collective-permute-start | bytes 319496 | tf_op jit(solution)/shard_map/ppermute | solution.py:387
  71.8 4.7 %collective-permute-start.8 = (bf16[208,256]{1,0:T(8,128)(2,1)S(1)}, bf16[208,256]{1,0:T(8,128)(2,1)S(1)}, u32[]{:S(2)}, u32[]{:S(2)}) collective-permute-start(bf16[208,256]{1,0:T(8,128)(2,1)S(1)} %get-tuple-element.42), channel_id=1, source_target_pairs={{1,0},{2,1},{3,2},{4,3},{5,4},{6,5},{7,6},{9,8},{10,9},{11,10},{12... | collective-permute-start | bytes 319496 | tf_op jit(solution)/shard_map/ppermute | solution.py:387
  76.5 1.2 collective-permute-done.7.low_y
  77.8 0.0 copy-start.6
  77.8 9.4 %collective-permute-done.8.high_y = bf16[208,256]{1,0:T(8,128)(2,1)S(1)} collective-permute-done((bf16[208,256]{1,0:T(8,128)(2,1)S(1)}, bf16[208,256]{1,0:T(8,128)(2,1)S(1)}, u32[]{:S(2)}, u32[]{:S(2)}) %collective-permute-start.8) | collective-permute-done | bytes 106528 | tf_op jit(solution)/shard_map/ppermute | solution.py:387
  87.2 0.0 copy-start.8
  87.2 0.0 copy-done.3
  87.2 0.0 copy-done.5
  87.2 0.0 copy-done.6
  87.2 0.6 copy-done.8
  87.8 12.1 %backward.1 = (bf16[2,192,512]{2,1,0:T(8,128)(2,1)}, bf16[2,192,512]{2,1,0:T(8,128)(2,1)}) custom-call(s32[2,3]{1,0:T(2,128)} %fine.5, s32[2,3]{1,0:T(2,128)} %coarse_pos.3, s32[2]{0:T(128)} %parents.3, s32[1]{0:T(128)S(6)} %copy.12.counts, bf16[2,208,512]{2,1,0:T(8,128)(2,1)} %get-tuple-element.37.own, bf16[208,128]{1,0:T(8,128)(2,1)} %copy-done.5, ...), custom_call_target="tpu_custom_call" | custom-call | flops 6000000000 | bytes 4000000 | tf_op jit(solution)/shard_map/backward/pallas_call | solution.py:427
  100.0 0.0 all-to-all-done.arrived
  100.0 0.2 pack.1
  100.2 19.5 %all_to_all.25.pieces = bf16[8,128,128]{2,1,0:T(8,128)(2,1)S(1)} all-to-all(bf16[8,128,128]{2,1,0:T(8,128)(2,1)S(1)} %bitcast.19), channel_id=1, replica_groups={{0,32,64,96,128,160,192,224},{8,40,72,104,136,168,200,232},{16,48,80,11..., dimensions={0} | all-to-all | bytes 524288 | tf_op jit(solution)/shard_map/all_to_all | solution.py:471
  119.8 13.6 %all_to_all.26.pieces = bf16[8,16,128]{2,1,0:T(8,128)(2,1)S(1)} all-to-all(bf16[8,16,128]{2,1,0:T(8,128)(2,1)S(1)} %bitcast.20), channel_id=1, replica_groups={{0,8,16,24,256,264,272,280},{32,40,48,56,288,296,304,312},{64,72,80,88,..., dimensions={0} | all-to-all | bytes 65536 | tf_op jit(solution)/shard_map/all_to_all | solution.py:471
  133.4 8.6 %all_to_all.27 = bf16[8,16,128]{2,1,0:T(8,128)(2,1)S(1)} all-to-all(bf16[8,16,128]{2,1,0:T(8,128)(2,1)S(1)} %shard_map.117), channel_id=1, replica_groups={{0,8,16,24,256,264,272,280},{32,40,48,56,288,296,304,312},{64,72,80,88,..., dimensions={0} | all-to-all | bytes 65536 | tf_op jit(solution)/shard_map/all_to_all | solution.py:471
  142.1 12.9 %all_to_all.28 = bf16[8,128,128]{2,1,0:T(8,128)(2,1)S(1)} all-to-all(bf16[8,128,128]{2,1,0:T(8,128)(2,1)S(1)} %broadcast_in_dim.8), channel_id=1, replica_groups={{0,32,64,96,128,160,192,224},{8,40,72,104,136,168,200,232},{16,48,80,11..., dimensions={0} | all-to-all | bytes 524288 | tf_op jit(solution)/shard_map/all_to_all | solution.py:471
  155.0 1.0 shard_map.118
  (5 shorter events, 0.1 us)
Async XLA Ops:
  5.8 11.5 %copy-start.1 = (bf16[4,208,128]{2,1,0:T(8,128)(2,1)S(1)}, bf16[4,208,128]{2,1,0:T(8,128)(2,1)}, u32[]{:S(2)}) copy-start(bf16[4,208,128]{2,1,0:T(8,128)(2,1)} %get-tuple-element.28.faces) | copy-start | bytes 638980
  6.6 10.6 %collective-permute-start.1 = (bf16[208,128]{1,0:T(8,128)(2,1)S(1)}, bf16[208,128]{1,0:T(8,128)(2,1)S(1)}, u32[]{:S(2)}, u32[]{:S(2)}) collective-permute-start(bf16[208,128]{1,0:T(8,128)(2,1)S(1)} %get-tuple-element.55), channel_id=1, source_target_pairs={{8,0},{16,8},{24,16},{32,24},{40,32},{48,40},{56,48},{64,56},{72,6... | collective-permute-start | bytes 159752 | tf_op jit(solution)/shard_map/ppermute | solution.py:387
  7.9 9.3 %collective-permute-start = (bf16[208,128]{1,0:T(8,128)(2,1)S(1)}, bf16[208,128]{1,0:T(8,128)(2,1)S(1)}, u32[]{:S(2)}, u32[]{:S(2)}) collective-permute-start(bf16[208,128]{1,0:T(8,128)(2,1)S(1)} %get-tuple-element.56), channel_id=1, source_target_pairs={{0,8},{8,16},{16,24},{24,32},{32,40},{40,48},{48,56},{56,64},{64,7... | collective-permute-start | bytes 159752 | tf_op jit(solution)/shard_map/ppermute | solution.py:387
  17.3 10.3 %copy-start.2 = (bf16[208,128]{1,0:T(8,128)(2,1)}, bf16[208,128]{1,0:T(8,128)(2,1)S(1)}, u32[]{:S(2)}) copy-start(bf16[208,128]{1,0:T(8,128)(2,1)S(1)} %collective-permute-done.1.from_high.high_x) | copy-start | bytes 159748
  17.3 10.2 %copy-start.4 = (bf16[208,128]{1,0:T(8,128)(2,1)}, bf16[208,128]{1,0:T(8,128)(2,1)S(1)}, u32[]{:S(2)}) copy-start(bf16[208,128]{1,0:T(8,128)(2,1)S(1)} %collective-permute-done.from_low.low_x) | copy-start | bytes 159748
  17.6 10.0 %collective-permute-start.2 = (bf16[208,256]{1,0:T(8,128)(2,1)S(1)}, bf16[208,256]{1,0:T(8,128)(2,1)S(1)}, u32[]{:S(2)}, u32[]{:S(2)}) collective-permute-start(bf16[208,256]{1,0:T(8,128)(2,1)S(1)} %get-tuple-element.33), channel_id=1, source_target_pairs={{0,1},{1,2},{2,3},{3,4},{4,5},{5,6},{6,7},{8,9},{9,10},{10,11},{11... | collective-permute-start | bytes 319496 | tf_op jit(solution)/shard_map/ppermute | solution.py:387
  19.5 8.2 %collective-permute-start.3 = (bf16[208,256]{1,0:T(8,128)(2,1)S(1)}, bf16[208,256]{1,0:T(8,128)(2,1)S(1)}, u32[]{:S(2)}, u32[]{:S(2)}) collective-permute-start(bf16[208,256]{1,0:T(8,128)(2,1)S(1)} %get-tuple-element.34), channel_id=1, source_target_pairs={{1,0},{2,1},{3,2},{4,3},{5,4},{6,5},{7,6},{9,8},{10,9},{11,10},{12... | collective-permute-start | bytes 319496 | tf_op jit(solution)/shard_map/ppermute | solution.py:387
  27.5 0.6 copy-start.7
  27.7 0.6 copy-start.9
  44.3 9.7 %collective-permute-start.4 = (bf16[4,24,5248]{2,1,0:T(8,128)(2,1)}, bf16[4,24,5248]{2,1,0:T(8,128)(2,1)S(1)}, u32[]{:S(2)}, u32[]{:S(2)}) collective-permute-start(bf16[4,24,5248]{2,1,0:T(8,128)(2,1)} %get-tuple-element.36), channel_id=1, source_target_pairs={{0,1},{1,0},{2,3},{3,2},{4,5},{5,4},{6,7},{7,6},{8,9},{9,8},{10,11... | collective-permute-start | bytes 3022856 | tf_op jit(solution)/shard_map/ppermute | solution.py:455
  56.8 5.2 %copy-start = (bf16[4,208,128]{2,1,0:T(8,128)(2,1)S(1)}, bf16[4,208,128]{2,1,0:T(8,128)(2,1)}, u32[]{:S(2)}) copy-start(bf16[4,208,128]{2,1,0:T(8,128)(2,1)} %get-tuple-element.38.faces) | copy-start | bytes 638980
  56.8 43.2 %all-to-all-start = ((bf16[4,24,5248]{2,1,0:T(8,128)(2,1)}), bf16[4,24,5248]{2,1,0:T(8,128)(2,1)S(1)}, u32[]{:S(2)}, u32[]{:S(2)}) async-start(bf16[4,24,5248]{2,1,0:T(8,128)(2,1)} %get-tuple-element.51), calls=%async_computation | async-start | bytes 2015232 | tf_op jit(solution)/shard_map/all_to_all | solution.py:458
  62.0 6.0 %collective-permute-start.6 = (bf16[208,128]{1,0:T(8,128)(2,1)S(1)}, bf16[208,128]{1,0:T(8,128)(2,1)S(1)}, u32[]{:S(2)}, u32[]{:S(2)}) collective-permute-start(bf16[208,128]{1,0:T(8,128)(2,1)S(1)} %get-tuple-element.53), channel_id=1, source_target_pairs={{8,0},{16,8},{24,16},{32,24},{40,32},{48,40},{56,48},{64,56},{72,6... | collective-permute-start | bytes 159752 | tf_op jit(solution)/shard_map/ppermute | solution.py:387
  63.3 6.3 %collective-permute-start.5 = (bf16[208,128]{1,0:T(8,128)(2,1)S(1)}, bf16[208,128]{1,0:T(8,128)(2,1)S(1)}, u32[]{:S(2)}, u32[]{:S(2)}) collective-permute-start(bf16[208,128]{1,0:T(8,128)(2,1)S(1)} %get-tuple-element.54), channel_id=1, source_target_pairs={{0,8},{8,16},{16,24},{24,32},{32,40},{40,48},{48,56},{56,64},{64,7... | collective-permute-start | bytes 159752 | tf_op jit(solution)/shard_map/ppermute | solution.py:387
  68.0 19.2 %copy-start.3 = (bf16[208,128]{1,0:T(8,128)(2,1)}, bf16[208,128]{1,0:T(8,128)(2,1)S(1)}, u32[]{:S(2)}) copy-start(bf16[208,128]{1,0:T(8,128)(2,1)S(1)} %collective-permute-done.6.from_high.high_x) | copy-start | bytes 159748
  69.6 17.6 %copy-start.5 = (bf16[208,128]{1,0:T(8,128)(2,1)}, bf16[208,128]{1,0:T(8,128)(2,1)S(1)}, u32[]{:S(2)}) copy-start(bf16[208,128]{1,0:T(8,128)(2,1)S(1)} %collective-permute-done.5.from_low.low_x) | copy-start | bytes 159748
  69.9 7.9 %collective-permute-start.7 = (bf16[208,256]{1,0:T(8,128)(2,1)S(1)}, bf16[208,256]{1,0:T(8,128)(2,1)S(1)}, u32[]{:S(2)}, u32[]{:S(2)}) collective-permute-start(bf16[208,256]{1,0:T(8,128)(2,1)S(1)} %get-tuple-element.41), channel_id=1, source_target_pairs={{0,1},{1,2},{2,3},{3,4},{4,5},{5,6},{6,7},{8,9},{9,10},{10,11},{11... | collective-permute-start | bytes 319496 | tf_op jit(solution)/shard_map/ppermute | solution.py:387
  71.8 15.4 %collective-permute-start.8 = (bf16[208,256]{1,0:T(8,128)(2,1)S(1)}, bf16[208,256]{1,0:T(8,128)(2,1)S(1)}, u32[]{:S(2)}, u32[]{:S(2)}) collective-permute-start(bf16[208,256]{1,0:T(8,128)(2,1)S(1)} %get-tuple-element.42), channel_id=1, source_target_pairs={{1,0},{2,1},{3,2},{4,3},{5,4},{6,5},{7,6},{9,8},{10,9},{11,10},{12... | collective-permute-start | bytes 319496 | tf_op jit(solution)/shard_map/ppermute | solution.py:387
  77.8 9.4 %copy-start.6 = (bf16[208,256]{1,0:T(8,128)(2,1)}, bf16[208,256]{1,0:T(8,128)(2,1)S(1)}, u32[]{:S(2)}) copy-start(bf16[208,256]{1,0:T(8,128)(2,1)S(1)} %collective-permute-done.7.low_y) | copy-start | bytes 319492
  87.2 0.6 copy-start.8

commit v5 on v3

--- a/solution.py
+++ b/solution.py
@@ -1,3 +1,5 @@
+import functools
+
 import jax
 import jax.numpy as jnp
 from jax import lax
@@ -156,16 +158,19 @@
     step_z = shift - 3 * step_y
     origin = (inner >> 6) * 128 + (((inner >> 3) & 7) + step_y) * 10 + (inner & 7) + step_z
     shifts = ones_where(iota((256, 9 * 128), 0) == origin)
-    for plane in range(9):
-        moved = dot(frame[:, 128 * plane : 128 * plane + 256], shifts).astype(BF16)
-        for step_x in range(3):
-            rest = plane - step_x
-            if rest < 0 or rest % 2 or rest > 6:
-                continue
-            at = 64 * rest
-            for g in range(9):
-                row = (step_x * 9 + g) * CH
-                taps[row : row + CH, at : at + 128] = moved[:, 128 * g : 128 * g + 128]
+    for pair in range(PLANES // 2):
+        moved = dot(frame[:, 256 * pair : 256 * pair + 256], shifts).astype(BF16)
+        for g in range(9):
+            part = moved[:, 128 * g : 128 * g + 128]
+            first, middle, last = (slice((9 * k + g) * CH, (9 * k + g + 1) * CH) for k in range(3))
+            if pair < 4:
+                taps[first, 128 * pair : 128 * pair + 128] = part
+            if pair > 0:
+                at = slice(128 * pair - 128, 128 * pair)
+                taps[last, at] = part
+                taps[middle, at] = jnp.concatenate(
+                    [taps[first, at][:, 64:128], part[:, 0:64]], axis=1
+                )
 
 
 def forward_kernel(
@@ -211,17 +216,13 @@
             send[high] = sums[pl.ds(other_start, part), :].astype(BF16)
 
 
-def backward_kernel(
-    fine, coarse_pos, parents, counts, own, low_x, high_x, low_y, high_y, weight, up,
-    skip_grad, coarse_grad, source, frame, taps,
-):
-    slot = pl.program_id(0)
+def backward_kernel(slot, fine, coarse_pos, parents, counts, own, *refs):
+    low_x, high_x, low_y, high_y, weight, up = refs[:6]
+    skip_grad, coarse_grad, source, frame, taps = refs[-5:]
     parent, position, octant = slot_scalars(fine, coarse_pos, parents, slot)
 
-    @pl.when(slot == 0)
-    def _():
-        gather_sources(source, own, low_x, high_x, low_y, high_y)
-        coarse_grad[...] = jnp.zeros_like(coarse_grad)
+    gather_sources(source, own, low_x, high_x, low_y, high_y)
+    coarse_grad[...] = jnp.zeros_like(coarse_grad) if slot == 0 else refs[7][...]
 
     fill_taps(source, frame, taps, position)
     occupied = occupied_of(counts, slot)
@@ -413,18 +414,23 @@
     )(fine, counts, core, *sources, cot, weight)
 
 
-def run_backward(fine, coarse_pos, parents, counts, sources, weight, up):
+def run_backward(slot, fine, coarse_pos, parents, counts, sources, weight, up, before=()):
+    aliases = {11: 0} if before else {}
+    earlier = [pl.BlockSpec(memory_space=pl.ANY), whole(2, CH, VOX)] if before else []
     return pl.pallas_call(
-        backward_kernel,
-        grid=(2,),
-        in_specs=[SMEM] * 4 + SOURCE_SPECS + [whole(CH, TAPS), whole(8, CH, CH)],
-        out_specs=[one_slot(CH, VOX), whole(2, CH, VOX)],
+        functools.partial(backward_kernel, slot),
+        grid=(1,),
+        in_specs=[SMEM] * 4 + SOURCE_SPECS + [whole(CH, TAPS), whole(8, CH, CH)] + earlier,
+        out_specs=[
+            pl.BlockSpec((1, CH, VOX), lambda step: (slot, 0, 0)),
+            whole(2, CH, VOX),
+        ],
         out_shape=[shaped((2, CH, VOX)), shaped((2, CH, VOX))],
         scratch_shapes=TAP_SCRATCH,
-        cost_estimate=cost(6_000_000_000, 4_000_000),
+        input_output_aliases=aliases,
+        cost_estimate=cost(3_000_000_000, 4_000_000),
         interpret=INTERPRET,
-        name="backward",
-    )(fine, coarse_pos, parents, counts, *sources, weight, up)
+    )(fine, coarse_pos, parents, counts, *sources, weight, up, *before)
 
 
 def gy_pairs(move):
@@ -455,7 +461,8 @@
     packed = small_kernel(pack_kernel, shaped((GROUP * 16, 128)), SMALL)(*terms)
     pieces = lax.all_to_all(packed.reshape(GROUP, 16, 128), "gx", 0, 0, tiled=True)
     spread = small_kernel(total_kernel, shaped((GROUP, 16, 128)), SMALL)(pieces)
-    packed = lax.all_to_all(spread, "gx", 0, 0, tiled=True).reshape(GROUP * 16, 128)
+    packed = lax.all_to_all(spread, "gx", 0, 0, tiled=True)
+    packed = packed.reshape(GROUP * 16, 128)
     part = terms[0].shape[0]
     return small_kernel(unpack_kernel, shaped((OFFSETS, part, CH), F32), SMALL)(packed)
 
@@ -486,10 +493,10 @@
     )
     terms = reduce_first(keep, send)
     grad_sources, _ = exchange(grad, grad_faces)
-    grad_skip, grad_coarse = run_backward(
-        fine_coords, coarse_coords, parents, counts, grad_sources, weight_back, up_back
-    )
-    terms, grad_skip = lax.optimization_barrier((terms, grad_skip))
+    scalars = (fine_coords, coarse_coords, parents, counts)
+    weights = (weight_back, up_back)
+    first = run_backward(0, *scalars, grad_sources, *weights)
+    grad_skip, grad_coarse = run_backward(1, *scalars, grad_sources, *weights, tuple(first))
     grad_conv = reduce_second(terms)
     return (grad_skip, grad_coarse, jnp.transpose(grad_conv, (1, 0, 2)))
 

time: 168 us -> 149 us (0.89)
  the two profiles are of different devices: /device:TPU:8 before, /device:TPU:1 now
where the time goes in v5:
time: 149 us; the launch traced here: 148 us
  starting transfers between devices  81.1 us (54%)
  Pallas kernels  46.5 us (31%)
  waiting for transfers between devices  15 us (10%)
  local copies, waits for them, and re-layouts  2.4 us (2%)
  other arithmetic  1.73 us (1%)
  between operations  1.63 us (1%)
    ppermute x4, starting transfers between devices, both_ways(): lax.ppermute(to_high, axis, forward)  21.6 us
    all_to_all x1, starting transfers between devices, reduce_second(): lax.all_to_all(packed.reshape(GROUP, 16, 128), 'gx', 0, 0, tiled=True)  20 us
    pallas_call x1, Pallas kernels, run_forward(): pl.pallas_call(forward_kernel, grid=(2,), in_specs=[SMEM] * 3 + SOURCE_SP...  15.9 us
    ppermute x3, starting transfers between devices, reduce_first(): lax.ppermute(piece, 'gy', gy_pairs(lambda h, c, s=step: ((h + s) % ZH, c)))  15.4 us
    all_to_all x1, starting transfers between devices, reduce_second(): packed = lax.all_to_all(spread, 'gx', 0, 0, tiled=True)  14.9 us
    pallas_call x2, Pallas kernels, run_backward(): pl.pallas_call(functools.partial(backward_kernel, slot), grid=(1,), in_sp...  14.8 us
    ppermute x3, waiting for transfers between devices, reduce_first(): lax.ppermute(piece, 'gy', gy_pairs(lambda h, c, s=step: ((h + s) % ZH, c)))  10.4 us
    ppermute x4, starting transfers between devices, both_ways(): lax.ppermute(to_low, axis, backward)  7.36 us
  transfers between devices with their start and end apart: 14, of which 7 were waited for; matrix products, arithmetic and copies ran while one was open for 0% of the time, Pallas kernels for 16%

profile of v5, /device:TPU:1, one launch (start us, length us, event | category | flops | bytes accessed | tf_op | source)
XLA Modules:
  0.0 148.4 jit_solution(9116099866784672079)
XLA Ops:
  1.3 4.5 %hidden.1 = (bf16[2,208,512]{2,1,0:T(8,128)(2,1)}, bf16[4,208,128]{2,1,0:T(8,128)(2,1)}) custom-call(s32[2,3]{1,0:T(2,128)} %fine.7, s32[2,3]{1,0:T(2,128)} %coarse_pos.5, s32[2]{0:T(128)} %parents.5, s32[1]{0:T(128)S(6)} %copy.14.counts, bf16[2,192,512]{2,1,0:T(8,128)(2,1)} %skip.1, bf16[2,192,512]{2,1,0:T(8,128)(2,1)} %coarse.1, bf16[8,192,192]{2,1,0:T(8,128)(2,1)} %up.3), custom_call_target="tpu_custom_call" | custom-call | flops 2000000000 | bytes 3000000 | tf_op jit(solution)/shard_map/hidden/pallas_call | solution.py:350
  5.8 0.0 copy-start.1
  5.8 0.9 slice_bitcast_fusion.2
  6.7 1.3 collective-permute-start.1
  8.0 4.6 %collective-permute-start = (bf16[208,128]{1,0:T(8,128)(2,1)S(1)}, bf16[208,128]{1,0:T(8,128)(2,1)S(1)}, u32[]{:S(2)}, u32[]{:S(2)}) collective-permute-start(bf16[208,128]{1,0:T(8,128)(2,1)S(1)} %get-tuple-element.53), channel_id=1, source_target_pairs={{0,8},{8,16},{16,24},{24,32},{32,40},{40,48},{48,56},{56,64},{64,7... | collective-permute-start | bytes 159752 | tf_op jit(solution)/shard_map/ppermute | solution.py:378
  12.5 4.8 %shard_map.112 = (bf16[192,5184]{1,0:T(8,128)(2,1)}, bf16[8,192,192]{2,1,0:T(8,128)(2,1)}) custom-call(bf16[27,192,192]{2,1,0:T(8,128)(2,1)} %bitcast.22, bf16[8,192,192]{2,1,0:T(8,128)(2,1)} %up.3), custom_call_target="tpu_custom_call" | custom-call | flops 1000000 | bytes 3000000 | tf_op jit(solution)/shard_map/pallas_call | solution.py:484
  17.3 0.0 collective-permute-done.1.from_high.high_x
  17.3 0.0 copy-start.2
  17.3 0.0 collective-permute-done.from_low.low_x
  17.3 0.0 copy-start.3
  17.3 0.0 copy-done.1
  17.3 0.3 shard_map.113
  17.6 7.2 %collective-permute-start.2 = (bf16[208,256]{1,0:T(8,128)(2,1)S(1)}, bf16[208,256]{1,0:T(8,128)(2,1)S(1)}, u32[]{:S(2)}, u32[]{:S(2)}) collective-permute-start(bf16[208,256]{1,0:T(8,128)(2,1)S(1)} %get-tuple-element.31), channel_id=1, source_target_pairs={{0,1},{1,2},{2,3},{3,4},{4,5},{5,6},{6,7},{8,9},{9,10},{10,11},{11... | collective-permute-start | bytes 319496 | tf_op jit(solution)/shard_map/ppermute | solution.py:378
  24.8 2.9 %collective-permute-start.3 = (bf16[208,256]{1,0:T(8,128)(2,1)S(1)}, bf16[208,256]{1,0:T(8,128)(2,1)S(1)}, u32[]{:S(2)}, u32[]{:S(2)}) collective-permute-start(bf16[208,256]{1,0:T(8,128)(2,1)S(1)} %get-tuple-element.32), channel_id=1, source_target_pairs={{1,0},{2,1},{3,2},{4,3},{5,4},{6,5},{7,6},{9,8},{10,9},{11,10},{12... | collective-permute-start | bytes 319496 | tf_op jit(solution)/shard_map/ppermute | solution.py:378
  27.6 3.4 %shard_map.114.weight = bf16[192,5184]{1,0:T(8,128)(2,1)} custom-call(bf16[27,192,192]{2,1,0:T(8,128)(2,1)} %bitcast.23), custom_call_target="tpu_custom_call" | custom-call | flops 1000000 | bytes 3000000 | tf_op jit(solution)/shard_map/pallas_call | solution.py:483
  31.1 0.0 copy-done.2
  31.1 0.0 copy-done.3
  31.1 0.0 collective-permute-done.2.low_y
  31.1 0.0 copy-start.6
  31.1 0.6 collective-permute-done.3.high_y
  31.7 0.0 copy-start.7
  31.7 0.0 copy-done.6
  31.7 0.6 copy-done.7
  32.3 15.9 %forward.1 = (bf16[2,208,512]{2,1,0:T(8,128)(2,1)}, bf16[4,208,128]{2,1,0:T(8,128)(2,1)}, f32[4,24,5248]{2,1,0:T(8,128)}, bf16[4,24,5248]{2,1,0:T(8,128)(2,1)}) custom-call(s32[2,3]{1,0:T(2,128)} %fine.7, s32[1]{0:T(128)S(6)} %copy.14.counts, s32[1]{0:T(128)} %bitcast.core, bf16[2,208,512]{2,1,0:T(8,128)(2,1)} %get-tuple-element.25.own, ...), custom_call_target="tpu_custom_call" | custom-call | flops 8000000000 | bytes 8000000 | tf_op jit(solution)/shard_map/forward/pallas_call | solution.py:393
  48.2 1.9 %collective-permute-start.8 = (bf16[4,24,5248]{2,1,0:T(8,128)(2,1)}, bf16[4,24,5248]{2,1,0:T(8,128)(2,1)S(1)}, u32[]{:S(2)}, u32[]{:S(2)}) collective-permute-start(bf16[4,24,5248]{2,1,0:T(8,128)(2,1)} %get-tuple-element.46), channel_id=1, source_target_pairs={{0,1},{1,0},{2,3},{3,2},{4,5},{5,4},{6,7},{7,6},{8,9},{9,8},{10,11... | collective-permute-start | bytes 3022856 | tf_op jit(solution)/shard_map/ppermute | solution.py:451
  50.2 2.7 %collective-permute-done.8 = bf16[4,24,5248]{2,1,0:T(8,128)(2,1)S(1)} collective-permute-done((bf16[4,24,5248]{2,1,0:T(8,128)(2,1)}, bf16[4,24,5248]{2,1,0:T(8,128)(2,1)S(1)}, u32[]{:S(2)}, u32[]{:S(2)}) %collective-permute-start.8) | collective-permute-done | bytes 1007648 | tf_op jit(solution)/shard_map/ppermute | solution.py:451
  52.9 1.7 %convert_add_fusion = f32[4,24,5248]{2,1,0:T(8,128)S(1)} fusion(f32[4,24,5248]{2,1,0:T(8,128)} %get-tuple-element.45, bf16[4,24,5248]{2,1,0:T(8,128)(2,1)S(1)} %collective-permute-done.8), kind=kLoop, calls=%fused_computation | loop fusion | flops 1007616 | bytes 5038080 | tf_op jit(solution)/shard_map/add | solution.py:452
  54.7 0.0 copy-start
  54.7 0.1 fusion.2
  54.8 8.8 %collective-permute-start.11 = (bf16[24,5248]{1,0:T(8,128)(2,1)S(1)}, bf16[24,5248]{1,0:T(8,128)(2,1)S(1)}, u32[]{:S(2)}, u32[]{:S(2)}) collective-permute-start(bf16[24,5248]{1,0:T(8,128)(2,1)S(1)} %get-tuple-element.47), channel_id=1, source_target_pairs={{0,4},{1,5},{2,6},{3,7},{4,0},{5,1},{6,2},{7,3},{8,12},{9,13},{10,... | collective-permute-start | bytes 755720 | tf_op jit(solution)/shard_map/ppermute | solution.py:456
  63.7 4.6 %collective-permute-start.10 = (bf16[24,5248]{1,0:T(8,128)(2,1)S(1)}, bf16[24,5248]{1,0:T(8,128)(2,1)S(1)}, u32[]{:S(2)}, u32[]{:S(2)}) collective-permute-start(bf16[24,5248]{1,0:T(8,128)(2,1)S(1)} %get-tuple-element.48), channel_id=1, source_target_pairs={{0,6},{1,7},{2,0},{3,1},{4,2},{5,3},{6,4},{7,5},{8,14},{9,15},{10,... | collective-permute-start | bytes 755720 | tf_op jit(solution)/shard_map/ppermute | solution.py:456
  68.3 1.9 %collective-permute-start.9 = (bf16[24,5248]{1,0:T(8,128)(2,1)S(1)}, bf16[24,5248]{1,0:T(8,128)(2,1)S(1)}, u32[]{:S(2)}, u32[]{:S(2)}) collective-permute-start(bf16[24,5248]{1,0:T(8,128)(2,1)S(1)} %get-tuple-element.49), channel_id=1, source_target_pairs={{0,2},{1,3},{2,4},{3,5},{4,6},{5,7},{6,0},{7,1},{8,10},{9,11},{10,... | collective-permute-start | bytes 755720 | tf_op jit(solution)/shard_map/ppermute | solution.py:456
  70.2 0.8 collective-permute-done.11.third
  71.1 2.4 %collective-permute-done.10.second = bf16[24,5248]{1,0:T(8,128)(2,1)S(1)} collective-permute-done((bf16[24,5248]{1,0:T(8,128)(2,1)S(1)}, bf16[24,5248]{1,0:T(8,128)(2,1)S(1)}, u32[]{:S(2)}, u32[]{:S(2)}) %collective-permute-start.10) | collective-permute-done | bytes 251936 | tf_op jit(solution)/shard_map/ppermute | solution.py:456
  73.5 7.2 %collective-permute-done.9.first = bf16[24,5248]{1,0:T(8,128)(2,1)S(1)} collective-permute-done((bf16[24,5248]{1,0:T(8,128)(2,1)S(1)}, bf16[24,5248]{1,0:T(8,128)(2,1)S(1)}, u32[]{:S(2)}, u32[]{:S(2)}) %collective-permute-start.9) | collective-permute-done | bytes 251936 | tf_op jit(solution)/shard_map/ppermute | solution.py:456
  80.7 0.8 shard_map.118
  81.5 20.0 %all-to-all-start = ((bf16[64,16,128]{2,1,0:T(8,128)(2,1)}), bf16[64,16,128]{2,1,0:T(8,128)(2,1)S(1)}, u32[]{:S(2)}, u32[]{:S(2)}) async-start(bf16[64,16,128]{2,1,0:T(8,128)(2,1)} %bitcast.10), calls=%async_computation | async-start | bytes 524288 | tf_op jit(solution)/shard_map/all_to_all | solution.py:462
  101.5 0.0 copy-done
  101.6 1.3 collective-permute-start.5
  102.9 4.0 %collective-permute-start.4 = (bf16[208,128]{1,0:T(8,128)(2,1)S(1)}, bf16[208,128]{1,0:T(8,128)(2,1)S(1)}, u32[]{:S(2)}, u32[]{:S(2)}) collective-permute-start(bf16[208,128]{1,0:T(8,128)(2,1)S(1)} %get-tuple-element.51), channel_id=1, source_target_pairs={{0,8},{8,16},{16,24},{24,32},{32,40},{40,48},{48,56},{56,64},{64,7... | collective-permute-start | bytes 159752 | tf_op jit(solution)/shard_map/ppermute | solution.py:378
  106.9 0.1 collective-permute-done.5.from_high.refs_1_
  107.0 0.0 copy-start.4
  107.0 1.1 collective-permute-done.4.from_low.refs_0_
  108.2 0.0 copy-start.5
  108.2 0.3 shard_map.115
  108.4 5.8 %collective-permute-start.6 = (bf16[208,256]{1,0:T(8,128)(2,1)S(1)}, bf16[208,256]{1,0:T(8,128)(2,1)S(1)}, u32[]{:S(2)}, u32[]{:S(2)}) collective-permute-start(bf16[208,256]{1,0:T(8,128)(2,1)S(1)} %get-tuple-element.37), channel_id=1, source_target_pairs={{0,1},{1,2},{2,3},{3,4},{4,5},{5,6},{6,7},{8,9},{9,10},{10,11},{11... | collective-permute-start | bytes 319496 | tf_op jit(solution)/shard_map/ppermute | solution.py:378
  114.3 1.9 %collective-permute-start.7 = (bf16[208,256]{1,0:T(8,128)(2,1)S(1)}, bf16[208,256]{1,0:T(8,128)(2,1)S(1)}, u32[]{:S(2)}, u32[]{:S(2)}) collective-permute-start(bf16[208,256]{1,0:T(8,128)(2,1)S(1)} %get-tuple-element.38), channel_id=1, source_target_pairs={{1,0},{2,1},{3,2},{4,3},{5,4},{6,5},{7,6},{9,8},{10,9},{11,10},{12... | collective-permute-start | bytes 319496 | tf_op jit(solution)/shard_map/ppermute | solution.py:378
  116.2 0.0 all-to-all-done.pieces
  116.2 0.8 shard_map.119
  117.0 14.9 %all-to-all-start.1 = ((bf16[64,16,128]{2,1,0:T(8,128)(2,1)}), bf16[64,16,128]{2,1,0:T(8,128)(2,1)S(1)}, u32[]{:S(2)}, u32[]{:S(2)}) async-start(bf16[64,16,128]{2,1,0:T(8,128)(2,1)} %shard_map.119), calls=%async_computation.1 | async-start | bytes 524288 | tf_op jit(solution)/shard_map/all_to_all | solution.py:464
  132.0 0.0 collective-permute-done.6.refs_2_
  132.0 0.0 copy-start.8
  132.0 0.0 collective-permute-done.7.refs_3_
  132.0 0.0 copy-start.9
  132.0 0.0 copy-done.4
  132.0 0.0 copy-done.5
  132.0 0.6 copy-done.8
  132.6 0.1 copy-done.9
  132.6 7.4 %shard_map.116 = (bf16[2,192,512]{2,1,0:T(8,128)(2,1)}, bf16[2,192,512]{2,1,0:T(8,128)(2,1)}) custom-call(s32[2,3]{1,0:T(2,128)} %fine.7, s32[2,3]{1,0:T(2,128)} %coarse_pos.5, s32[2]{0:T(128)} %parents.5, s32[1]{0:T(128)S(6)} %copy.14.counts, bf16[2,208,512]{2,1,0:T(8,128)(2,1)} %get-tuple-element.33.own, bf16[208,128]{1,0:T(8,128)(2,1)} %copy-done.5, ...), custom_call_target="tpu_custom_call" | custom-call | flops 3000000000 | bytes 4000000 | tf_op jit(solution)/shard_map/pallas_call | solution.py:420
  140.0 7.4 %shard_map.117 = (bf16[2,192,512]{2,1,0:T(8,128)(2,1)}, bf16[2,192,512]{2,1,0:T(8,128)(2,1)}) custom-call(s32[2,3]{1,0:T(2,128)} %fine.7, s32[2,3]{1,0:T(2,128)} %coarse_pos.5, s32[2]{0:T(128)} %parents.5, s32[1]{0:T(128)S(6)} %copy.14.counts, bf16[2,208,512]{2,1,0:T(8,128)(2,1)} %get-tuple-element.33.own, ...), custom_call_target="tpu_custom_call", output_to_operand_aliasing={{0}: (11, {})} | custom-call | flops 3000000000 | bytes 4000000 | tf_op jit(solution)/shard_map/pallas_call | solution.py:420
  147.4 0.0 all-to-all-done.1
  147.4 1.0 shard_map.120
  (2 shorter events, 0.1 us)
Async XLA Ops:
  5.8 11.5 %copy-start.1 = (bf16[4,208,128]{2,1,0:T(8,128)(2,1)S(1)}, bf16[4,208,128]{2,1,0:T(8,128)(2,1)}, u32[]{:S(2)}) copy-start(bf16[4,208,128]{2,1,0:T(8,128)(2,1)} %get-tuple-element.26.faces) | copy-start | bytes 638980
  6.7 10.6 %collective-permute-start.1 = (bf16[208,128]{1,0:T(8,128)(2,1)S(1)}, bf16[208,128]{1,0:T(8,128)(2,1)S(1)}, u32[]{:S(2)}, u32[]{:S(2)}) collective-permute-start(bf16[208,128]{1,0:T(8,128)(2,1)S(1)} %get-tuple-element.52), channel_id=1, source_target_pairs={{8,0},{16,8},{24,16},{32,24},{40,32},{48,40},{56,48},{64,56},{72,6... | collective-permute-start | bytes 159752 | tf_op jit(solution)/shard_map/ppermute | solution.py:378
  8.0 9.3 %collective-permute-start = (bf16[208,128]{1,0:T(8,128)(2,1)S(1)}, bf16[208,128]{1,0:T(8,128)(2,1)S(1)}, u32[]{:S(2)}, u32[]{:S(2)}) collective-permute-start(bf16[208,128]{1,0:T(8,128)(2,1)S(1)} %get-tuple-element.53), channel_id=1, source_target_pairs={{0,8},{8,16},{16,24},{24,32},{32,40},{40,48},{48,56},{56,64},{64,7... | collective-permute-start | bytes 159752 | tf_op jit(solution)/shard_map/ppermute | solution.py:378
  17.3 13.8 %copy-start.2 = (bf16[208,128]{1,0:T(8,128)(2,1)}, bf16[208,128]{1,0:T(8,128)(2,1)S(1)}, u32[]{:S(2)}) copy-start(bf16[208,128]{1,0:T(8,128)(2,1)S(1)} %collective-permute-done.1.from_high.high_x) | copy-start | bytes 159748
  17.3 13.8 %copy-start.3 = (bf16[208,128]{1,0:T(8,128)(2,1)}, bf16[208,128]{1,0:T(8,128)(2,1)S(1)}, u32[]{:S(2)}) copy-start(bf16[208,128]{1,0:T(8,128)(2,1)S(1)} %collective-permute-done.from_low.low_x) | copy-start | bytes 159748
  17.6 13.5 %collective-permute-start.2 = (bf16[208,256]{1,0:T(8,128)(2,1)S(1)}, bf16[208,256]{1,0:T(8,128)(2,1)S(1)}, u32[]{:S(2)}, u32[]{:S(2)}) collective-permute-start(bf16[208,256]{1,0:T(8,128)(2,1)S(1)} %get-tuple-element.31), channel_id=1, source_target_pairs={{0,1},{1,2},{2,3},{3,4},{4,5},{5,6},{6,7},{8,9},{9,10},{10,11},{11... | collective-permute-start | bytes 319496 | tf_op jit(solution)/shard_map/ppermute | solution.py:378
  24.8 6.9 %collective-permute-start.3 = (bf16[208,256]{1,0:T(8,128)(2,1)S(1)}, bf16[208,256]{1,0:T(8,128)(2,1)S(1)}, u32[]{:S(2)}, u32[]{:S(2)}) collective-permute-start(bf16[208,256]{1,0:T(8,128)(2,1)S(1)} %get-tuple-element.32), channel_id=1, source_target_pairs={{1,0},{2,1},{3,2},{4,3},{5,4},{6,5},{7,6},{9,8},{10,9},{11,10},{12... | collective-permute-start | bytes 319496 | tf_op jit(solution)/shard_map/ppermute | solution.py:378
  31.1 0.6 copy-start.6
  31.7 0.6 copy-start.7
  48.2 4.7 %collective-permute-start.8 = (bf16[4,24,5248]{2,1,0:T(8,128)(2,1)}, bf16[4,24,5248]{2,1,0:T(8,128)(2,1)S(1)}, u32[]{:S(2)}, u32[]{:S(2)}) collective-permute-start(bf16[4,24,5248]{2,1,0:T(8,128)(2,1)} %get-tuple-element.46), channel_id=1, source_target_pairs={{0,1},{1,0},{2,3},{3,2},{4,5},{5,4},{6,7},{7,6},{8,9},{9,8},{10,11... | collective-permute-start | bytes 3022856 | tf_op jit(solution)/shard_map/ppermute | solution.py:451
  54.7 46.9 %copy-start = (bf16[4,208,128]{2,1,0:T(8,128)(2,1)S(1)}, bf16[4,208,128]{2,1,0:T(8,128)(2,1)}, u32[]{:S(2)}) copy-start(bf16[4,208,128]{2,1,0:T(8,128)(2,1)} %get-tuple-element.34.faces) | copy-start | bytes 638980
  54.8 16.3 %collective-permute-start.11 = (bf16[24,5248]{1,0:T(8,128)(2,1)S(1)}, bf16[24,5248]{1,0:T(8,128)(2,1)S(1)}, u32[]{:S(2)}, u32[]{:S(2)}) collective-permute-start(bf16[24,5248]{1,0:T(8,128)(2,1)S(1)} %get-tuple-element.47), channel_id=1, source_target_pairs={{0,4},{1,5},{2,6},{3,7},{4,0},{5,1},{6,2},{7,3},{8,12},{9,13},{10,... | collective-permute-start | bytes 755720 | tf_op jit(solution)/shard_map/ppermute | solution.py:456
  63.7 9.9 %collective-permute-start.10 = (bf16[24,5248]{1,0:T(8,128)(2,1)S(1)}, bf16[24,5248]{1,0:T(8,128)(2,1)S(1)}, u32[]{:S(2)}, u32[]{:S(2)}) collective-permute-start(bf16[24,5248]{1,0:T(8,128)(2,1)S(1)} %get-tuple-element.48), channel_id=1, source_target_pairs={{0,6},{1,7},{2,0},{3,1},{4,2},{5,3},{6,4},{7,5},{8,14},{9,15},{10,... | collective-permute-start | bytes 755720 | tf_op jit(solution)/shard_map/ppermute | solution.py:456
  68.3 12.4 %collective-permute-start.9 = (bf16[24,5248]{1,0:T(8,128)(2,1)S(1)}, bf16[24,5248]{1,0:T(8,128)(2,1)S(1)}, u32[]{:S(2)}, u32[]{:S(2)}) collective-permute-start(bf16[24,5248]{1,0:T(8,128)(2,1)S(1)} %get-tuple-element.49), channel_id=1, source_target_pairs={{0,2},{1,3},{2,4},{3,5},{4,6},{5,7},{6,0},{7,1},{8,10},{9,11},{10,... | collective-permute-start | bytes 755720 | tf_op jit(solution)/shard_map/ppermute | solution.py:456
  81.5 34.7 %all-to-all-start = ((bf16[64,16,128]{2,1,0:T(8,128)(2,1)}), bf16[64,16,128]{2,1,0:T(8,128)(2,1)S(1)}, u32[]{:S(2)}, u32[]{:S(2)}) async-start(bf16[64,16,128]{2,1,0:T(8,128)(2,1)} %bitcast.10), calls=%async_computation | async-start | bytes 524288 | tf_op jit(solution)/shard_map/all_to_all | solution.py:462
  101.6 5.4 %collective-permute-start.5 = (bf16[208,128]{1,0:T(8,128)(2,1)S(1)}, bf16[208,128]{1,0:T(8,128)(2,1)S(1)}, u32[]{:S(2)}, u32[]{:S(2)}) collective-permute-start(bf16[208,128]{1,0:T(8,128)(2,1)S(1)} %get-tuple-element.50), channel_id=1, source_target_pairs={{8,0},{16,8},{24,16},{32,24},{40,32},{48,40},{56,48},{64,56},{72,6... | collective-permute-start | bytes 159752 | tf_op jit(solution)/shard_map/ppermute | solution.py:378
  102.9 5.3 %collective-permute-start.4 = (bf16[208,128]{1,0:T(8,128)(2,1)S(1)}, bf16[208,128]{1,0:T(8,128)(2,1)S(1)}, u32[]{:S(2)}, u32[]{:S(2)}) collective-permute-start(bf16[208,128]{1,0:T(8,128)(2,1)S(1)} %get-tuple-element.51), channel_id=1, source_target_pairs={{0,8},{8,16},{16,24},{24,32},{32,40},{40,48},{48,56},{56,64},{64,7... | collective-permute-start | bytes 159752 | tf_op jit(solution)/shard_map/ppermute | solution.py:378
  107.0 25.0 %copy-start.4 = (bf16[208,128]{1,0:T(8,128)(2,1)}, bf16[208,128]{1,0:T(8,128)(2,1)S(1)}, u32[]{:S(2)}) copy-start(bf16[208,128]{1,0:T(8,128)(2,1)S(1)} %collective-permute-done.5.from_high.refs_1_) | copy-start | bytes 159748
  108.2 23.8 %copy-start.5 = (bf16[208,128]{1,0:T(8,128)(2,1)}, bf16[208,128]{1,0:T(8,128)(2,1)S(1)}, u32[]{:S(2)}) copy-start(bf16[208,128]{1,0:T(8,128)(2,1)S(1)} %collective-permute-done.4.from_low.refs_0_) | copy-start | bytes 159748
  108.4 23.5 %collective-permute-start.6 = (bf16[208,256]{1,0:T(8,128)(2,1)S(1)}, bf16[208,256]{1,0:T(8,128)(2,1)S(1)}, u32[]{:S(2)}, u32[]{:S(2)}) collective-permute-start(bf16[208,256]{1,0:T(8,128)(2,1)S(1)} %get-tuple-element.37), channel_id=1, source_target_pairs={{0,1},{1,2},{2,3},{3,4},{4,5},{5,6},{6,7},{8,9},{9,10},{10,11},{11... | collective-permute-start | bytes 319496 | tf_op jit(solution)/shard_map/ppermute | solution.py:378
  114.3 17.7 %collective-permute-start.7 = (bf16[208,256]{1,0:T(8,128)(2,1)S(1)}, bf16[208,256]{1,0:T(8,128)(2,1)S(1)}, u32[]{:S(2)}, u32[]{:S(2)}) collective-permute-start(bf16[208,256]{1,0:T(8,128)(2,1)S(1)} %get-tuple-element.38), channel_id=1, source_target_pairs={{1,0},{2,1},{3,2},{4,3},{5,4},{6,5},{7,6},{9,8},{10,9},{11,10},{12... | collective-permute-start | bytes 319496 | tf_op jit(solution)/shard_map/ppermute | solution.py:378
  117.0 30.4 %all-to-all-start.1 = ((bf16[64,16,128]{2,1,0:T(8,128)(2,1)}), bf16[64,16,128]{2,1,0:T(8,128)(2,1)S(1)}, u32[]{:S(2)}, u32[]{:S(2)}) async-start(bf16[64,16,128]{2,1,0:T(8,128)(2,1)} %shard_map.119), calls=%async_computation.1 | async-start | bytes 524288 | tf_op jit(solution)/shard_map/all_to_all | solution.py:464
  132.0 0.6 copy-start.8
  132.0 0.7 copy-start.9

commit v6 on v5

--- a/solution.py
+++ b/solution.py
@@ -78,15 +78,16 @@
     return dot(block, ones_where(iota((VOX, 4 * FACE), 0) == source))
 
 
-def store_faces(faces_ref, total):
+def store_faces(faces, total):
     row = iota((ROWS, FACE), 0)
     shifts = ((CH, -16.0), (CH, 16.0), (CH + 1, -16.0), (CH + 1, 16.0))
     for face, (where, shift) in enumerate(shifts):
         part = total[:, face * FACE : (face + 1) * FACE]
-        faces_ref[face] = (part + jnp.where(row == where, shift, 0.0)).astype(BF16)
-
-
-def hidden_kernel(fine, coarse_pos, parents, counts, skip, coarse, up, own, faces, total):
+        faces[face][...] = (part + jnp.where(row == where, shift, 0.0)).astype(BF16)
+
+
+def hidden_kernel(fine, coarse_pos, parents, counts, skip, coarse, up, own, *refs):
+    faces, total = refs[:4], refs[4]
     slot = pl.program_id(0)
     parent, position, octant = slot_scalars(fine, coarse_pos, parents, slot)
     voxel = iota((1, VOX), 1)
@@ -113,11 +114,11 @@
         store_faces(faces, total[...] + columns)
 
 
-def edges_kernel(faces, from_low, from_high, to_high, to_low):
+def edges_kernel(y_high, y_low, from_low, from_high, to_high, to_low):
     row = iota((ROWS, FACE), 0)
     lane = iota((1, FACE), 1)
     inside = lane & 15
-    for target, face, edge, shift in ((to_high, 2, 56, -16.0), (to_low, 3, 0, 16.0)):
+    for target, face, edge, shift in ((to_high, y_high, 56, -16.0), (to_low, y_low, 0, 16.0)):
         source = (inside >> 3) * 64 + edge + (inside & 7)
         first = ones_where(iota((FACE, FACE), 0) == jnp.where(lane < 16, source, -1))
         second = ones_where(
@@ -125,7 +126,7 @@
         )
         value = dot(from_low[...], first) + dot(from_high[...], second)
         value = value + jnp.where(row == CH + 1, shift, 0.0)
-        target[:, 0:FACE] = faces[face]
+        target[:, 0:FACE] = face[...]
         target[:, FACE : 2 * FACE] = value.astype(BF16)
 
 
@@ -175,21 +176,30 @@
 
 def forward_kernel(
     fine, counts, core, own, low_x, high_x, low_y, high_y, cot, weight,
-    grad, faces, keep, send, source, frame, taps, total, sums,
+    grad, face0, face1, face2, face3, keep, send, source, frame, taps, total, sums,
+    held_weight, arrival,
 ):
+    faces = (face0, face1, face2, face3)
+    load = pltpu.make_async_copy(weight, held_weight, arrival)
     slot = pl.program_id(0)
     position = [fine[slot, axis] for axis in range(3)]
 
     @pl.when(slot == 0)
     def _():
+        load.start()
         gather_sources(source, own, low_x, high_x, low_y, high_y)
-        sums[...] = jnp.zeros_like(sums)
+        sums[:, PADDED - 128 :] = jnp.zeros((CH, 128), F32)
 
     fill_taps(source, frame, taps, position)
+
+    @pl.when(slot == 0)
+    def _():
+        load.wait()
+
     occupied = occupied_of(counts, slot)
     for half in range(2):
         at = slice(256 * half, 256 * half + 256)
-        pre = dot(weight[...], taps[:, at])
+        pre = dot(held_weight[...], taps[:, at])
         sigma = jax.nn.sigmoid(pre)
         value = cot[0, :, at].astype(F32) * (sigma * (1.0 + pre * (1.0 - sigma))) * occupied
         grad[slot, 0:CH, at] = value.astype(BF16)
@@ -197,7 +207,8 @@
     values = grad[slot, 0:CH, :]
     for start in range(0, TAPS, 512):
         size = min(512, TAPS - start)
-        sums[:, start : start + size] += dot_nt(values, taps[start : start + size, :])
+        earlier = jnp.where(slot == 0, 0.0, sums[:, start : start + size])
+        sums[:, start : start + size] = earlier + dot_nt(values, taps[start : start + size, :])
     columns = face_columns(grad[slot], slot)
 
     @pl.when(slot == 0)
@@ -218,7 +229,9 @@
 
 def backward_kernel(slot, fine, coarse_pos, parents, counts, own, *refs):
     low_x, high_x, low_y, high_y, weight, up = refs[:6]
-    skip_grad, coarse_grad, source, frame, taps = refs[-5:]
+    skip_grad, coarse_grad, source, frame, taps, held_weight, arrival = refs[-7:]
+    load = pltpu.make_async_copy(weight, held_weight, arrival)
+    load.start()
     parent, position, octant = slot_scalars(fine, coarse_pos, parents, slot)
 
     gather_sources(source, own, low_x, high_x, low_y, high_y)
@@ -226,9 +239,10 @@
 
     fill_taps(source, frame, taps, position)
     occupied = occupied_of(counts, slot)
+    load.wait()
     for half in range(2):
         at = slice(256 * half, 256 * half + 256)
-        skip_grad[0, :, at] = (dot(weight[...], taps[:, at]) * occupied).astype(BF16)
+        skip_grad[0, :, at] = (dot(held_weight[...], taps[:, at]) * occupied).astype(BF16)
     lane = iota((1, 8 * 128), 1)
     kind = lane >> 7
     inner = lane & 127
@@ -314,6 +328,8 @@
 
 
 SMEM = pl.BlockSpec(memory_space=pltpu.SMEM)
+ANYWHERE = pl.BlockSpec(memory_space=pl.ANY)
+WEIGHT_SCRATCH = [pltpu.VMEM((CH, TAPS), BF16), pltpu.SemaphoreType.DMA]
 
 
 def whole(*shape):
@@ -352,8 +368,8 @@
         grid=(2,),
         in_specs=[SMEM] * 4
         + [one_slot(CH, VOX), whole(2, CH, VOX), whole(8, CH, CH)],
-        out_specs=[whole(2, ROWS, VOX), whole(4, ROWS, FACE)],
-        out_shape=[shaped((2, ROWS, VOX)), shaped((4, ROWS, FACE))],
+        out_specs=[whole(2, ROWS, VOX)] + [whole(ROWS, FACE)] * 4,
+        out_shape=[shaped((2, ROWS, VOX))] + [shaped((ROWS, FACE))] * 4,
         scratch_shapes=[pltpu.VMEM((ROWS, 4 * FACE), F32)],
         cost_estimate=cost(2_000_000_000, 3_000_000),
         interpret=INTERPRET,
@@ -382,7 +398,7 @@
     low_x, high_x = both_ways("gx", faces[0], faces[1])
     low_x, high_x, beside_x = lax.optimization_barrier((low_x, high_x, beside_x))
     to_high, to_low = small_kernel(edges_kernel, [shaped((ROWS, 2 * FACE))] * 2, SMALL)(
-        faces, low_x, high_x
+        faces[2], faces[3], low_x, high_x
     )
     low_y, high_y = both_ways("gy", to_high, to_low)
     return (own, low_x, high_x, low_y, high_y), beside_x
@@ -393,21 +409,22 @@
     return pl.pallas_call(
         forward_kernel,
         grid=(2,),
-        in_specs=[SMEM] * 3 + SOURCE_SPECS + [one_slot(CH, VOX), whole(CH, TAPS)],
+        in_specs=[SMEM] * 3 + SOURCE_SPECS + [one_slot(CH, VOX), ANYWHERE],
         out_specs=[
             whole(2, ROWS, VOX),
-            whole(4, ROWS, FACE),
+            *[whole(ROWS, FACE)] * 4,
             whole(ZH, part, PADDED),
             whole(ZH, part, PADDED),
         ],
         out_shape=[
             shaped((2, ROWS, VOX)),
-            shaped((4, ROWS, FACE)),
+            *[shaped((ROWS, FACE))] * 4,
             shaped((ZH, part, PADDED), F32),
             shaped((ZH, part, PADDED)),
         ],
         scratch_shapes=TAP_SCRATCH
-        + [pltpu.VMEM((ROWS, 4 * FACE), F32), pltpu.VMEM((CH, PADDED), F32)],
+        + [pltpu.VMEM((ROWS, 4 * FACE), F32), pltpu.VMEM((CH, PADDED), F32)]
+        + WEIGHT_SCRATCH,
         cost_estimate=cost(8_000_000_000, 8_000_000),
         interpret=INTERPRET,
         name="forward",
@@ -416,17 +433,17 @@
 
 def run_backward(slot, fine, coarse_pos, parents, counts, sources, weight, up, before=()):
     aliases = {11: 0} if before else {}
-    earlier = [pl.BlockSpec(memory_space=pl.ANY), whole(2, CH, VOX)] if before else []
+    earlier = [ANYWHERE, whole(2, CH, VOX)] if before else []
     return pl.pallas_call(
         functools.partial(backward_kernel, slot),
         grid=(1,),
-        in_specs=[SMEM] * 4 + SOURCE_SPECS + [whole(CH, TAPS), whole(8, CH, CH)] + earlier,
+        in_specs=[SMEM] * 4 + SOURCE_SPECS + [ANYWHERE, whole(8, CH, CH)] + earlier,
         out_specs=[
             pl.BlockSpec((1, CH, VOX), lambda step: (slot, 0, 0)),
             whole(2, CH, VOX),
         ],
         out_shape=[shaped((2, CH, VOX)), shaped((2, CH, VOX))],
-        scratch_shapes=TAP_SCRATCH,
+        scratch_shapes=TAP_SCRATCH + WEIGHT_SCRATCH,
         input_output_aliases=aliases,
         cost_estimate=cost(3_000_000_000, 4_000_000),
         interpret=INTERPRET,
@@ -484,11 +501,11 @@
     backs = small_kernel(
         flatten_back_kernel, [shaped((CH, TAPS)), shaped((8, CH, CH))]
     )(by_offset, up_weight)
-    own, faces = make_hidden(
+    own, *faces = make_hidden(
         fine_coords, coarse_coords, parents, counts, skip_feature_rows, coarse_features, up_weight
     )
     sources, (weight_back, up_back) = exchange(own, faces, tuple(backs))
-    grad, grad_faces, keep, send = run_forward(
+    grad, *grad_faces, keep, send = run_forward(
         fine_coords, counts, core, sources, cotangent, weight_flat
     )
     terms = reduce_first(keep, send)

time: 149 us -> 149 us (level)
  starting transfers between devices: 81.1 us -> 76.5 us
  waiting for transfers between devices: 15 us -> 19 us
    ppermute x4, waiting for transfers between devices: 0.74 us -> 5.77 us  [both_ways(): lax.ppermute(to_low, axis, backward)]
    all_to_all x1, starting transfers between devices: 14.9 us -> 12.9 us  [reduce_second(): packed = lax.all_to_all(spread, 'gx', 0, 0, tiled=True)]
    ppermute x4, starting transfers between devices: 21.6 us -> 19.7 us  [both_ways(): lax.ppermute(to_high, axis, forward)]
  transfers between devices with their start and end apart: 14 -> 14, of which waited for: 7 -> 6; matrix products, arithmetic and copies ran while one was open for 0% -> 0% of each run, Pallas kernels for 16% -> 17%
where the time goes in v6:
time: 149 us; the launch traced here: 148 us
  starting transfers between devices  76.5 us (51%)
  Pallas kernels  47.3 us (32%)
  waiting for transfers between devices  19 us (13%)
  other arithmetic  1.73 us (1%)
  between operations  1.7 us (1%)
  local copies, waits for them, and re-layouts  1.51 us (1%)
    all_to_all x1, starting transfers between devices, reduce_second(): lax.all_to_all(packed.reshape(GROUP, 16, 128), 'gx', 0, 0, tiled=True)  20.1 us
    ppermute x4, starting transfers between devices, both_ways(): lax.ppermute(to_high, axis, forward)  19.7 us
    pallas_call x1, Pallas kernels, run_forward(): pl.pallas_call(forward_kernel, grid=(2,), in_specs=[SMEM] * 3 + SOURCE_SP...  15.9 us
    pallas_call x2, Pallas kernels, run_backward(): pl.pallas_call(functools.partial(backward_kernel, slot), grid=(1,), in_sp...  15.6 us
    ppermute x3, starting transfers between devices, reduce_first(): lax.ppermute(piece, 'gy', gy_pairs(lambda h, c, s=step: ((h + s) % ZH, c)))  15.4 us
    all_to_all x1, starting transfers between devices, reduce_second(): packed = lax.all_to_all(spread, 'gx', 0, 0, tiled=True)  12.9 us
    ppermute x3, waiting for transfers between devices, reduce_first(): lax.ppermute(piece, 'gy', gy_pairs(lambda h, c, s=step: ((h + s) % ZH, c)))  10.5 us
    ppermute x4, starting transfers between devices, both_ways(): lax.ppermute(to_low, axis, backward)  6.43 us
  transfers between devices with their start and end apart: 14, of which 6 were waited for; matrix products, arithmetic and copies ran while one was open for 0% of the time, Pallas kernels for 17%

profile of v6, /device:TPU:1, one launch (start us, length us, event | category | flops | bytes accessed | tf_op | source)
XLA Modules:
  0.0 147.8 jit_solution(2182493319533364830)
XLA Ops:
  1.3 4.5 %hidden.1 = (bf16[2,208,512]{2,1,0:T(8,128)(2,1)}, bf16[208,128]{1,0:T(8,128)(2,1)}, bf16[208,128]{1,0:T(8,128)(2,1)}, bf16[208,128]{1,0:T(8,128)(2,1)}, bf16[208,128]{1,0:T(8,128)(2,1)}) custom-call(s32[2,3]{1,0:T(2,128)} %fine.7, s32[2,3]{1,0:T(2,128)} %coarse_pos.5, s32[2]{0:T(128)} %parents.5, s32[1]{0:T(128)S(6)} %copy.14.counts, ...), custom_call_target="tpu_custom_call" | custom-call | flops 2000000000 | bytes 3000000 | tf_op jit(solution)/shard_map/hidden/pallas_call | solution.py:366
  5.8 0.0 copy-start.6
  5.8 4.1 %collective-permute-start = (bf16[208,128]{1,0:T(8,128)(2,1)}, bf16[208,128]{1,0:T(8,128)(2,1)S(1)}, u32[]{:S(2)}, u32[]{:S(2)}) collective-permute-start(bf16[208,128]{1,0:T(8,128)(2,1)} %get-tuple-element.32), channel_id=1, source_target_pairs={{0,8},{8,16},{16,24},{24,32},{32,40},{40,48},{48,56},{56,64},{64,7... | collective-permute-start | bytes 159752 | tf_op jit(solution)/shard_map/ppermute | solution.py:394
  9.8 1.3 collective-permute-start.1
  11.1 4.7 %shard_map.112 = (bf16[192,5184]{1,0:T(8,128)(2,1)}, bf16[8,192,192]{2,1,0:T(8,128)(2,1)}) custom-call(bf16[27,192,192]{2,1,0:T(8,128)(2,1)} %bitcast.14, bf16[8,192,192]{2,1,0:T(8,128)(2,1)} %up.3), custom_call_target="tpu_custom_call" | custom-call | flops 1000000 | bytes 3000000 | tf_op jit(solution)/shard_map/pallas_call | solution.py:501
  15.9 0.0 collective-permute-done.from_low.low_x
  15.9 0.0 collective-permute-done.1.from_high.high_x
  15.9 0.0 copy-start.3
  15.9 0.0 copy-done.6
  15.9 0.0 copy-done.7
  15.9 0.3 shard_map.113
  16.2 6.8 %collective-permute-start.2 = (bf16[208,256]{1,0:T(8,128)(2,1)S(1)}, bf16[208,256]{1,0:T(8,128)(2,1)S(1)}, u32[]{:S(2)}, u32[]{:S(2)}) collective-permute-start(bf16[208,256]{1,0:T(8,128)(2,1)S(1)} %get-tuple-element.40), channel_id=1, source_target_pairs={{0,1},{1,2},{2,3},{3,4},{4,5},{5,6},{6,7},{8,9},{9,10},{10,11},{11... | collective-permute-start | bytes 319496 | tf_op jit(solution)/shard_map/ppermute | solution.py:394
  23.0 1.9 %collective-permute-start.3 = (bf16[208,256]{1,0:T(8,128)(2,1)S(1)}, bf16[208,256]{1,0:T(8,128)(2,1)S(1)}, u32[]{:S(2)}, u32[]{:S(2)}) collective-permute-start(bf16[208,256]{1,0:T(8,128)(2,1)S(1)} %get-tuple-element.41), channel_id=1, source_target_pairs={{1,0},{2,1},{3,2},{4,3},{5,4},{6,5},{7,6},{9,8},{10,9},{11,10},{12... | collective-permute-start | bytes 319496 | tf_op jit(solution)/shard_map/ppermute | solution.py:394
  25.0 3.4 %shard_map.114.weight = bf16[192,5184]{1,0:T(8,128)(2,1)} custom-call(bf16[27,192,192]{2,1,0:T(8,128)(2,1)} %bitcast.15), custom_call_target="tpu_custom_call" | custom-call | flops 1000000 | bytes 3000000 | tf_op jit(solution)/shard_map/pallas_call | solution.py:500
  28.4 0.0 copy-done.2
  28.4 0.0 copy-done.3
  28.4 0.0 collective-permute-done.2.low_y
  28.4 0.0 copy-start.8
  28.4 1.5 %collective-permute-done.3.high_y = bf16[208,256]{1,0:T(8,128)(2,1)S(1)} collective-permute-done((bf16[208,256]{1,0:T(8,128)(2,1)S(1)}, bf16[208,256]{1,0:T(8,128)(2,1)S(1)}, u32[]{:S(2)}, u32[]{:S(2)}) %collective-permute-start.3) | collective-permute-done | bytes 106528 | tf_op jit(solution)/shard_map/ppermute | solution.py:394
  29.9 0.0 copy-done.8
  29.9 0.6 copy-done.9
  30.6 15.9 %forward.1 = (bf16[2,208,512]{2,1,0:T(8,128)(2,1)}, bf16[208,128]{1,0:T(8,128)(2,1)}, bf16[208,128]{1,0:T(8,128)(2,1)}, bf16[208,128]{1,0:T(8,128)(2,1)}, bf16[2...) custom-call(s32[2,3]{1,0:T(2,128)} %fine.7, s32[1]{0:T(128)S(6)} %copy.14.counts, ...), custom_call_target="tpu_custom_call" | custom-call | flops 8000000000 | bytes 8000000 | tf_op jit(solution)/shard_map/forward/pallas_call | solution.py:409
  46.5 1.9 %collective-permute-start.8 = (bf16[4,24,5248]{2,1,0:T(8,128)(2,1)}, bf16[4,24,5248]{2,1,0:T(8,128)(2,1)S(1)}, u32[]{:S(2)}, u32[]{:S(2)}) collective-permute-start(bf16[4,24,5248]{2,1,0:T(8,128)(2,1)} %get-tuple-element.58), channel_id=1, source_target_pairs={{0,1},{1,0},{2,3},{3,2},{4,5},{5,4},{6,7},{7,6},{8,9},{9,8},{10,11... | collective-permute-start | bytes 3022856 | tf_op jit(solution)/shard_map/ppermute | solution.py:468
  48.5 2.7 %collective-permute-done.8 = bf16[4,24,5248]{2,1,0:T(8,128)(2,1)S(1)} collective-permute-done((bf16[4,24,5248]{2,1,0:T(8,128)(2,1)}, bf16[4,24,5248]{2,1,0:T(8,128)(2,1)S(1)}, u32[]{:S(2)}, u32[]{:S(2)}) %collective-permute-start.8) | collective-permute-done | bytes 1007648 | tf_op jit(solution)/shard_map/ppermute | solution.py:468
  51.2 1.7 %convert_add_fusion = f32[4,24,5248]{2,1,0:T(8,128)S(1)} fusion(f32[4,24,5248]{2,1,0:T(8,128)} %get-tuple-element.57, bf16[4,24,5248]{2,1,0:T(8,128)(2,1)S(1)} %collective-permute-done.8), kind=kLoop, calls=%fused_computation | loop fusion | flops 1007616 | bytes 5038080 | tf_op jit(solution)/shard_map/add | solution.py:469
  52.9 0.0 copy-start.13
  53.0 0.0 copy-start.12
  53.0 0.0 copy-start
  53.0 0.0 copy-start.1
  53.0 0.1 fusion.2
  53.1 8.8 %collective-permute-start.11 = (bf16[24,5248]{1,0:T(8,128)(2,1)S(1)}, bf16[24,5248]{1,0:T(8,128)(2,1)S(1)}, u32[]{:S(2)}, u32[]{:S(2)}) collective-permute-start(bf16[24,5248]{1,0:T(8,128)(2,1)S(1)} %get-tuple-element.59), channel_id=1, source_target_pairs={{0,4},{1,5},{2,6},{3,7},{4,0},{5,1},{6,2},{7,3},{8,12},{9,13},{10,... | collective-permute-start | bytes 755720 | tf_op jit(solution)/shard_map/ppermute | solution.py:473
  62.0 4.6 %collective-permute-start.10 = (bf16[24,5248]{1,0:T(8,128)(2,1)S(1)}, bf16[24,5248]{1,0:T(8,128)(2,1)S(1)}, u32[]{:S(2)}, u32[]{:S(2)}) collective-permute-start(bf16[24,5248]{1,0:T(8,128)(2,1)S(1)} %get-tuple-element.60), channel_id=1, source_target_pairs={{0,6},{1,7},{2,0},{3,1},{4,2},{5,3},{6,4},{7,5},{8,14},{9,15},{10,... | collective-permute-start | bytes 755720 | tf_op jit(solution)/shard_map/ppermute | solution.py:473
  66.6 1.9 %collective-permute-start.9 = (bf16[24,5248]{1,0:T(8,128)(2,1)S(1)}, bf16[24,5248]{1,0:T(8,128)(2,1)S(1)}, u32[]{:S(2)}, u32[]{:S(2)}) collective-permute-start(bf16[24,5248]{1,0:T(8,128)(2,1)S(1)} %get-tuple-element.61), channel_id=1, source_target_pairs={{0,2},{1,3},{2,4},{3,5},{4,6},{5,7},{6,0},{7,1},{8,10},{9,11},{10,... | collective-permute-start | bytes 755720 | tf_op jit(solution)/shard_map/ppermute | solution.py:473
  68.6 0.9 collective-permute-done.11.third
  69.4 2.9 %collective-permute-done.10.second = bf16[24,5248]{1,0:T(8,128)(2,1)S(1)} collective-permute-done((bf16[24,5248]{1,0:T(8,128)(2,1)S(1)}, bf16[24,5248]{1,0:T(8,128)(2,1)S(1)}, u32[]{:S(2)}, u32[]{:S(2)}) %collective-permute-start.10) | collective-permute-done | bytes 251936 | tf_op jit(solution)/shard_map/ppermute | solution.py:473
  72.4 6.7 %collective-permute-done.9.first = bf16[24,5248]{1,0:T(8,128)(2,1)S(1)} collective-permute-done((bf16[24,5248]{1,0:T(8,128)(2,1)S(1)}, bf16[24,5248]{1,0:T(8,128)(2,1)S(1)}, u32[]{:S(2)}, u32[]{:S(2)}) %collective-permute-start.9) | collective-permute-done | bytes 251936 | tf_op jit(solution)/shard_map/ppermute | solution.py:473
  79.1 0.8 shard_map.118
  79.9 20.1 %all-to-all-start = ((bf16[64,16,128]{2,1,0:T(8,128)(2,1)}), bf16[64,16,128]{2,1,0:T(8,128)(2,1)S(1)}, u32[]{:S(2)}, u32[]{:S(2)}) async-start(bf16[64,16,128]{2,1,0:T(8,128)(2,1)} %bitcast.6), calls=%async_computation | async-start | bytes 524288 | tf_op jit(solution)/shard_map/all_to_all | solution.py:479
  100.0 0.0 copy-done.13
  100.1 2.9 %collective-permute-start.4 = (bf16[208,128]{1,0:T(8,128)(2,1)S(1)}, bf16[208,128]{1,0:T(8,128)(2,1)S(1)}, u32[]{:S(2)}, u32[]{:S(2)}) collective-permute-start(bf16[208,128]{1,0:T(8,128)(2,1)S(1)} %copy-done.13), channel_id=1, source_target_pairs={{0,8},{8,16},{16,24},{24,32},{32,40},{40,48},{48,56},{56,64},{64,7... | collective-permute-start | bytes 159752 | tf_op jit(solution)/shard_map/ppermute | solution.py:394
  103.0 0.0 copy-done.12
  103.0 1.3 collective-permute-start.5
  104.3 0.0 collective-permute-done.4.from_low.refs_0_
  104.3 4.2 %collective-permute-done.5.from_high.refs_1_ = bf16[208,128]{1,0:T(8,128)(2,1)S(1)} collective-permute-done((bf16[208,128]{1,0:T(8,128)(2,1)S(1)}, bf16[208,128]{1,0:T(8,128)(2,1)S(1)}, u32[]{:S(2)}, u32[]{:S(2)}) %collective-permute-start.5) | collective-permute-done | bytes 53280 | tf_op jit(solution)/shard_map/ppermute | solution.py:394
  108.6 0.0 copy-done
  108.6 0.0 copy-done.1
  108.6 0.3 shard_map.115
  108.8 5.9 %collective-permute-start.6 = (bf16[208,256]{1,0:T(8,128)(2,1)S(1)}, bf16[208,256]{1,0:T(8,128)(2,1)S(1)}, u32[]{:S(2)}, u32[]{:S(2)}) collective-permute-start(bf16[208,256]{1,0:T(8,128)(2,1)S(1)} %get-tuple-element.49), channel_id=1, source_target_pairs={{0,1},{1,2},{2,3},{3,4},{4,5},{5,6},{6,7},{8,9},{9,10},{10,11},{11... | collective-permute-start | bytes 319496 | tf_op jit(solution)/shard_map/ppermute | solution.py:394
  114.8 1.9 %collective-permute-start.7 = (bf16[208,256]{1,0:T(8,128)(2,1)S(1)}, bf16[208,256]{1,0:T(8,128)(2,1)S(1)}, u32[]{:S(2)}, u32[]{:S(2)}) collective-permute-start(bf16[208,256]{1,0:T(8,128)(2,1)S(1)} %get-tuple-element.50), channel_id=1, source_target_pairs={{1,0},{2,1},{3,2},{4,3},{5,4},{6,5},{7,6},{9,8},{10,9},{11,10},{12... | collective-permute-start | bytes 319496 | tf_op jit(solution)/shard_map/ppermute | solution.py:394
  116.7 0.0 all-to-all-done.pieces
  116.7 0.8 shard_map.119
  117.5 12.9 %all-to-all-start.1 = ((bf16[64,16,128]{2,1,0:T(8,128)(2,1)}), bf16[64,16,128]{2,1,0:T(8,128)(2,1)S(1)}, u32[]{:S(2)}, u32[]{:S(2)}) async-start(bf16[64,16,128]{2,1,0:T(8,128)(2,1)} %shard_map.119), calls=%async_computation.1 | async-start | bytes 524288 | tf_op jit(solution)/shard_map/all_to_all | solution.py:481
  130.5 0.0 collective-permute-done.6.refs_2_
  130.5 0.0 copy-start.10
  130.5 0.0 collective-permute-done.7.refs_3_
  130.5 0.0 copy-start.11
  130.5 0.0 copy-done.4
  130.5 0.0 copy-done.5
  130.5 0.6 copy-done.10
  131.1 0.0 copy-done.11
  131.2 7.1 %shard_map.116 = (bf16[2,192,512]{2,1,0:T(8,128)(2,1)}, bf16[2,192,512]{2,1,0:T(8,128)(2,1)}) custom-call(s32[2,3]{1,0:T(2,128)} %fine.7, s32[2,3]{1,0:T(2,128)} %coarse_pos.5, s32[2]{0:T(128)} %parents.5, s32[1]{0:T(128)S(6)} %copy.14.counts, bf16[2,208,512]{2,1,0:T(8,128)(2,1)} %get-tuple-element.42.own, bf16[208,128]{1,0:T(8,128)(2,1)} %copy-done.4, ...), custom_call_target="tpu_custom_call" | custom-call | flops 3000000000 | bytes 4000000 | tf_op jit(solution)/shard_map/pallas_call | solution.py:437
  138.2 8.5 %shard_map.117 = (bf16[2,192,512]{2,1,0:T(8,128)(2,1)}, bf16[2,192,512]{2,1,0:T(8,128)(2,1)}) custom-call(s32[2,3]{1,0:T(2,128)} %fine.7, s32[2,3]{1,0:T(2,128)} %coarse_pos.5, s32[2]{0:T(128)} %parents.5, s32[1]{0:T(128)S(6)} %copy.14.counts, bf16[2,208,512]{2,1,0:T(8,128)(2,1)} %get-tuple-element.42.own, ...), custom_call_target="tpu_custom_call", output_to_operand_aliasing={{0}: (11, {})} | custom-call | flops 3000000000 | bytes 4000000 | tf_op jit(solution)/shard_map/pallas_call | solution.py:437
  146.8 0.0 all-to-all-done.1
  146.8 1.0 shard_map.120
  (6 shorter events, 0.1 us)
Async XLA Ops:
  5.8 10.1 %copy-start.6 = (bf16[208,128]{1,0:T(8,128)(2,1)S(1)}, bf16[208,128]{1,0:T(8,128)(2,1)}, u32[]{:S(2)}) copy-start(bf16[208,128]{1,0:T(8,128)(2,1)} %get-tuple-element.38.y_high) | copy-start | bytes 159748
  5.8 10.2 %copy-start.7 = (bf16[208,128]{1,0:T(8,128)(2,1)S(1)}, bf16[208,128]{1,0:T(8,128)(2,1)}, u32[]{:S(2)}) copy-start(bf16[208,128]{1,0:T(8,128)(2,1)} %get-tuple-element.39.y_low) | copy-start | bytes 159748
  5.8 10.1 %collective-permute-start = (bf16[208,128]{1,0:T(8,128)(2,1)}, bf16[208,128]{1,0:T(8,128)(2,1)S(1)}, u32[]{:S(2)}, u32[]{:S(2)}) collective-permute-start(bf16[208,128]{1,0:T(8,128)(2,1)} %get-tuple-element.32), channel_id=1, source_target_pairs={{0,8},{8,16},{16,24},{24,32},{32,40},{40,48},{48,56},{56,64},{64,7... | collective-permute-start | bytes 159752 | tf_op jit(solution)/shard_map/ppermute | solution.py:394
  9.8 6.0 %collective-permute-start.1 = (bf16[208,128]{1,0:T(8,128)(2,1)}, bf16[208,128]{1,0:T(8,128)(2,1)S(1)}, u32[]{:S(2)}, u32[]{:S(2)}) collective-permute-start(bf16[208,128]{1,0:T(8,128)(2,1)} %get-tuple-element.33), channel_id=1, source_target_pairs={{8,0},{16,8},{24,16},{32,24},{40,32},{48,40},{56,48},{64,56},{72,6... | collective-permute-start | bytes 159752 | tf_op jit(solution)/shard_map/ppermute | solution.py:394
  15.9 12.5 %copy-start.2 = (bf16[208,128]{1,0:T(8,128)(2,1)}, bf16[208,128]{1,0:T(8,128)(2,1)S(1)}, u32[]{:S(2)}) copy-start(bf16[208,128]{1,0:T(8,128)(2,1)S(1)} %collective-permute-done.from_low.low_x) | copy-start | bytes 159748
  15.9 12.5 %copy-start.3 = (bf16[208,128]{1,0:T(8,128)(2,1)}, bf16[208,128]{1,0:T(8,128)(2,1)S(1)}, u32[]{:S(2)}) copy-start(bf16[208,128]{1,0:T(8,128)(2,1)S(1)} %collective-permute-done.1.from_high.high_x) | copy-start | bytes 159748
  16.2 12.2 %collective-permute-start.2 = (bf16[208,256]{1,0:T(8,128)(2,1)S(1)}, bf16[208,256]{1,0:T(8,128)(2,1)S(1)}, u32[]{:S(2)}, u32[]{:S(2)}) collective-permute-start(bf16[208,256]{1,0:T(8,128)(2,1)S(1)} %get-tuple-element.40), channel_id=1, source_target_pairs={{0,1},{1,2},{2,3},{3,4},{4,5},{5,6},{6,7},{8,9},{9,10},{10,11},{11... | collective-permute-start | bytes 319496 | tf_op jit(solution)/shard_map/ppermute | solution.py:394
  23.0 6.9 %collective-permute-start.3 = (bf16[208,256]{1,0:T(8,128)(2,1)S(1)}, bf16[208,256]{1,0:T(8,128)(2,1)S(1)}, u32[]{:S(2)}, u32[]{:S(2)}) collective-permute-start(bf16[208,256]{1,0:T(8,128)(2,1)S(1)} %get-tuple-element.41), channel_id=1, source_target_pairs={{1,0},{2,1},{3,2},{4,3},{5,4},{6,5},{7,6},{9,8},{10,9},{11,10},{12... | collective-permute-start | bytes 319496 | tf_op jit(solution)/shard_map/ppermute | solution.py:394
  28.4 1.6 %copy-start.8 = (bf16[208,256]{1,0:T(8,128)(2,1)}, bf16[208,256]{1,0:T(8,128)(2,1)S(1)}, u32[]{:S(2)}) copy-start(bf16[208,256]{1,0:T(8,128)(2,1)S(1)} %collective-permute-done.2.low_y) | copy-start | bytes 319492
  29.9 0.6 copy-start.9
  46.5 4.7 %collective-permute-start.8 = (bf16[4,24,5248]{2,1,0:T(8,128)(2,1)}, bf16[4,24,5248]{2,1,0:T(8,128)(2,1)S(1)}, u32[]{:S(2)}, u32[]{:S(2)}) collective-permute-start(bf16[4,24,5248]{2,1,0:T(8,128)(2,1)} %get-tuple-element.58), channel_id=1, source_target_pairs={{0,1},{1,0},{2,3},{3,2},{4,5},{5,4},{6,7},{7,6},{8,9},{9,8},{10,11... | collective-permute-start | bytes 3022856 | tf_op jit(solution)/shard_map/ppermute | solution.py:468
  52.9 47.1 %copy-start.13 = (bf16[208,128]{1,0:T(8,128)(2,1)S(1)}, bf16[208,128]{1,0:T(8,128)(2,1)}, u32[]{:S(2)}) copy-start(bf16[208,128]{1,0:T(8,128)(2,1)} %get-tuple-element.43) | copy-start | bytes 159748
  53.0 50.0 %copy-start.12 = (bf16[208,128]{1,0:T(8,128)(2,1)S(1)}, bf16[208,128]{1,0:T(8,128)(2,1)}, u32[]{:S(2)}) copy-start(bf16[208,128]{1,0:T(8,128)(2,1)} %get-tuple-element.44) | copy-start | bytes 159748
  53.0 55.6 %copy-start = (bf16[208,128]{1,0:T(8,128)(2,1)S(1)}, bf16[208,128]{1,0:T(8,128)(2,1)}, u32[]{:S(2)}) copy-start(bf16[208,128]{1,0:T(8,128)(2,1)} %get-tuple-element.47.y_high) | copy-start | bytes 159748
  53.0 55.6 %copy-start.1 = (bf16[208,128]{1,0:T(8,128)(2,1)S(1)}, bf16[208,128]{1,0:T(8,128)(2,1)}, u32[]{:S(2)}) copy-start(bf16[208,128]{1,0:T(8,128)(2,1)} %get-tuple-element.48.y_low) | copy-start | bytes 159748
  53.1 16.3 %collective-permute-start.11 = (bf16[24,5248]{1,0:T(8,128)(2,1)S(1)}, bf16[24,5248]{1,0:T(8,128)(2,1)S(1)}, u32[]{:S(2)}, u32[]{:S(2)}) collective-permute-start(bf16[24,5248]{1,0:T(8,128)(2,1)S(1)} %get-tuple-element.59), channel_id=1, source_target_pairs={{0,4},{1,5},{2,6},{3,7},{4,0},{5,1},{6,2},{7,3},{8,12},{9,13},{10,... | collective-permute-start | bytes 755720 | tf_op jit(solution)/shard_map/ppermute | solution.py:473
  62.0 10.4 %collective-permute-start.10 = (bf16[24,5248]{1,0:T(8,128)(2,1)S(1)}, bf16[24,5248]{1,0:T(8,128)(2,1)S(1)}, u32[]{:S(2)}, u32[]{:S(2)}) collective-permute-start(bf16[24,5248]{1,0:T(8,128)(2,1)S(1)} %get-tuple-element.60), channel_id=1, source_target_pairs={{0,6},{1,7},{2,0},{3,1},{4,2},{5,3},{6,4},{7,5},{8,14},{9,15},{10,... | collective-permute-start | bytes 755720 | tf_op jit(solution)/shard_map/ppermute | solution.py:473
  66.6 12.5 %collective-permute-start.9 = (bf16[24,5248]{1,0:T(8,128)(2,1)S(1)}, bf16[24,5248]{1,0:T(8,128)(2,1)S(1)}, u32[]{:S(2)}, u32[]{:S(2)}) collective-permute-start(bf16[24,5248]{1,0:T(8,128)(2,1)S(1)} %get-tuple-element.61), channel_id=1, source_target_pairs={{0,2},{1,3},{2,4},{3,5},{4,6},{5,7},{6,0},{7,1},{8,10},{9,11},{10,... | collective-permute-start | bytes 755720 | tf_op jit(solution)/shard_map/ppermute | solution.py:473
  79.9 36.8 %all-to-all-start = ((bf16[64,16,128]{2,1,0:T(8,128)(2,1)}), bf16[64,16,128]{2,1,0:T(8,128)(2,1)S(1)}, u32[]{:S(2)}, u32[]{:S(2)}) async-start(bf16[64,16,128]{2,1,0:T(8,128)(2,1)} %bitcast.6), calls=%async_computation | async-start | bytes 524288 | tf_op jit(solution)/shard_map/all_to_all | solution.py:479
  100.1 4.3 %collective-permute-start.4 = (bf16[208,128]{1,0:T(8,128)(2,1)S(1)}, bf16[208,128]{1,0:T(8,128)(2,1)S(1)}, u32[]{:S(2)}, u32[]{:S(2)}) collective-permute-start(bf16[208,128]{1,0:T(8,128)(2,1)S(1)} %copy-done.13), channel_id=1, source_target_pairs={{0,8},{8,16},{16,24},{24,32},{32,40},{40,48},{48,56},{56,64},{64,7... | collective-permute-start | bytes 159752 | tf_op jit(solution)/shard_map/ppermute | solution.py:394
  103.0 5.6 %collective-permute-start.5 = (bf16[208,128]{1,0:T(8,128)(2,1)S(1)}, bf16[208,128]{1,0:T(8,128)(2,1)S(1)}, u32[]{:S(2)}, u32[]{:S(2)}) collective-permute-start(bf16[208,128]{1,0:T(8,128)(2,1)S(1)} %copy-done.12), channel_id=1, source_target_pairs={{8,0},{16,8},{24,16},{32,24},{40,32},{48,40},{56,48},{64,56},{72,6... | collective-permute-start | bytes 159752 | tf_op jit(solution)/shard_map/ppermute | solution.py:394
  104.3 26.2 %copy-start.4 = (bf16[208,128]{1,0:T(8,128)(2,1)}, bf16[208,128]{1,0:T(8,128)(2,1)S(1)}, u32[]{:S(2)}) copy-start(bf16[208,128]{1,0:T(8,128)(2,1)S(1)} %collective-permute-done.4.from_low.refs_0_) | copy-start | bytes 159748
  108.6 22.0 %copy-start.5 = (bf16[208,128]{1,0:T(8,128)(2,1)}, bf16[208,128]{1,0:T(8,128)(2,1)S(1)}, u32[]{:S(2)}) copy-start(bf16[208,128]{1,0:T(8,128)(2,1)S(1)} %collective-permute-done.5.from_high.refs_1_) | copy-start | bytes 159748
  108.8 21.6 %collective-permute-start.6 = (bf16[208,256]{1,0:T(8,128)(2,1)S(1)}, bf16[208,256]{1,0:T(8,128)(2,1)S(1)}, u32[]{:S(2)}, u32[]{:S(2)}) collective-permute-start(bf16[208,256]{1,0:T(8,128)(2,1)S(1)} %get-tuple-element.49), channel_id=1, source_target_pairs={{0,1},{1,2},{2,3},{3,4},{4,5},{5,6},{6,7},{8,9},{9,10},{10,11},{11... | collective-permute-start | bytes 319496 | tf_op jit(solution)/shard_map/ppermute | solution.py:394
  114.8 15.7 %collective-permute-start.7 = (bf16[208,256]{1,0:T(8,128)(2,1)S(1)}, bf16[208,256]{1,0:T(8,128)(2,1)S(1)}, u32[]{:S(2)}, u32[]{:S(2)}) collective-permute-start(bf16[208,256]{1,0:T(8,128)(2,1)S(1)} %get-tuple-element.50), channel_id=1, source_target_pairs={{1,0},{2,1},{3,2},{4,3},{5,4},{6,5},{7,6},{9,8},{10,9},{11,10},{12... | collective-permute-start | bytes 319496 | tf_op jit(solution)/shard_map/ppermute | solution.py:394
  117.5 29.3 %all-to-all-start.1 = ((bf16[64,16,128]{2,1,0:T(8,128)(2,1)}), bf16[64,16,128]{2,1,0:T(8,128)(2,1)S(1)}, u32[]{:S(2)}, u32[]{:S(2)}) async-start(bf16[64,16,128]{2,1,0:T(8,128)(2,1)} %shard_map.119), calls=%async_computation.1 | async-start | bytes 524288 | tf_op jit(solution)/shard_map/all_to_all | solution.py:481
  130.5 0.6 copy-start.10
  130.5 0.7 copy-start.11
